TPU v7x, 128 devices: a whole 4x4x4 slice. The times are simulated.
128 devices in a mesh: chan: 2 (over x_hi), blk: 64 (over y, z, x_lo, core).
Axes of the slice: x: 4 (x_hi: 2, x_lo: 2; x = x_hi * 2 + x_lo), y: 4, z: 4, core: 2. Of those that a mesh axis runs over, the one named last changes fastest.
Arguments:
- features: bfloat16 [64, 2, 256, 128], P('blk', 'chan'), may hold values from -6 to 6
- transforms: bfloat16 [8, 128, 128], replicated, may hold values from -0.5 to 0.5
- self_weight: bfloat16 [128, 128], replicated, may hold values from -0.5 to 0.5
- tile_rows: int32 [8, 64, 64, 8], P('chan', 'blk'), may hold values from 0 to 3
- tile_cols: int32 [8, 64, 64, 8], P('chan', 'blk'), may hold values from 0 to 3
- tile_ids: int32 [8, 64, 64, 8], P('chan', 'blk'), may hold values from 0 to 31
- tile_count: int32 [8, 64, 64], P('chan', 'blk'), may hold values from 0 to 8
- tile_pool: bfloat16 [8, 64, 32, 128, 128], P('chan', 'blk'), may hold values from -0.0234375 to 0.0234375
Outputs:
- updated: bfloat16 [64, 2, 256, 128], P('blk', 'chan')
All inputs are finite; a program needn't handle non-finite values.
Results may differ from a plain program's by a relative error of at most 0.0041.
Values may be sent and summed in bfloat16 or wider, within the bound.
No kernel may reach another device: no remote copies, remote signals or barrier semaphores. Data moves between devices by JAX's collectives and lax.ppermute only.
A program may use at most 128 MiB of HBM per device.

v0:
```python
import math

import jax
import jax.numpy as jnp
from jax import lax
from jax.sharding import PartitionSpec as P


def shards(
    features, transforms, self_weight, tile_rows, tile_cols, tile_ids, tile_count, tile_pool
):
    chan_count = lax.axis_size("chan")
    chan_index = lax.axis_index("chan")
    own_rows = features[0, 0]
    half_rows = own_rows.shape[0]
    width = own_rows.shape[1]
    tile_size = tile_pool.shape[-1]
    pool_size = tile_pool.shape[2]
    block_rows = half_rows * chan_count
    tiles_block = block_rows // tile_size
    rel_dev = transforms.shape[0] // chan_count
    slot_count = tile_rows.shape[-1]
    rows_list = tile_rows[:, 0]
    cols_list = tile_cols[:, 0]
    ids_list = tile_ids[:, 0]
    count_list = tile_count[:, 0]
    pool_flat = tile_pool[:, 0].reshape(rel_dev, pool_size, tile_size * tile_size)
    slot_range = jnp.arange(slot_count)
    tile_range = jnp.arange(tiles_block)
    pool_range = jnp.arange(pool_size)

    def apply_group(total, hidden_group, first):
        group = hidden_group.shape[1]
        cols_now = lax.dynamic_slice_in_dim(cols_list, first, group, 1)
        rows_now = lax.dynamic_slice_in_dim(rows_list, first, group, 1)
        ids_now = lax.dynamic_slice_in_dim(ids_list, first, group, 1)
        count_now = lax.dynamic_slice_in_dim(count_list, first, group, 1)
        pick_cols = (cols_now[..., None] == tile_range).astype(jnp.bfloat16)
        flat_hidden = hidden_group.reshape(rel_dev, group, tiles_block, tile_size * width)
        picked = jnp.einsum(
            "rgks,rgsx->rgkx", pick_cols, flat_hidden, preferred_element_type=jnp.float32
        ).astype(jnp.bfloat16)
        picked = picked.reshape(rel_dev, group, slot_count, tile_size, width)
        pick_ids = (ids_now[..., None] == pool_range).astype(jnp.bfloat16)
        weights = jnp.einsum(
            "rgkp,rpx->rgkx", pick_ids, pool_flat, preferred_element_type=jnp.float32
        ).astype(jnp.bfloat16)
        weights = weights.reshape(rel_dev, group, slot_count, tile_size, tile_size)
        product = jnp.einsum(
            "rgkab,rgkbd->rgkad", weights, picked, preferred_element_type=jnp.float32
        )
        live = (slot_range < count_now[..., None]).astype(jnp.float32)
        onehot = (rows_now[..., None] == tile_range).astype(jnp.float32) * live[..., None]
        return total + jnp.einsum(
            "rgkt,rgkad->tad", onehot, product, precision=lax.Precision.HIGHEST
        )

    empty = jnp.zeros((tiles_block, tile_size, width), jnp.float32)
    all_hidden = jnp.einsum(
        "nd,rde->rne", own_rows, transforms, preferred_element_type=jnp.float32
    ).astype(jnp.bfloat16)
    mine = lax.all_to_all(all_hidden, "chan", split_axis=0, concat_axis=1, tiled=True)
    piece = lax.all_gather(mine, "blk", axis=1, tiled=True)
    blocks_here = piece.shape[1] // block_rows

    def fetch(offset, group):
        part_rows = lax.dynamic_slice_in_dim(piece, offset * block_rows, group * block_rows, 1)
        return part_rows.reshape(rel_dev, group, tiles_block, tile_size, width)

    group = math.gcd(blocks_here, 4)
    turns = blocks_here // group

    def step_once(turn, carry):
        return apply_group(carry, fetch(turn * group, group), turn * group)

    agg = lax.fori_loop(0, turns, step_once, empty)
    partial_rows = agg.reshape(block_rows, width)
    summed = lax.psum(partial_rows, "chan")
    share = lax.dynamic_slice_in_dim(summed, chan_index * half_rows, half_rows, 0)
    selfterm = jnp.dot(own_rows, self_weight, preferred_element_type=jnp.float32)
    updated = jax.nn.relu(selfterm + share).astype(jnp.bfloat16)
    return updated.reshape(1, 1, half_rows, width)


def solution(mesh):
    placed = (
        P("blk", "chan", None, None),
        P(),
        P(),
        P("chan", "blk", None, None),
        P("chan", "blk", None, None),
        P("chan", "blk", None, None),
        P("chan", "blk", None),
        P("chan", "blk", None, None, None),
    )
    return jax.shard_map(
        shards, mesh=mesh, in_specs=placed, out_specs=P("blk", "chan", None, None), check_vma=False
    )
```

profile of v0, /device:TPU:1, one launch (start us, length us, event | category | flops | bytes accessed | tf_op | source)
XLA Modules:
  0.0 706.5 jit_solution(2026471395278241592)
XLA Ops:
  8.7 13.2 %all_to_all.18 = bf16[8,256,128]{1,2,0:T(8,128)(2,1)S(1)} all-to-all(bf16[8,256,128]{1,2,0:T(8,128)(2,1)S(1)} %fusion.31), channel_id=1, replica_groups=mesh['chan'=2,'blk'=64] {'chan'}, dimensions={0} | all-to-all | bytes 1048576 | tf_op jit(solution)/shard_map/all_to_all | solution.py:62
  23.0 7.3 %reshape_squeeze.3 = bf16[4,32,16384]{2,1,0:T(8,128)(2,1)} reshape(bf16[4,1,32,128,128]{4,3,2,1,0:T(8,128)(2,1)} %param.17) | data formatting | bytes 8388608 | tf_op jit(solution)/shard_map/reshape;squeeze | solution.py:27
  30.8 181.1 %all-gather.2.cloned.1.call-done = bf16[4,32768,128]{2,1,0:T(8,128)(2,1)} async-done(((bf16[4,512,128]{2,1,0:T(8,128)(2,1)}), bf16[4,32768,128]{2,1,0:T(8,128)(2,1)}) %all-gather.2.cloned.1.call-update) | async-done | bytes 33554448 | tf_op jit(solution)/shard_map/all_gather | solution.py:63
  211.9 453.9 %while.17 = (s32[]{:T(128)}, f32[4,128,128]{2,0,1:T(4,128)S(1)}, s32[4,64,8]{2,0,1:T(4,128)S(1)}, s32[4,64]{0,1:T(8,128)S(1)}, s32[4,64,8]{2,1,0:T(8,128)S(1)}, ...) while((s32[]{:T(128)}, f32[4,128,128]{2,0,1:T(4,128)S(1)}, ...), condition=%wide.region_1.0_spmd.clone.clone, body=%wide.region_0.0_spmd.clone.clone.sunk | while | flops 792860416 | bytes 65542100 | solution.py:76
  211.9 3.1 constant_dynamic-slice_fusion.9
  214.9 2.6 reshape.58
  221.1 4.5 fusion.61
  225.6 14.6 %fusion.63 = f32[4,128,128]{2,0,1:T(4,128)S(1)} fusion(f32[4,4,8,128,128]{4,3,2,1,0:T(8,128)} %fusion.61, f32[4,128,128]{2,0,1:T(4,128)S(1)} %get-tuple-element.418, pred[]{:T(512)S(6)} %compare.3, f32[4,4,8]{2,0,1:T(4,128)S(1)} %fusion.62, s32[4,4,8]{2,0,1:T(4,128)S(1)} %get-tuple-element.402), kind=kOutput, calls=%fused_computation.14.clone.1 | convolution fusion | flops 100795392 | bytes 8913921 | tf_op jit(solution)/shard_map/while/body/eval_jaxpr/rgkt,rgkad->tad/dot_general | solution.py:54
  240.2 3.1 constant_dynamic-slice_fusion.9
  243.3 2.6 reshape.58
  249.4 4.5 fusion.61
  254.0 14.6 %fusion.63 = f32[4,128,128]{2,0,1:T(4,128)S(1)} fusion(f32[4,4,8,128,128]{4,3,2,1,0:T(8,128)} %fusion.61, f32[4,128,128]{2,0,1:T(4,128)S(1)} %get-tuple-element.418, pred[]{:T(512)S(6)} %compare.3, f32[4,4,8]{2,0,1:T(4,128)S(1)} %fusion.62, s32[4,4,8]{2,0,1:T(4,128)S(1)} %get-tuple-element.402), kind=kOutput, calls=%fused_computation.14.clone.1 | convolution fusion | flops 100795392 | bytes 8913921 | tf_op jit(solution)/shard_map/while/body/eval_jaxpr/rgkt,rgkad->tad/dot_general | solution.py:54
  268.6 3.1 constant_dynamic-slice_fusion.9
  271.7 2.6 reshape.58
  277.8 4.5 fusion.61
  282.3 14.6 %fusion.63 = f32[4,128,128]{2,0,1:T(4,128)S(1)} fusion(f32[4,4,8,128,128]{4,3,2,1,0:T(8,128)} %fusion.61, f32[4,128,128]{2,0,1:T(4,128)S(1)} %get-tuple-element.418, pred[]{:T(512)S(6)} %compare.3, f32[4,4,8]{2,0,1:T(4,128)S(1)} %fusion.62, s32[4,4,8]{2,0,1:T(4,128)S(1)} %get-tuple-element.402), kind=kOutput, calls=%fused_computation.14.clone.1 | convolution fusion | flops 100795392 | bytes 8913921 | tf_op jit(solution)/shard_map/while/body/eval_jaxpr/rgkt,rgkad->tad/dot_general | solution.py:54
  297.0 3.1 constant_dynamic-slice_fusion.9
  300.1 2.6 reshape.58
  306.2 4.5 fusion.61
  310.7 14.6 %fusion.63 = f32[4,128,128]{2,0,1:T(4,128)S(1)} fusion(f32[4,4,8,128,128]{4,3,2,1,0:T(8,128)} %fusion.61, f32[4,128,128]{2,0,1:T(4,128)S(1)} %get-tuple-element.418, pred[]{:T(512)S(6)} %compare.3, f32[4,4,8]{2,0,1:T(4,128)S(1)} %fusion.62, s32[4,4,8]{2,0,1:T(4,128)S(1)} %get-tuple-element.402), kind=kOutput, calls=%fused_computation.14.clone.1 | convolution fusion | flops 100795392 | bytes 8913921 | tf_op jit(solution)/shard_map/while/body/eval_jaxpr/rgkt,rgkad->tad/dot_general | solution.py:54
  325.4 3.1 constant_dynamic-slice_fusion.9
  328.4 2.6 reshape.58
  334.5 4.5 fusion.61
  339.1 14.6 %fusion.63 = f32[4,128,128]{2,0,1:T(4,128)S(1)} fusion(f32[4,4,8,128,128]{4,3,2,1,0:T(8,128)} %fusion.61, f32[4,128,128]{2,0,1:T(4,128)S(1)} %get-tuple-element.418, pred[]{:T(512)S(6)} %compare.3, f32[4,4,8]{2,0,1:T(4,128)S(1)} %fusion.62, s32[4,4,8]{2,0,1:T(4,128)S(1)} %get-tuple-element.402), kind=kOutput, calls=%fused_computation.14.clone.1 | convolution fusion | flops 100795392 | bytes 8913921 | tf_op jit(solution)/shard_map/while/body/eval_jaxpr/rgkt,rgkad->tad/dot_general | solution.py:54
  353.7 3.1 constant_dynamic-slice_fusion.9
  356.8 2.6 reshape.58
  362.9 4.5 fusion.61
  367.5 14.6 %fusion.63 = f32[4,128,128]{2,0,1:T(4,128)S(1)} fusion(f32[4,4,8,128,128]{4,3,2,1,0:T(8,128)} %fusion.61, f32[4,128,128]{2,0,1:T(4,128)S(1)} %get-tuple-element.418, pred[]{:T(512)S(6)} %compare.3, f32[4,4,8]{2,0,1:T(4,128)S(1)} %fusion.62, s32[4,4,8]{2,0,1:T(4,128)S(1)} %get-tuple-element.402), kind=kOutput, calls=%fused_computation.14.clone.1 | convolution fusion | flops 100795392 | bytes 8913921 | tf_op jit(solution)/shard_map/while/body/eval_jaxpr/rgkt,rgkad->tad/dot_general | solution.py:54
  382.1 3.1 constant_dynamic-slice_fusion.9
  385.2 2.6 reshape.58
  391.3 4.5 fusion.61
  395.8 14.6 %fusion.63 = f32[4,128,128]{2,0,1:T(4,128)S(1)} fusion(f32[4,4,8,128,128]{4,3,2,1,0:T(8,128)} %fusion.61, f32[4,128,128]{2,0,1:T(4,128)S(1)} %get-tuple-element.418, pred[]{:T(512)S(6)} %compare.3, f32[4,4,8]{2,0,1:T(4,128)S(1)} %fusion.62, s32[4,4,8]{2,0,1:T(4,128)S(1)} %get-tuple-element.402), kind=kOutput, calls=%fused_computation.14.clone.1 | convolution fusion | flops 100795392 | bytes 8913921 | tf_op jit(solution)/shard_map/while/body/eval_jaxpr/rgkt,rgkad->tad/dot_general | solution.py:54
  410.5 3.1 constant_dynamic-slice_fusion.9
  413.5 2.6 reshape.58
  419.7 4.5 fusion.61
  424.2 14.6 %fusion.63 = f32[4,128,128]{2,0,1:T(4,128)S(1)} fusion(f32[4,4,8,128,128]{4,3,2,1,0:T(8,128)} %fusion.61, f32[4,128,128]{2,0,1:T(4,128)S(1)} %get-tuple-element.418, pred[]{:T(512)S(6)} %compare.3, f32[4,4,8]{2,0,1:T(4,128)S(1)} %fusion.62, s32[4,4,8]{2,0,1:T(4,128)S(1)} %get-tuple-element.402), kind=kOutput, calls=%fused_computation.14.clone.1 | convolution fusion | flops 100795392 | bytes 8913921 | tf_op jit(solution)/shard_map/while/body/eval_jaxpr/rgkt,rgkad->tad/dot_general | solution.py:54
  438.8 3.1 constant_dynamic-slice_fusion.9
  441.9 2.6 reshape.58
  448.0 4.5 fusion.61
  452.6 14.6 %fusion.63 = f32[4,128,128]{2,0,1:T(4,128)S(1)} fusion(f32[4,4,8,128,128]{4,3,2,1,0:T(8,128)} %fusion.61, f32[4,128,128]{2,0,1:T(4,128)S(1)} %get-tuple-element.418, pred[]{:T(512)S(6)} %compare.3, f32[4,4,8]{2,0,1:T(4,128)S(1)} %fusion.62, s32[4,4,8]{2,0,1:T(4,128)S(1)} %get-tuple-element.402), kind=kOutput, calls=%fused_computation.14.clone.1 | convolution fusion | flops 100795392 | bytes 8913921 | tf_op jit(solution)/shard_map/while/body/eval_jaxpr/rgkt,rgkad->tad/dot_general | solution.py:54
  467.2 3.1 constant_dynamic-slice_fusion.9
  470.3 2.6 reshape.58
  476.4 4.5 fusion.61
  480.9 14.6 %fusion.63 = f32[4,128,128]{2,0,1:T(4,128)S(1)} fusion(f32[4,4,8,128,128]{4,3,2,1,0:T(8,128)} %fusion.61, f32[4,128,128]{2,0,1:T(4,128)S(1)} %get-tuple-element.418, pred[]{:T(512)S(6)} %compare.3, f32[4,4,8]{2,0,1:T(4,128)S(1)} %fusion.62, s32[4,4,8]{2,0,1:T(4,128)S(1)} %get-tuple-element.402), kind=kOutput, calls=%fused_computation.14.clone.1 | convolution fusion | flops 100795392 | bytes 8913921 | tf_op jit(solution)/shard_map/while/body/eval_jaxpr/rgkt,rgkad->tad/dot_general | solution.py:54
  495.6 3.1 constant_dynamic-slice_fusion.9
  498.6 2.6 reshape.58
  504.8 4.5 fusion.61
  509.3 14.6 %fusion.63 = f32[4,128,128]{2,0,1:T(4,128)S(1)} fusion(f32[4,4,8,128,128]{4,3,2,1,0:T(8,128)} %fusion.61, f32[4,128,128]{2,0,1:T(4,128)S(1)} %get-tuple-element.418, pred[]{:T(512)S(6)} %compare.3, f32[4,4,8]{2,0,1:T(4,128)S(1)} %fusion.62, s32[4,4,8]{2,0,1:T(4,128)S(1)} %get-tuple-element.402), kind=kOutput, calls=%fused_computation.14.clone.1 | convolution fusion | flops 100795392 | bytes 8913921 | tf_op jit(solution)/shard_map/while/body/eval_jaxpr/rgkt,rgkad->tad/dot_general | solution.py:54
  524.0 3.1 constant_dynamic-slice_fusion.9
  533.1 4.5 fusion.61
  537.7 14.6 %fusion.63 = f32[4,128,128]{2,0,1:T(4,128)S(1)} fusion(f32[4,4,8,128,128]{4,3,2,1,0:T(8,128)} %fusion.61, f32[4,128,128]{2,0,1:T(4,128)S(1)} %get-tuple-element.418, pred[]{:T(512)S(6)} %compare.3, f32[4,4,8]{2,0,1:T(4,128)S(1)} %fusion.62, s32[4,4,8]{2,0,1:T(4,128)S(1)} %get-tuple-element.402), kind=kOutput, calls=%fused_computation.14.clone.1 | convolution fusion | flops 100795392 | bytes 8913921 | tf_op jit(solution)/shard_map/while/body/eval_jaxpr/rgkt,rgkad->tad/dot_general | solution.py:54
  552.3 3.1 constant_dynamic-slice_fusion.9
  561.5 4.5 fusion.61
  566.0 14.6 %fusion.63 = f32[4,128,128]{2,0,1:T(4,128)S(1)} fusion(f32[4,4,8,128,128]{4,3,2,1,0:T(8,128)} %fusion.61, f32[4,128,128]{2,0,1:T(4,128)S(1)} %get-tuple-element.418, pred[]{:T(512)S(6)} %compare.3, f32[4,4,8]{2,0,1:T(4,128)S(1)} %fusion.62, s32[4,4,8]{2,0,1:T(4,128)S(1)} %get-tuple-element.402), kind=kOutput, calls=%fused_computation.14.clone.1 | convolution fusion | flops 100795392 | bytes 8913921 | tf_op jit(solution)/shard_map/while/body/eval_jaxpr/rgkt,rgkad->tad/dot_general | solution.py:54
  580.7 3.1 constant_dynamic-slice_fusion.9
  589.9 4.5 fusion.61
  594.4 14.6 %fusion.63 = f32[4,128,128]{2,0,1:T(4,128)S(1)} fusion(f32[4,4,8,128,128]{4,3,2,1,0:T(8,128)} %fusion.61, f32[4,128,128]{2,0,1:T(4,128)S(1)} %get-tuple-element.418, pred[]{:T(512)S(6)} %compare.3, f32[4,4,8]{2,0,1:T(4,128)S(1)} %fusion.62, s32[4,4,8]{2,0,1:T(4,128)S(1)} %get-tuple-element.402), kind=kOutput, calls=%fused_computation.14.clone.1 | convolution fusion | flops 100795392 | bytes 8913921 | tf_op jit(solution)/shard_map/while/body/eval_jaxpr/rgkt,rgkad->tad/dot_general | solution.py:54
  609.1 3.1 constant_dynamic-slice_fusion.9
  618.2 4.5 fusion.61
  622.8 14.6 %fusion.63 = f32[4,128,128]{2,0,1:T(4,128)S(1)} fusion(f32[4,4,8,128,128]{4,3,2,1,0:T(8,128)} %fusion.61, f32[4,128,128]{2,0,1:T(4,128)S(1)} %get-tuple-element.418, pred[]{:T(512)S(6)} %compare.3, f32[4,4,8]{2,0,1:T(4,128)S(1)} %fusion.62, s32[4,4,8]{2,0,1:T(4,128)S(1)} %get-tuple-element.402), kind=kOutput, calls=%fused_computation.14.clone.1 | convolution fusion | flops 100795392 | bytes 8913921 | tf_op jit(solution)/shard_map/while/body/eval_jaxpr/rgkt,rgkad->tad/dot_general | solution.py:54
  637.4 3.1 constant_dynamic-slice_fusion.9
  646.6 4.5 fusion.61
  651.2 14.6 %fusion.63 = f32[4,128,128]{2,0,1:T(4,128)S(1)} fusion(f32[4,4,8,128,128]{4,3,2,1,0:T(8,128)} %fusion.61, f32[4,128,128]{2,0,1:T(4,128)S(1)} %get-tuple-element.418, pred[]{:T(512)S(6)} %compare.3, f32[4,4,8]{2,0,1:T(4,128)S(1)} %fusion.62, s32[4,4,8]{2,0,1:T(4,128)S(1)} %get-tuple-element.402), kind=kOutput, calls=%fused_computation.14.clone.1 | convolution fusion | flops 100795392 | bytes 8913921 | tf_op jit(solution)/shard_map/while/body/eval_jaxpr/rgkt,rgkad->tad/dot_general | solution.py:54
  666.5 31.5 %all-reduce.2.cloned.1.call-done = f32[512,128]{1,0:T(8,128)} async-done(((f32[512,128]{1,0:T(8,128)}), f32[512,128]{1,0:T(8,128)}) %all-reduce.2.cloned.1.call-update) | async-done | bytes 262160 | tf_op jit(solution)/shard_map/psum | solution.py:78
  (160 shorter events, 75.9 us)
Async XLA Ops:
  6.5 1.0 copy-start
  6.5 205.3 %all-gather.2.cloned.1.call-start = ((), (), s32[]{:S(2)}) async-start(), calls=%async_computation.1 | async-start | bytes 34078720 | tf_op jit(solution)/shard_map/all_gather | solution.py:63
  22.9 675.1 %all-reduce.2.cloned.1.call-start = ((), (), s32[]{:S(2)}) async-start(), calls=%async_computation.2 | async-start | bytes 524288 | tf_op jit(solution)/shard_map/psum | solution.py:78
  22.9 7.4 %copy-start.4 = (s32[4,1,64,8]{2,3,1,0:T(8,128)S(1)}, s32[4,1,64,8]{2,3,1,0:T(8,128)}, u32[]{:S(2)}) copy-start(s32[4,1,64,8]{2,3,1,0:T(8,128)} %param.13) | copy-start | bytes 24580
  23.0 7.5 %copy-start.5 = (s32[4,1,64,8]{2,3,1,0:T(8,128)S(1)}, s32[4,1,64,8]{2,3,1,0:T(8,128)}, u32[]{:S(2)}) copy-start(s32[4,1,64,8]{2,3,1,0:T(8,128)} %param.15) | copy-start | bytes 24580
  23.0 7.6 %copy-start.6 = (s32[4,1,64,8]{2,3,1,0:T(8,128)S(1)}, s32[4,1,64,8]{2,3,1,0:T(8,128)}, u32[]{:S(2)}) copy-start(s32[4,1,64,8]{2,3,1,0:T(8,128)} %param.14) | copy-start | bytes 24580
  23.0 7.7 %copy-start.7 = (s32[4,1,64]{2,1,0:T(1,128)S(1)}, s32[4,1,64]{2,1,0:T(1,128)}, u32[]{:S(2)}) copy-start(s32[4,1,64]{2,1,0:T(1,128)} %param.16) | copy-start | bytes 3076
  211.8 486.1 %copy-start.2 = (bf16[1,1,256,128]{3,2,1,0:T(8,128)(2,1)S(1)}, bf16[1,1,256,128]{3,2,1,0:T(8,128)(2,1)}, u32[]{:S(2)}) copy-start(bf16[1,1,256,128]{3,2,1,0:T(8,128)(2,1)} %param.10) | copy-start | bytes 196612
  211.9 486.1 %copy-start.3 = (bf16[128,128]{1,0:T(8,128)(2,1)S(1)}, bf16[128,128]{1,0:T(8,128)(2,1)}, u32[]{:S(2)}) copy-start(bf16[128,128]{1,0:T(8,128)(2,1)} %param.12) | copy-start | bytes 98308
  217.6 2.2 copy-start.1
  245.9 2.2 copy-start.1
  274.3 2.2 copy-start.1
  302.7 2.2 copy-start.1
  331.1 2.2 copy-start.1
  359.4 2.2 copy-start.1
  387.8 2.2 copy-start.1
  416.2 2.2 copy-start.1
  444.5 2.2 copy-start.1
  472.9 2.2 copy-start.1
  501.3 2.2 copy-start.1
  529.6 2.2 copy-start.1
  558.0 2.2 copy-start.1
  586.4 2.2 copy-start.1
  614.8 2.2 copy-start.1
  643.1 2.2 copy-start.1
Sparse Core Ops, SparseCore 0:
  23.0 188.7 all-gather.1
  666.6 31.2 all-reduce.1
where the time goes:
time: 709 us; the launch traced here: 706 us
  matrix products  357 us (50%)
  waiting for transfers between devices  213 us (30%)
  local copies, waits for them, and re-layouts  108 us (15%)
  between operations  13.5 us (2%)
  blocking collectives  13.2 us (2%)
    dot_general x16, matrix products, apply_group(): jnp.einsum('rgkt,rgkad->tad', onehot, product, precision=lax.Precision.HI...  233 us
    all_gather x1, waiting for transfers between devices, shards(): piece = lax.all_gather(mine, 'blk', axis=1, tiled=True)  181 us
    dot_general x16, matrix products, apply_group(): jnp.einsum('rgkab,rgkbd->rgkad', weights, picked, preferred_element_type=...  71.4 us
    dynamic_slice x16, local copies, waits for them, and re-layouts, fetch(): lax.dynamic_slice_in_dim(piece, offset * block_rows, group * block_rows, 1)  49 us
    reshape x16, local copies, waits for them, and re-layouts, apply_group(): hidden_group.reshape(rel_dev, group, tiles_block, tile_size * width)  42 us
    psum x1, waiting for transfers between devices, shards(): summed = lax.psum(partial_rows, 'chan')  31.5 us
    dot_general x16, matrix products, apply_group(): jnp.einsum('rgks,rgsx->rgkx', pick_cols, flat_hidden, preferred_element_t...  28.2 us
    dot_general x16, matrix products, apply_group(): jnp.einsum('rgkp,rpx->rgkx', pick_ids, pool_flat, preferred_element_type=...  20.7 us
  transfers between devices with their start and end apart: 2, of which 2 were waited for; matrix products, arithmetic and copies ran while one was open for 1% of the time, Pallas kernels for 0%

commit v1 on v0

v1 whole, which is shorter than its diff:
```python
import functools

import jax
import jax.numpy as jnp
from jax import lax
from jax.experimental import pallas as pl
from jax.experimental.pallas import tpu as pltpu
from jax.sharding import Mesh, PartitionSpec as P

SIDE = 4
TILE = 128
RELS = 4
POOL = 32
TPB = 4
SLOTS = 8
BLOCKS = 64
ZERO = RELS * POOL
UNIT = 4
WIDE = (16, 16, 8, 8)
SIZES = (2, 4, 1, 1)
STAGES = len(SIZES)


def most_chunks(st):
    most = (RELS * 64 * SIZES[st] + (UNIT - 1) * RELS * TPB) // UNIT
    return -(-most // WIDE[st]) * WIDE[st]


STARTS = tuple(sum(most_chunks(i) for i in range(st)) for st in range(STAGES + 1))
PAY_ROWS = -(-STARTS[-1] * UNIT // (8 * TILE)) * 8
TAB_ROWS = 8
GROUPS = STAGES * RELS * TPB

FLAT = ("chan", "y", "z", "xl", "core")


def flat_index(x, y, z, core):
    return ((((x // 2) * SIDE + y) * SIDE + z) * 2 + x % 2) * 2 + core


def shift(axis_first, axis_second, by):
    pairs = []
    for x in range(SIDE):
        for y in range(SIDE):
            for z in range(SIDE):
                for core in range(2):
                    to = [x, y, z]
                    axis = (axis_first, axis_second)[core]
                    to[axis] = (to[axis] + by) % SIDE
                    pairs.append((flat_index(x, y, z, core), flat_index(*to, core)))
    return pairs


def ring(rows, axis_first, axis_second):
    return [rows] + [lax.ppermute(rows, FLAT, shift(axis_first, axis_second, by)) for by in (1, -1, 2)]


def sibling(rows):
    return lax.ppermute(rows, "core", [(0, 1), (1, 0)])


SMEM = pl.BlockSpec(memory_space=pltpu.SMEM)
VMEM = pl.BlockSpec(memory_space=pltpu.VMEM)
ANY = pl.BlockSpec(memory_space=pl.ANY)


def iota(shape, axis):
    return lax.broadcasted_iota(jnp.int32, shape, axis)


def exact_dot(left, right):
    return jnp.dot(left.astype(jnp.bfloat16), right.astype(jnp.bfloat16), preferred_element_type=jnp.float32)


def sort_kernel(here_ref, packed_ref, pay_ref, tab_ref):
    shape = (SLOTS, BLOCKS)
    my_x, my_y, my_z, my_core = (here_ref[i] for i in range(4))
    block, slot = iota(shape, 1), iota(shape, 0)
    y, z, low, core = block >> 4, (block >> 2) & 3, (block >> 1) & 1, block & 1

    def place(offset):
        offset = offset & 3
        return jnp.where(offset == 0, 0, jnp.where(offset == 3, 1, offset + 1))

    dy, dz = place(y - my_y), place(z - my_z)
    second, third = jnp.where(core == 0, dy, dz), jnp.where(core == 0, dz, dy)
    other = jnp.where(core == my_core, 0, 1)
    stage = jnp.where(third == 0, 0, jnp.where(third == 3, 2 + other, 1))
    buf = jnp.where(third == 0, other, jnp.where(third == 3, 0, (third - 1) * 2 + other))
    lists, at, ids = [], [], []
    for r in range(RELS):
        packed = packed_ref[r]
        cols = (packed >> 2) & 3
        ids.append((packed >> 4) & 31)
        dx = place((cols >> 1) * 2 + low - my_x)
        at.append(buf * 32 + (second * 4 + dx) * 2 + (cols & 1))
        live = slot < (packed >> 9)
        lists.append(jnp.where(live, stage * TPB + (packed & 3), STAGES * TPB))
    members = [
        jnp.where(lists[r] == st * TPB + t, 1.0, 0.0)
        for st in range(STAGES)
        for r in range(RELS)
        for t in range(TPB)
    ]
    member = jnp.concatenate(members, 0)
    lanes = (BLOCKS, BLOCKS)
    ahead = exact_dot(member, jnp.where(iota(lanes, 0) < iota(lanes, 1), 1.0, 0.0))
    row_sum = exact_dot(member, jnp.ones((BLOCKS, TILE), jnp.float32))
    wide = (GROUPS * SLOTS, GROUPS * SLOTS)
    row, col = iota(wide, 0), iota(wide, 1)
    same = (row >> 3) == (col >> 3)
    above = exact_dot(jnp.where(same & (col < row), 1.0, 0.0), row_sum)
    length = exact_dot(jnp.where(same, 1.0, 0.0), row_sum)
    chunks = ((length.astype(jnp.int32) + (UNIT - 1)) >> 2).astype(jnp.float32)
    earlier = ((row >> 7) == (col >> 7)) & ((col >> 3) < (row >> 3)) & ((col & 7) == 0)
    begin = exact_dot(jnp.where(earlier, 1.0, 0.0), chunks)
    step = iota(begin.shape, 0) >> 7
    base = jnp.where(step == 0, STARTS[0], jnp.where(step == 1, STARTS[1], jnp.where(step == 2, STARTS[2], STARTS[3])))
    begin = begin + base.astype(jnp.float32)
    end = (begin + chunks).astype(jnp.int32)
    pos = member * ((begin * UNIT + above)[:, :BLOCKS] + ahead)

    out = jnp.zeros((PAY_ROWS, 2 * TILE), jnp.float32)
    for r in range(RELS):
        where = jnp.zeros(shape, jnp.float32)
        for st in range(STAGES):
            for t in range(TPB):
                first = ((st * RELS + r) * TPB + t) * SLOTS
                where = where + pos[first : first + SLOTS]
        where = jnp.where(lists[r] == STAGES * TPB, -1, where.astype(jnp.int32))
        high, low_part = where >> 7, where & 127
        weight = (ids[r] + (r * POOL - ZERO)).astype(jnp.float32)
        source = at[r].astype(jnp.float32)
        for k in range(SLOTS):
            left = jnp.where(iota((PAY_ROWS, BLOCKS), 0) == high[k : k + 1], 1.0, 0.0)
            hit = iota((TILE, BLOCKS), 0) == low_part[k : k + 1]
            right = jnp.concatenate(
                [jnp.where(hit, weight[k : k + 1], 0.0), jnp.where(hit, source[k : k + 1], 0.0)], 0
            )
            out = out + lax.dot_general(
                left.astype(jnp.bfloat16),
                right.astype(jnp.bfloat16),
                (((1,), (1,)), ((), ())),
                preferred_element_type=jnp.float32,
            )
    out = out.astype(jnp.int32)
    pay_ref[...] = ((out[:, :TILE] + ZERO) << 7) | out[:, TILE:]

    index = iota((TAB_ROWS, TILE), 0) * TILE + iota((TAB_ROWS, TILE), 1)
    table = jnp.zeros((TAB_ROWS, TILE), jnp.int32)
    for st in range(STAGES):
        tile = jnp.zeros((TAB_ROWS, TILE), jnp.int32)
        for g in range(RELS * TPB):
            first = (st * RELS * TPB + g) * SLOTS
            tile = tile + jnp.where(index >= end[first : first + SLOTS], 1, 0)
        inside = (index >= STARTS[st]) & (index < STARTS[st + 1])
        table = jnp.where(inside, jnp.minimum(tile, RELS * TPB - 1), table)
        last = (st * RELS * TPB + RELS * TPB - 1) * SLOTS
        total = end[last : last + SLOTS] - STARTS[st]
        table = jnp.where(index == (TAB_ROWS - 1) * TILE + st, total, table)
    tab_ref[...] = table


def sort_slots(here, packed):
    return pl.pallas_call(
        sort_kernel,
        out_shape=[
            jax.ShapeDtypeStruct((PAY_ROWS, TILE), jnp.int32),
            jax.ShapeDtypeStruct((TAB_ROWS, TILE), jnp.int32),
        ],
        in_specs=[SMEM, VMEM],
        out_specs=[VMEM] * 2,
        compiler_params=pltpu.CompilerParams(vmem_limit_bytes=24 << 20),
        cost_estimate=pl.CostEstimate(flops=0, bytes_accessed=8 << 20, transcendentals=0),
        name="sort_slots",
    )(here, packed)


def stage_kernel(st, count, first, last, *refs):
    refs = list(refs)
    pay, tab = refs[:2]
    del refs[:2]
    if last:
        chan = refs.pop(0)
    pool = refs.pop(0)
    bufs = refs[:count]
    del refs[:count]
    copies = []
    if first:
        total, full, *refs = refs
        copies.append((pool, full.at[pl.ds(0, ZERO)]))
        full[ZERO] = jnp.zeros((TILE, TILE), full.dtype)
        total[...] = jnp.zeros_like(total)
        pool = full
    else:
        before = refs.pop(0)
        if last:
            transforms, selfterm, mine, theirs, total, agg, *refs = refs
            total[...] = before[...]
        else:
            total = refs.pop(0)
    if count > 1:
        rows, sems = refs
        for i, buf in enumerate(bufs):
            size = buf.shape[0]
            copies.append((buf, rows.at[pl.ds(i * size, size)]))
        copies = [pltpu.make_async_copy(*copy, sems.at[i]) for i, copy in enumerate(copies)]
        for copy in copies:
            copy.start()
        for copy in copies:
            copy.wait()
    else:
        rows = bufs[0]

    def turn(i, _):
        for c in range(WIDE[st]):
            chunk = STARTS[st] + i * WIDE[st] + c
            left, right = [], []
            for u in range(UNIT):
                value = pay[chunk >> 5, (chunk & 31) * UNIT + u]
                left.append(pool[value >> 7])
                right.append(rows[value & 127])
            total[tab[chunk >> 7, chunk & 127]] += jnp.dot(
                jnp.concatenate(left, 1), jnp.concatenate(right, 0), preferred_element_type=jnp.float32
            )
        return 0

    turns = (tab[TAB_ROWS - 1, st] + (WIDE[st] - 1)) >> (WIDE[st].bit_length() - 1)
    lax.fori_loop(0, turns, turn, 0)
    if last:
        for t in range(TPB):
            acc = None
            for r in range(RELS):
                part = jnp.dot(
                    total[r * TPB + t].astype(jnp.bfloat16), transforms[r], preferred_element_type=jnp.float32
                )
                acc = part if acc is None else acc + part
            agg[t] = acc
        half = TPB // 2
        for u in range(half):
            mine[u] = agg[chan[0] * half + u] + selfterm[u]
            theirs[u] = agg[(1 - chan[0]) * half + u].astype(jnp.bfloat16)


def run_stage(st, lists, pool, bufs, before=None, tail=None):
    first, last = before is None, tail is not None
    args, specs = list(lists), [SMEM] * 2
    if last:
        args.append(tail[0])
        specs.append(SMEM)
    args += [pool, *bufs]
    specs += [ANY if first else VMEM] + [ANY if len(bufs) > 1 else VMEM] * len(bufs)
    wide = (RELS * TPB, TILE, TILE)
    scratch, aliases = [], {}
    if first:
        out = [
            jax.ShapeDtypeStruct(wide, jnp.float32),
            jax.ShapeDtypeStruct((ZERO + 1, TILE, TILE), pool.dtype),
        ]
    else:
        args.append(before)
        specs.append(VMEM)
        if last:
            args += tail[1:]
            specs += [VMEM] * 2
            half = (TPB // 2, TILE, TILE)
            out = [jax.ShapeDtypeStruct(half, jnp.float32), jax.ShapeDtypeStruct(half, jnp.bfloat16)]
            scratch = [pltpu.VMEM(wide, jnp.float32), pltpu.VMEM((TPB, TILE, TILE), jnp.float32)]
        else:
            out = [jax.ShapeDtypeStruct(wide, jnp.float32)]
            aliases = {len(args) - 1: 0}
    if len(bufs) > 1:
        scratch.append(pltpu.VMEM((32 * SIZES[st], TILE, TILE), jnp.bfloat16))
        scratch.append(pltpu.SemaphoreType.DMA((len(bufs) + 1,)))
    slots = 16 * 8 * SIZES[st]
    return pl.pallas_call(
        functools.partial(stage_kernel, st, len(bufs), first, last),
        out_shape=out,
        in_specs=specs,
        out_specs=[VMEM] * len(out),
        scratch_shapes=scratch,
        input_output_aliases=aliases,
        compiler_params=pltpu.CompilerParams(vmem_limit_bytes=24 << 20),
        cost_estimate=pl.CostEstimate(
            flops=slots * 2 * TILE**3 * 4, bytes_accessed=(6 + SIZES[st]) << 20, transcendentals=0
        ),
        name=f"stage{st}",
    )(*args)


def shards(features, transforms, self_weight, tile_rows, tile_cols, tile_ids, tile_count, tile_pool):
    chan, xl = lax.axis_index("chan"), lax.axis_index("xl")
    own = features[0, 0]
    half_rows, width = own.shape
    here = jnp.stack(
        [chan * 2 + xl, lax.axis_index("y"), lax.axis_index("z"), lax.axis_index("core")]
    ).astype(jnp.int32)

    def by_slot(table):
        return table[:, 0].transpose(0, 2, 1)

    line = jnp.concatenate(ring(own, 0, 0), 0)
    selfterm = jnp.dot(own, self_weight, preferred_element_type=jnp.float32).reshape(-1, TILE, width)
    now = lax.dynamic_slice_in_dim(transforms, chan * RELS, RELS, 0)
    packed = by_slot(tile_rows) | (by_slot(tile_cols) << 2) | (by_slot(tile_ids) << 4)
    packed = packed | (tile_count[:, 0][:, None, :] << 9)
    line, packed, selfterm, now = lax.optimization_barrier((line, packed, selfterm, now))
    plane = jnp.concatenate(ring(line, 1, 2), 0)
    lists = sort_slots(here, packed)
    plane, lists = lax.optimization_barrier((plane, lists))
    plane = plane.reshape(-1, TILE, width)
    left = lax.ppermute(plane, FLAT, shift(2, 1, 1))
    right = lax.ppermute(plane, FLAT, shift(2, 1, -1))
    pool = tile_pool.reshape(RELS * POOL, TILE, TILE)
    total, pool = run_stage(0, lists, pool, [plane, sibling(plane)])
    left, right, total = lax.optimization_barrier((left, right, total))
    half = plane.shape[0] // 2
    far = [
        lax.ppermute(left[:half], FLAT, shift(2, 1, 1)),
        lax.ppermute(right[half:], FLAT, shift(2, 1, -1)),
    ]
    total = run_stage(1, lists, pool, [left, sibling(left), right, sibling(right)], total)[0]
    *far, total = lax.optimization_barrier((*far, total))
    beyond = [sibling(piece) for piece in far]
    total = run_stage(2, lists, pool, far, total)[0]
    kept, sent = run_stage(3, lists, pool, beyond, total, (here[:1] >> 1, now, selfterm))
    got = lax.ppermute(sent, "chan", [(0, 1), (1, 0)])
    updated = jax.nn.relu(kept + got.astype(jnp.float32)).astype(jnp.bfloat16)
    return updated.reshape(1, 1, half_rows, width)


def solution(mesh):
    fine = Mesh(mesh.devices.reshape(2, SIDE, SIDE, 2, 2), FLAT)
    blk = ("y", "z", "xl", "core")
    placed = (
        P(blk, "chan", None, None),
        P(),
        P(),
        P("chan", blk, None, None),
        P("chan", blk, None, None),
        P("chan", blk, None, None),
        P("chan", blk, None),
        P("chan", blk, None, None, None),
    )
    return jax.shard_map(
        shards, mesh=fine, in_specs=placed, out_specs=P(blk, "chan", None, None), check_vma=False
    )
```

time: 709 us -> 67.5 us (0.10)
  matrix products: 357 us -> 0.98 us
  waiting for transfers between devices: 213 us -> 14.6 us
  local copies, waits for them, and re-layouts: 108 us -> 2.29 us
  Pallas kernels: 0 us -> 23.4 us
  starting transfers between devices: 0.04 us -> 22.8 us
  between operations: 13.5 us -> 0.15 us
  blocking collectives: 13.2 us -> 0 us
    dot_general x66 -> x1, matrix products: 357 us -> 0.98 us  [shards(): jnp.dot(own, self_weight, preferred_element_type=jnp.float32)]
    all_gather x1 -> x0, waiting for transfers between devices: 181 us -> none  [shards(): piece = lax.all_gather(mine, 'blk', axis=1, tiled=True)]
    dynamic_slice x64 -> x1, local copies, waits for them, and re-layouts: 49.5 us -> 0.02 us  [shards(): now = lax.dynamic_slice_in_dim(transforms, chan * RELS, RELS, 0)]
    reshape x16 -> x0, local copies, waits for them, and re-layouts: 42 us -> none  [apply_group(): hidden_group.reshape(rel_dev, group, tiles_block, tile_size * width)]
    psum x1 -> x0, waiting for transfers between devices: 31.5 us -> none  [shards(): summed = lax.psum(partial_rows, 'chan')]
    pallas_call x0 -> x5, Pallas kernels: none -> 23.4 us  [the longest x4 20.4 us: run_stage(): pl.pallas_call(functools.partial(stage_kernel, st, len(bufs), first, last...]
    ppermute x0 -> x16, starting transfers between devices: none -> 22.8 us  [the longest x6 10.3 us: ring(): lax.ppermute(rows, FLAT, shift(axis_first, axis_second, by))]
    ppermute x0 -> x16, waiting for transfers between devices: none -> 14.6 us  [the longest x1 5.19 us: shards(): left = lax.ppermute(plane, FLAT, shift(2, 1, 1))]
  transfers between devices with their start and end apart: 2 -> 16, of which waited for: 2 -> 7; matrix products, arithmetic and copies ran while one was open for 1% -> 4% of each run, Pallas kernels for 0% -> 29%
where the time goes in v1:
time: 67.5 us; the launch traced here: 67.4 us
  Pallas kernels  23.4 us (35%)
  starting transfers between devices  22.8 us (34%)
  waiting for transfers between devices  14.6 us (22%)
  other arithmetic  3.1 us (5%)
  local copies, waits for them, and re-layouts  2.29 us (3%)
  matrix products  0.98 us (1%)
    pallas_call x4, Pallas kernels, run_stage(): pl.pallas_call(functools.partial(stage_kernel, st, len(bufs), first, last...  20.4 us
    ppermute x6, starting transfers between devices, ring(): lax.ppermute(rows, FLAT, shift(axis_first, axis_second, by))  10.3 us
    ppermute x5, starting transfers between devices, sibling(): return lax.ppermute(rows, 'core', [(0, 1), (1, 0)])  5.96 us
    ppermute x1, waiting for transfers between devices, shards(): left = lax.ppermute(plane, FLAT, shift(2, 1, 1))  5.19 us
    ppermute x6, waiting for transfers between devices, ring(): lax.ppermute(rows, FLAT, shift(axis_first, axis_second, by))  4.35 us
    ppermute x1, waiting for transfers between devices, shards(): got = lax.ppermute(sent, 'chan', [(0, 1), (1, 0)])  3.18 us
    pallas_call x1, Pallas kernels, sort_slots(): pl.pallas_call(sort_kernel, out_shape=[jax.ShapeDtypeStruct((PAY_ROWS, TI...  2.98 us
    unnamed x4, local copies, waits for them, and re-layouts  2.19 us
  transfers between devices with their start and end apart: 16, of which 7 were waited for; matrix products, arithmetic and copies ran while one was open for 4% of the time, Pallas kernels for 29%

profile of v1, /device:TPU:1, one launch (start us, length us, event | category | flops | bytes accessed | tf_op | source)
XLA Modules:
  0.0 67.4 jit_solution(3902314008718857125)
XLA Ops:
  0.0 0.0 copy-start
  0.0 2.0 %collective-permute-start = (bf16[256,128]{1,0:T(8,128)(2,1)}, bf16[256,128]{1,0:T(8,128)(2,1)S(1)}, u32[]{:S(2)}, u32[]{:S(2)}) collective-permute-start(bf16[256,128]{1,0:T(8,128)(2,1)} %bitcast.39), channel_id=1, source_target_pairs={{0,2},{1,3},{4,6},{5,7},{8,10},{9,11},{12,14},{13,15},{16,18},{17,... | collective-permute-start | bytes 196616 | tf_op jit(solution)/shard_map/ppermute | solution.py:55
  2.0 1.3 %collective-permute-start.1 = (bf16[256,128]{1,0:T(8,128)(2,1)}, bf16[256,128]{1,0:T(8,128)(2,1)S(1)}, u32[]{:S(2)}, u32[]{:S(2)}) collective-permute-start(bf16[256,128]{1,0:T(8,128)(2,1)} %bitcast.40), channel_id=1, source_target_pairs={{0,66},{1,67},{4,70},{5,71},{8,74},{9,75},{12,78},{13,79},{16,82},... | collective-permute-start | bytes 196616 | tf_op jit(solution)/shard_map/ppermute | solution.py:55
  3.4 1.7 %collective-permute-start.2 = (bf16[256,128]{1,0:T(8,128)(2,1)}, bf16[256,128]{1,0:T(8,128)(2,1)S(1)}, u32[]{:S(2)}, u32[]{:S(2)}) collective-permute-start(bf16[256,128]{1,0:T(8,128)(2,1)} %bitcast.41), channel_id=1, source_target_pairs={{0,64},{1,65},{4,68},{5,69},{8,72},{9,73},{12,76},{13,77},{16,80},... | collective-permute-start | bytes 196616 | tf_op jit(solution)/shard_map/ppermute | solution.py:55
  5.0 0.7 %broadcast_shift-left_fusion = s32[4,1,64]{2,1,0:T(1,128)S(1)} fusion(s32[4,1,64]{2,1,0:T(1,128)} %param.14), kind=kLoop, calls=%fused_computation.11 | loop fusion | flops 256 | bytes 2048 | tf_op jit(solution)/shard_map/shift_left | solution.py:306
  5.7 1.0 %fusion.refs_8_ = f32[2,128,128]{2,1,0:T(8,128)S(1)} fusion(bf16[2,128,128]{2,1,0:T(8,128)(2,1)} %bitcast.42, bf16[128,128]{1,0:T(8,128)(2,1)} %param.10), kind=kOutput, calls=%fused_computation.3 | convolution fusion | flops 8388608 | bytes 229376 | tf_op jit(solution)/shard_map/dot_general | solution.py:303
  6.7 0.8 %fusion.2.packed_ref = s32[4,8,64]{2,1,0:T(8,128)S(1)} fusion(s32[4,1,64,8]{2,3,1,0:T(8,128)} %param.13, s32[4,1,64,8]{2,3,1,0:T(8,128)} %param.12, s32[4,1,64,8]{2,3,1,0:T(8,128)} %param.11, s32[4,64]{1,0:T(4,128)S(1)} %bitcast.44), kind=kLoop, calls=%fused_computation.6 | loop fusion | flops 10240 | bytes 33792 | tf_op jit(solution)/shard_map/or | solution.py:306
  7.5 0.0 copy-done
  7.5 0.0 collective-permute-done
  7.5 0.0 collective-permute-done.1
  7.5 0.7 %collective-permute-done.2 = bf16[256,128]{1,0:T(8,128)(2,1)S(1)} collective-permute-done((bf16[256,128]{1,0:T(8,128)(2,1)}, bf16[256,128]{1,0:T(8,128)(2,1)S(1)}, u32[]{:S(2)}, u32[]{:S(2)}) %collective-permute-start.2) | collective-permute-done | bytes 65568 | tf_op jit(solution)/shard_map/ppermute | solution.py:55
  8.2 0.9 %pad_maximum_fusion.1 = bf16[1024,128]{1,0:T(8,128)(2,1)S(1)} fusion(bf16[256,128]{1,0:T(8,128)(2,1)S(1)} %collective-permute-done.2, bf16[256,128]{1,0:T(8,128)(2,1)S(1)} %collective-permute-done.1, bf16[256,128]{1,0:T(8,128)(2,1)S(1)} %collective-permute-done, bf16[256,128]{1,0:T(8,128)(2,1)} %bitcast.43), kind=kLoop, calls=%fused_computation.1 | loop fusion | flops 1048576 | bytes 524288 | tf_op jit(solution)/shard_map/concatenate | solution.py:302
  9.1 1.8 %collective-permute-start.3 = (bf16[1024,128]{1,0:T(8,128)(2,1)S(1)}, bf16[1024,128]{1,0:T(8,128)(2,1)S(1)}, u32[]{:S(2)}, u32[]{:S(2)}) collective-permute-start(bf16[1024,128]{1,0:T(8,128)(2,1)S(1)} %pad_maximum_fusion.1), channel_id=1, source_target_pairs={{0,16},{1,5},{4,20},{5,9},{8,24},{9,13},{12,28},{13,1},{16,32},{17... | collective-permute-start | bytes 786440 | tf_op jit(solution)/shard_map/ppermute | solution.py:55
  10.9 2.2 %collective-permute-start.4 = (bf16[1024,128]{1,0:T(8,128)(2,1)S(1)}, bf16[1024,128]{1,0:T(8,128)(2,1)S(1)}, u32[]{:S(2)}, u32[]{:S(2)}) collective-permute-start(bf16[1024,128]{1,0:T(8,128)(2,1)S(1)} %pad_maximum_fusion.1), channel_id=1, source_target_pairs={{0,48},{1,13},{4,52},{5,1},{8,56},{9,5},{12,60},{13,9},{16,0},{17,... | collective-permute-start | bytes 786440 | tf_op jit(solution)/shard_map/ppermute | solution.py:55
  13.1 1.2 %collective-permute-start.5 = (bf16[1024,128]{1,0:T(8,128)(2,1)S(1)}, bf16[1024,128]{1,0:T(8,128)(2,1)S(1)}, u32[]{:S(2)}, u32[]{:S(2)}) collective-permute-start(bf16[1024,128]{1,0:T(8,128)(2,1)S(1)} %pad_maximum_fusion.1), channel_id=1, source_target_pairs={{0,32},{1,9},{4,36},{5,13},{8,40},{9,1},{12,44},{13,5},{16,48},{17... | collective-permute-start | bytes 786440 | tf_op jit(solution)/shard_map/ppermute | solution.py:55
  14.3 0.1 pad_add_fusion.here_ref
  14.4 3.0 %sort_slots.1 = (s32[24,128]{1,0:T(8,128)S(1)}, s32[8,128]{1,0:T(8,128)S(1)}) custom-call(s32[4]{0:T(128)S(1)} %pad_add_fusion.here_ref, s32[4,8,64]{2,1,0:T(8,128)S(1)} %fusion.2.packed_ref), custom_call_target="tpu_custom_call" | custom-call | bytes 8388608 | tf_op jit(solution)/shard_map/sort_slots/pallas_call | solution.py:165
  17.4 0.0 collective-permute-done.3
  17.4 1.8 %collective-permute-done.4 = bf16[1024,128]{1,0:T(8,128)(2,1)S(1)} collective-permute-done((bf16[1024,128]{1,0:T(8,128)(2,1)S(1)}, bf16[1024,128]{1,0:T(8,128)(2,1)S(1)}, u32[]{:S(2)}, u32[]{:S(2)}) %collective-permute-start.4) | collective-permute-done | bytes 262176 | tf_op jit(solution)/shard_map/ppermute | solution.py:55
  19.2 1.8 %collective-permute-done.5 = bf16[1024,128]{1,0:T(8,128)(2,1)S(1)} collective-permute-done((bf16[1024,128]{1,0:T(8,128)(2,1)S(1)}, bf16[1024,128]{1,0:T(8,128)(2,1)S(1)}, u32[]{:S(2)}, u32[]{:S(2)}) %collective-permute-start.5) | collective-permute-done | bytes 262176 | tf_op jit(solution)/shard_map/ppermute | solution.py:55
  21.1 0.1 pad_maximum_fusion
  21.1 2.3 %collective-permute-start.6 = (bf16[32,128,128]{2,1,0:T(8,128)(2,1)S(1)}, bf16[32,128,128]{2,1,0:T(8,128)(2,1)S(1)}, u32[]{:S(2)}, u32[]{:S(2)}) collective-permute-start(bf16[32,128,128]{2,1,0:T(8,128)(2,1)S(1)} %bitcast.34), channel_id=1, source_target_pairs={{0,1},{1,0},{2,3},{3,2},{4,5},{5,4},{6,7},{7,6},{8,9},{9,8},{10,11... | collective-permute-start | bytes 3145736 | tf_op jit(solution)/shard_map/ppermute | solution.py:59
  23.4 1.1 %collective-permute-start.7 = (bf16[32,128,128]{2,1,0:T(8,128)(2,1)S(1)}, bf16[32,128,128]{2,1,0:T(8,128)(2,1)S(1)}, u32[]{:S(2)}, u32[]{:S(2)}) collective-permute-start(bf16[32,128,128]{2,1,0:T(8,128)(2,1)S(1)} %bitcast.35), channel_id=1, source_target_pairs={{0,4},{1,17},{4,8},{5,21},{8,12},{9,25},{12,0},{13,29},{16,20},{17... | collective-permute-start | bytes 3145736 | tf_op jit(solution)/shard_map/ppermute | solution.py:312
  24.6 1.5 %collective-permute-start.8 = (bf16[32,128,128]{2,1,0:T(8,128)(2,1)S(1)}, bf16[32,128,128]{2,1,0:T(8,128)(2,1)S(1)}, u32[]{:S(2)}, u32[]{:S(2)}) collective-permute-start(bf16[32,128,128]{2,1,0:T(8,128)(2,1)S(1)} %bitcast.36), channel_id=1, source_target_pairs={{0,12},{1,49},{4,0},{5,53},{8,4},{9,57},{12,8},{13,61},{16,28},{17... | collective-permute-start | bytes 3145736 | tf_op jit(solution)/shard_map/ppermute | solution.py:313
  26.1 0.0 collective-permute-done.6.refs_4_
  26.1 0.0 copy-start.1
  26.1 2.2 %copy-done.1 = bf16[4,1,32,128,128]{4,3,2,1,0:T(8,128)(2,1)S(1)} copy-done((bf16[4,1,32,128,128]{4,3,2,1,0:T(8,128)(2,1)S(1)}, bf16[4,1,32,128,128]{4,3,2,1,0:T(8,128)(2,1)}, u32[]{:S(2)}) %copy-start.1) | copy-done | bytes 4194328
  28.3 5.1 %stage0.1 = (f32[16,128,128]{2,1,0:T(8,128)S(1)}, bf16[129,128,128]{2,1,0:T(8,128)(2,1)S(1)}) custom-call(s32[24,128]{1,0:T(8,128)S(1)} %get-tuple-element.28.refs_0_, s32[8,128]{1,0:T(8,128)S(1)} %get-tuple-element.29.refs_1_, bf16[128,128,128]{2,1,0:T(8,128)(2,1)S(1)} %bitcast.38, bf16[32,128,128]{2,1,0:T(8,128)(2,1)S(1)} %bitcast.37, ...), custom_call_target="tpu_custom_call" | custom-call | flops 4294967296 | bytes 8388608 | tf_op jit(solution)/shard_map/stage0/pallas_call | solution.py:276
  33.4 5.2 %collective-permute-done.7.refs_3_ = bf16[32,128,128]{2,1,0:T(8,128)(2,1)S(1)} collective-permute-done((bf16[32,128,128]{2,1,0:T(8,128)(2,1)S(1)}, bf16[32,128,128]{2,1,0:T(8,128)(2,1)S(1)}, u32[]{:S(2)}, u32[]{:S(2)}) %collective-permute-start.7) | collective-permute-done | bytes 1048608 | tf_op jit(solution)/shard_map/ppermute | solution.py:312
  38.6 0.0 collective-permute-done.8.refs_5_
  38.6 1.7 %collective-permute-start.11 = (bf16[32,128,128]{2,1,0:T(8,128)(2,1)S(1)}, bf16[32,128,128]{2,1,0:T(8,128)(2,1)S(1)}, u32[]{:S(2)}, u32[]{:S(2)}) collective-permute-start(bf16[32,128,128]{2,1,0:T(8,128)(2,1)S(1)} %collective-permute-done.7.refs_3_), channel_id=1, source_target_pairs={{0,1},{1,0},{2,3},{3,2},{4,5},{5,4},{6,7},{7,6},{8,9},{9,8},{10,11... | collective-permute-start | bytes 3145736 | tf_op jit(solution)/shard_map/ppermute | solution.py:59
  40.3 0.0 collective-permute-start.12
  40.4 1.8 %collective-permute-start.10 = (bf16[16,128,128]{2,1,0:T(8,128)(2,1)S(1)}, bf16[16,128,128]{2,1,0:T(8,128)(2,1)S(1)}, u32[]{:S(2)}, u32[]{:S(2)}) collective-permute-start(bf16[16,128,128]{2,1,0:T(8,128)(2,1)S(1)} %slice.7), channel_id=1, source_target_pairs={{0,12},{1,49},{4,0},{5,53},{8,4},{9,57},{12,8},{13,61},{16,28},{17... | collective-permute-start | bytes 1572872 | tf_op jit(solution)/shard_map/ppermute | solution.py:320
  42.2 0.0 collective-permute-start.9
  42.2 0.4 collective-permute-done.11.refs_4_
  42.6 1.5 %collective-permute-done.12.refs_6_ = bf16[32,128,128]{2,1,0:T(8,128)(2,1)S(1)} collective-permute-done((bf16[32,128,128]{2,1,0:T(8,128)(2,1)S(1)}, bf16[32,128,128]{2,1,0:T(8,128)(2,1)S(1)}, u32[]{:S(2)}, u32[]{:S(2)}) %collective-permute-start.12) | collective-permute-done | bytes 1048608 | tf_op jit(solution)/shard_map/ppermute | solution.py:59
  44.1 8.7 %stage1.1.refs_5_ = f32[16,128,128]{2,1,0:T(8,128)S(1)} custom-call(s32[24,128]{1,0:T(8,128)S(1)} %get-tuple-element.28.refs_0_, s32[8,128]{1,0:T(8,128)S(1)} %get-tuple-element.29.refs_1_, bf16[129,128,128]{2,1,0:T(8,128)(2,1)S(1)} %get-tuple-element.31.refs_2_.refs_3_, ...), custom_call_target="tpu_custom_call", output_to_operand_aliasing={{}: (7, {})} | custom-call | flops 8589934592 | bytes 10485760 | tf_op jit(solution)/shard_map/stage1/pallas_call | solution.py:276
  52.8 0.0 collective-permute-done.10.refs_4_
  52.8 0.0 collective-permute-done.9.refs_3_
  52.8 1.9 %collective-permute-start.13 = (bf16[16,128,128]{2,1,0:T(8,128)(2,1)S(1)}, bf16[16,128,128]{2,1,0:T(8,128)(2,1)S(1)}, u32[]{:S(2)}, u32[]{:S(2)}) collective-permute-start(bf16[16,128,128]{2,1,0:T(8,128)(2,1)S(1)} %collective-permute-done.9.refs_3_), channel_id=1, source_target_pairs={{0,1},{1,0},{2,3},{3,2},{4,5},{5,4},{6,7},{7,6},{8,9},{9,8},{10,11... | collective-permute-start | bytes 1572872 | tf_op jit(solution)/shard_map/ppermute | solution.py:59
  54.7 0.0 collective-permute-start.14
  54.7 3.2 %stage2.1.refs_6_ = f32[16,128,128]{2,1,0:T(8,128)S(1)} custom-call(s32[24,128]{1,0:T(8,128)S(1)} %get-tuple-element.28.refs_0_, s32[8,128]{1,0:T(8,128)S(1)} %get-tuple-element.29.refs_1_, bf16[129,128,128]{2,1,0:T(8,128)(2,1)S(1)} %get-tuple-element.31.refs_2_.refs_3_, ...), custom_call_target="tpu_custom_call", output_to_operand_aliasing={{}: (5, {})} | custom-call | flops 2147483648 | bytes 7340032 | tf_op jit(solution)/shard_map/stage2/pallas_call | solution.py:276
  57.9 0.0 collective-permute-done.13.refs_4_
  57.9 0.0 collective-permute-done.14.refs_5_
  57.9 3.5 %stage3.1 = (f32[2,128,128]{2,1,0:T(8,128)S(1)}, bf16[2,128,128]{2,1,0:T(8,128)(2,1)S(1)}) custom-call(s32[24,128]{1,0:T(8,128)S(1)} %get-tuple-element.28.refs_0_, s32[8,128]{1,0:T(8,128)S(1)} %get-tuple-element.29.refs_1_, s32[1]{0:T(128)S(6)} %shift_right_arithmetic.3.refs_2_, bf16[129,128,128]{2,1,0:T(8,128)(2,1)S(1)} %get-tuple-element.31.refs_2_.refs_3_, ...), custom_call_target="tpu_custom_call" | custom-call | flops 2147483648 | bytes 7340032 | tf_op jit(solution)/shard_map/stage3/pallas_call | solution.py:276
  61.5 2.1 %collective-permute-start.15 = (bf16[2,128,128]{2,1,0:T(8,128)(2,1)S(1)}, bf16[2,128,128]{2,1,0:T(8,128)(2,1)S(1)}, u32[]{:S(2)}, u32[]{:S(2)}) collective-permute-start(bf16[2,128,128]{2,1,0:T(8,128)(2,1)S(1)} %get-tuple-element.42), channel_id=1, source_target_pairs={{0,64},{64,0},{1,65},{65,1},{2,66},{66,2},{3,67},{67,3},{4,68},{68... | collective-permute-start | bytes 196616 | tf_op jit(solution)/shard_map/ppermute | solution.py:327
  63.5 3.2 %collective-permute-done.15 = bf16[2,128,128]{2,1,0:T(8,128)(2,1)S(1)} collective-permute-done((bf16[2,128,128]{2,1,0:T(8,128)(2,1)S(1)}, bf16[2,128,128]{2,1,0:T(8,128)(2,1)S(1)}, u32[]{:S(2)}, u32[]{:S(2)}) %collective-permute-start.15) | collective-permute-done | bytes 65568 | tf_op jit(solution)/shard_map/ppermute | solution.py:327
  66.7 0.6 maximum_convert_fusion
  (3 shorter events, 0.1 us)
Async XLA Ops:
  0.0 7.5 %copy-start = (bf16[8,128,128]{2,1,0:T(8,128)(2,1)S(1)}, bf16[8,128,128]{2,1,0:T(8,128)(2,1)}, u32[]{:S(2)}) copy-start(bf16[8,128,128]{2,1,0:T(8,128)(2,1)} %param.9) | copy-start | bytes 786436
  0.0 7.5 %collective-permute-start = (bf16[256,128]{1,0:T(8,128)(2,1)}, bf16[256,128]{1,0:T(8,128)(2,1)S(1)}, u32[]{:S(2)}, u32[]{:S(2)}) collective-permute-start(bf16[256,128]{1,0:T(8,128)(2,1)} %bitcast.39), channel_id=1, source_target_pairs={{0,2},{1,3},{4,6},{5,7},{8,10},{9,11},{12,14},{13,15},{16,18},{17,... | collective-permute-start | bytes 196616 | tf_op jit(solution)/shard_map/ppermute | solution.py:55
  2.0 5.5 %collective-permute-start.1 = (bf16[256,128]{1,0:T(8,128)(2,1)}, bf16[256,128]{1,0:T(8,128)(2,1)S(1)}, u32[]{:S(2)}, u32[]{:S(2)}) collective-permute-start(bf16[256,128]{1,0:T(8,128)(2,1)} %bitcast.40), channel_id=1, source_target_pairs={{0,66},{1,67},{4,70},{5,71},{8,74},{9,75},{12,78},{13,79},{16,82},... | collective-permute-start | bytes 196616 | tf_op jit(solution)/shard_map/ppermute | solution.py:55
  3.4 4.8 %collective-permute-start.2 = (bf16[256,128]{1,0:T(8,128)(2,1)}, bf16[256,128]{1,0:T(8,128)(2,1)S(1)}, u32[]{:S(2)}, u32[]{:S(2)}) collective-permute-start(bf16[256,128]{1,0:T(8,128)(2,1)} %bitcast.41), channel_id=1, source_target_pairs={{0,64},{1,65},{4,68},{5,69},{8,72},{9,73},{12,76},{13,77},{16,80},... | collective-permute-start | bytes 196616 | tf_op jit(solution)/shard_map/ppermute | solution.py:55
  9.1 8.3 %collective-permute-start.3 = (bf16[1024,128]{1,0:T(8,128)(2,1)S(1)}, bf16[1024,128]{1,0:T(8,128)(2,1)S(1)}, u32[]{:S(2)}, u32[]{:S(2)}) collective-permute-start(bf16[1024,128]{1,0:T(8,128)(2,1)S(1)} %pad_maximum_fusion.1), channel_id=1, source_target_pairs={{0,16},{1,5},{4,20},{5,9},{8,24},{9,13},{12,28},{13,1},{16,32},{17... | collective-permute-start | bytes 786440 | tf_op jit(solution)/shard_map/ppermute | solution.py:55
  10.9 8.3 %collective-permute-start.4 = (bf16[1024,128]{1,0:T(8,128)(2,1)S(1)}, bf16[1024,128]{1,0:T(8,128)(2,1)S(1)}, u32[]{:S(2)}, u32[]{:S(2)}) collective-permute-start(bf16[1024,128]{1,0:T(8,128)(2,1)S(1)} %pad_maximum_fusion.1), channel_id=1, source_target_pairs={{0,48},{1,13},{4,52},{5,1},{8,56},{9,5},{12,60},{13,9},{16,0},{17,... | collective-permute-start | bytes 786440 | tf_op jit(solution)/shard_map/ppermute | solution.py:55
  13.1 8.0 %collective-permute-start.5 = (bf16[1024,128]{1,0:T(8,128)(2,1)S(1)}, bf16[1024,128]{1,0:T(8,128)(2,1)S(1)}, u32[]{:S(2)}, u32[]{:S(2)}) collective-permute-start(bf16[1024,128]{1,0:T(8,128)(2,1)S(1)} %pad_maximum_fusion.1), channel_id=1, source_target_pairs={{0,32},{1,9},{4,36},{5,13},{8,40},{9,1},{12,44},{13,5},{16,48},{17... | collective-permute-start | bytes 786440 | tf_op jit(solution)/shard_map/ppermute | solution.py:55
  21.1 5.0 %collective-permute-start.6 = (bf16[32,128,128]{2,1,0:T(8,128)(2,1)S(1)}, bf16[32,128,128]{2,1,0:T(8,128)(2,1)S(1)}, u32[]{:S(2)}, u32[]{:S(2)}) collective-permute-start(bf16[32,128,128]{2,1,0:T(8,128)(2,1)S(1)} %bitcast.34), channel_id=1, source_target_pairs={{0,1},{1,0},{2,3},{3,2},{4,5},{5,4},{6,7},{7,6},{8,9},{9,8},{10,11... | collective-permute-start | bytes 3145736 | tf_op jit(solution)/shard_map/ppermute | solution.py:59
  23.4 15.2 %collective-permute-start.7 = (bf16[32,128,128]{2,1,0:T(8,128)(2,1)S(1)}, bf16[32,128,128]{2,1,0:T(8,128)(2,1)S(1)}, u32[]{:S(2)}, u32[]{:S(2)}) collective-permute-start(bf16[32,128,128]{2,1,0:T(8,128)(2,1)S(1)} %bitcast.35), channel_id=1, source_target_pairs={{0,4},{1,17},{4,8},{5,21},{8,12},{9,25},{12,0},{13,29},{16,20},{17... | collective-permute-start | bytes 3145736 | tf_op jit(solution)/shard_map/ppermute | solution.py:312
  24.6 14.0 %collective-permute-start.8 = (bf16[32,128,128]{2,1,0:T(8,128)(2,1)S(1)}, bf16[32,128,128]{2,1,0:T(8,128)(2,1)S(1)}, u32[]{:S(2)}, u32[]{:S(2)}) collective-permute-start(bf16[32,128,128]{2,1,0:T(8,128)(2,1)S(1)} %bitcast.36), channel_id=1, source_target_pairs={{0,12},{1,49},{4,0},{5,53},{8,4},{9,57},{12,8},{13,61},{16,28},{17... | collective-permute-start | bytes 3145736 | tf_op jit(solution)/shard_map/ppermute | solution.py:313
  26.1 2.2 %copy-start.1 = (bf16[4,1,32,128,128]{4,3,2,1,0:T(8,128)(2,1)S(1)}, bf16[4,1,32,128,128]{4,3,2,1,0:T(8,128)(2,1)}, u32[]{:S(2)}) copy-start(bf16[4,1,32,128,128]{4,3,2,1,0:T(8,128)(2,1)} %param.15) | copy-start | bytes 12582916
  38.6 4.0 %collective-permute-start.11 = (bf16[32,128,128]{2,1,0:T(8,128)(2,1)S(1)}, bf16[32,128,128]{2,1,0:T(8,128)(2,1)S(1)}, u32[]{:S(2)}, u32[]{:S(2)}) collective-permute-start(bf16[32,128,128]{2,1,0:T(8,128)(2,1)S(1)} %collective-permute-done.7.refs_3_), channel_id=1, source_target_pairs={{0,1},{1,0},{2,3},{3,2},{4,5},{5,4},{6,7},{7,6},{8,9},{9,8},{10,11... | collective-permute-start | bytes 3145736 | tf_op jit(solution)/shard_map/ppermute | solution.py:59
  40.3 3.8 %collective-permute-start.12 = (bf16[32,128,128]{2,1,0:T(8,128)(2,1)S(1)}, bf16[32,128,128]{2,1,0:T(8,128)(2,1)S(1)}, u32[]{:S(2)}, u32[]{:S(2)}) collective-permute-start(bf16[32,128,128]{2,1,0:T(8,128)(2,1)S(1)} %collective-permute-done.8.refs_5_), channel_id=1, source_target_pairs={{0,1},{1,0},{2,3},{3,2},{4,5},{5,4},{6,7},{7,6},{8,9},{9,8},{10,11... | collective-permute-start | bytes 3145736 | tf_op jit(solution)/shard_map/ppermute | solution.py:59
  40.4 12.3 %collective-permute-start.10 = (bf16[16,128,128]{2,1,0:T(8,128)(2,1)S(1)}, bf16[16,128,128]{2,1,0:T(8,128)(2,1)S(1)}, u32[]{:S(2)}, u32[]{:S(2)}) collective-permute-start(bf16[16,128,128]{2,1,0:T(8,128)(2,1)S(1)} %slice.7), channel_id=1, source_target_pairs={{0,12},{1,49},{4,0},{5,53},{8,4},{9,57},{12,8},{13,61},{16,28},{17... | collective-permute-start | bytes 1572872 | tf_op jit(solution)/shard_map/ppermute | solution.py:320
  42.2 10.6 %collective-permute-start.9 = (bf16[16,128,128]{2,1,0:T(8,128)(2,1)S(1)}, bf16[16,128,128]{2,1,0:T(8,128)(2,1)S(1)}, u32[]{:S(2)}, u32[]{:S(2)}) collective-permute-start(bf16[16,128,128]{2,1,0:T(8,128)(2,1)S(1)} %slice.6), channel_id=1, source_target_pairs={{0,4},{1,17},{4,8},{5,21},{8,12},{9,25},{12,0},{13,29},{16,20},{17... | collective-permute-start | bytes 1572872 | tf_op jit(solution)/shard_map/ppermute | solution.py:319
  52.8 5.1 %collective-permute-start.13 = (bf16[16,128,128]{2,1,0:T(8,128)(2,1)S(1)}, bf16[16,128,128]{2,1,0:T(8,128)(2,1)S(1)}, u32[]{:S(2)}, u32[]{:S(2)}) collective-permute-start(bf16[16,128,128]{2,1,0:T(8,128)(2,1)S(1)} %collective-permute-done.9.refs_3_), channel_id=1, source_target_pairs={{0,1},{1,0},{2,3},{3,2},{4,5},{5,4},{6,7},{7,6},{8,9},{9,8},{10,11... | collective-permute-start | bytes 1572872 | tf_op jit(solution)/shard_map/ppermute | solution.py:59
  54.7 3.2 %collective-permute-start.14 = (bf16[16,128,128]{2,1,0:T(8,128)(2,1)S(1)}, bf16[16,128,128]{2,1,0:T(8,128)(2,1)S(1)}, u32[]{:S(2)}, u32[]{:S(2)}) collective-permute-start(bf16[16,128,128]{2,1,0:T(8,128)(2,1)S(1)} %collective-permute-done.10.refs_4_), channel_id=1, source_target_pairs={{0,1},{1,0},{2,3},{3,2},{4,5},{5,4},{6,7},{7,6},{8,9},{9,8},{10,11... | collective-permute-start | bytes 1572872 | tf_op jit(solution)/shard_map/ppermute | solution.py:59
  61.5 5.2 %collective-permute-start.15 = (bf16[2,128,128]{2,1,0:T(8,128)(2,1)S(1)}, bf16[2,128,128]{2,1,0:T(8,128)(2,1)S(1)}, u32[]{:S(2)}, u32[]{:S(2)}) collective-permute-start(bf16[2,128,128]{2,1,0:T(8,128)(2,1)S(1)} %get-tuple-element.42), channel_id=1, source_target_pairs={{0,64},{64,0},{1,65},{65,1},{2,66},{66,2},{3,67},{67,3},{4,68},{68... | collective-permute-start | bytes 196616 | tf_op jit(solution)/shard_map/ppermute | solution.py:327

commit v2 on v1

--- a/solution.py
+++ b/solution.py
@@ -16,13 +16,14 @@
 BLOCKS = 64
 ZERO = RELS * POOL
 UNIT = 4
-WIDE = (16, 16, 8, 8)
-SIZES = (2, 4, 1, 1)
+WIDE = (16, 16, 8, 8, 8)
+SIZES = (64, 128, 16, 32, 16)
 STAGES = len(SIZES)
+FLOPS = (4 << 30, 8 << 30, 1 << 30, 2 << 30, 1 << 30)
 
 
 def most_chunks(st):
-    most = (RELS * 64 * SIZES[st] + (UNIT - 1) * RELS * TPB) // UNIT
+    most = (RELS * 2 * SIZES[st] + (UNIT - 1) * RELS * TPB) // UNIT
     return -(-most // WIDE[st]) * WIDE[st]
 
 
@@ -72,7 +73,10 @@
     return jnp.dot(left.astype(jnp.bfloat16), right.astype(jnp.bfloat16), preferred_element_type=jnp.float32)
 
 
-def sort_kernel(here_ref, packed_ref, pay_ref, tab_ref):
+def sort_kernel(here_ref, packed_ref, pool_hbm, pay_ref, tab_ref, pool_ref, sem):
+    fetch = pltpu.make_async_copy(pool_hbm, pool_ref.at[pl.ds(0, ZERO)], sem)
+    fetch.start()
+    pool_ref[ZERO] = jnp.zeros((TILE, TILE), pool_ref.dtype)
     shape = (SLOTS, BLOCKS)
     my_x, my_y, my_z, my_core = (here_ref[i] for i in range(4))
     block, slot = iota(shape, 1), iota(shape, 0)
@@ -85,15 +89,16 @@
     dy, dz = place(y - my_y), place(z - my_z)
     second, third = jnp.where(core == 0, dy, dz), jnp.where(core == 0, dz, dy)
     other = jnp.where(core == my_core, 0, 1)
-    stage = jnp.where(third == 0, 0, jnp.where(third == 3, 2 + other, 1))
-    buf = jnp.where(third == 0, other, jnp.where(third == 3, 0, (third - 1) * 2 + other))
+    far_stage = jnp.where(second < 2, 2, 3) + other
+    stage = jnp.where(third == 3, far_stage, jnp.where(third == 0, 0, 1))
+    buf = jnp.where(third == 3, jnp.where(far_stage == 4, -16, 0), (jnp.where(third == 2, 2, 0) + other) * 32)
     lists, at, ids = [], [], []
     for r in range(RELS):
         packed = packed_ref[r]
         cols = (packed >> 2) & 3
         ids.append((packed >> 4) & 31)
         dx = place((cols >> 1) * 2 + low - my_x)
-        at.append(buf * 32 + (second * 4 + dx) * 2 + (cols & 1))
+        at.append(buf + (second * 4 + dx) * 2 + (cols & 1))
         live = slot < (packed >> 9)
         lists.append(jnp.where(live, stage * TPB + (packed & 3), STAGES * TPB))
     members = [
@@ -115,7 +120,9 @@
     earlier = ((row >> 7) == (col >> 7)) & ((col >> 3) < (row >> 3)) & ((col & 7) == 0)
     begin = exact_dot(jnp.where(earlier, 1.0, 0.0), chunks)
     step = iota(begin.shape, 0) >> 7
-    base = jnp.where(step == 0, STARTS[0], jnp.where(step == 1, STARTS[1], jnp.where(step == 2, STARTS[2], STARTS[3])))
+    base = jnp.zeros_like(step)
+    for st in range(1, STAGES):
+        base = jnp.where(step == st, STARTS[st], base)
     begin = begin + base.astype(jnp.float32)
     end = (begin + chunks).astype(jnp.int32)
     pos = member * ((begin * UNIT + above)[:, :BLOCKS] + ahead)
@@ -159,21 +166,24 @@
         total = end[last : last + SLOTS] - STARTS[st]
         table = jnp.where(index == (TAB_ROWS - 1) * TILE + st, total, table)
     tab_ref[...] = table
-
-
-def sort_slots(here, packed):
+    fetch.wait()
+
+
+def sort_slots(here, packed, pool):
     return pl.pallas_call(
         sort_kernel,
         out_shape=[
             jax.ShapeDtypeStruct((PAY_ROWS, TILE), jnp.int32),
             jax.ShapeDtypeStruct((TAB_ROWS, TILE), jnp.int32),
+            jax.ShapeDtypeStruct((ZERO + 1, TILE, TILE), pool.dtype),
         ],
-        in_specs=[SMEM, VMEM],
-        out_specs=[VMEM] * 2,
+        in_specs=[SMEM, VMEM, ANY],
+        out_specs=[VMEM] * 3,
+        scratch_shapes=[pltpu.SemaphoreType.DMA],
         compiler_params=pltpu.CompilerParams(vmem_limit_bytes=24 << 20),
         cost_estimate=pl.CostEstimate(flops=0, bytes_accessed=8 << 20, transcendentals=0),
         name="sort_slots",
-    )(here, packed)
+    )(here, packed, pool)
 
 
 def stage_kernel(st, count, first, last, *refs):
@@ -187,11 +197,8 @@
     del refs[:count]
     copies = []
     if first:
-        total, full, *refs = refs
-        copies.append((pool, full.at[pl.ds(0, ZERO)]))
-        full[ZERO] = jnp.zeros((TILE, TILE), full.dtype)
+        total = refs.pop(0)
         total[...] = jnp.zeros_like(total)
-        pool = full
     else:
         before = refs.pop(0)
         if last:
@@ -201,9 +208,10 @@
             total = refs.pop(0)
     if count > 1:
         rows, sems = refs
-        for i, buf in enumerate(bufs):
-            size = buf.shape[0]
-            copies.append((buf, rows.at[pl.ds(i * size, size)]))
+        at = 0
+        for buf in bufs:
+            copies.append((buf, rows.at[pl.ds(at, buf.shape[0])]))
+            at += buf.shape[0]
         copies = [pltpu.make_async_copy(*copy, sems.at[i]) for i, copy in enumerate(copies)]
         for copy in copies:
             copy.start()
@@ -249,14 +257,11 @@
         args.append(tail[0])
         specs.append(SMEM)
     args += [pool, *bufs]
-    specs += [ANY if first else VMEM] + [ANY if len(bufs) > 1 else VMEM] * len(bufs)
+    specs += [VMEM] + [ANY if len(bufs) > 1 else VMEM] * len(bufs)
     wide = (RELS * TPB, TILE, TILE)
     scratch, aliases = [], {}
     if first:
-        out = [
-            jax.ShapeDtypeStruct(wide, jnp.float32),
-            jax.ShapeDtypeStruct((ZERO + 1, TILE, TILE), pool.dtype),
-        ]
+        out = [jax.ShapeDtypeStruct(wide, jnp.float32)]
     else:
         args.append(before)
         specs.append(VMEM)
@@ -270,9 +275,8 @@
             out = [jax.ShapeDtypeStruct(wide, jnp.float32)]
             aliases = {len(args) - 1: 0}
     if len(bufs) > 1:
-        scratch.append(pltpu.VMEM((32 * SIZES[st], TILE, TILE), jnp.bfloat16))
-        scratch.append(pltpu.SemaphoreType.DMA((len(bufs) + 1,)))
-    slots = 16 * 8 * SIZES[st]
+        scratch.append(pltpu.VMEM((SIZES[st], TILE, TILE), jnp.bfloat16))
+        scratch.append(pltpu.SemaphoreType.DMA((len(bufs),)))
     return pl.pallas_call(
         functools.partial(stage_kernel, st, len(bufs), first, last),
         out_shape=out,
@@ -281,9 +285,7 @@
         scratch_shapes=scratch,
         input_output_aliases=aliases,
         compiler_params=pltpu.CompilerParams(vmem_limit_bytes=24 << 20),
-        cost_estimate=pl.CostEstimate(
-            flops=slots * 2 * TILE**3 * 4, bytes_accessed=(6 + SIZES[st]) << 20, transcendentals=0
-        ),
+        cost_estimate=pl.CostEstimate(flops=FLOPS[st], bytes_accessed=8 << 20, transcendentals=0),
         name=f"stage{st}",
     )(*args)
 
@@ -306,24 +308,26 @@
     packed = packed | (tile_count[:, 0][:, None, :] << 9)
     line, packed, selfterm, now = lax.optimization_barrier((line, packed, selfterm, now))
     plane = jnp.concatenate(ring(line, 1, 2), 0)
-    lists = sort_slots(here, packed)
-    plane, lists = lax.optimization_barrier((plane, lists))
+    pool = tile_pool.reshape(RELS * POOL, TILE, TILE)
+    pay, tab, pool = sort_slots(here, packed, pool)
+    lists = (pay, tab)
+    plane, lists, pool = lax.optimization_barrier((plane, lists, pool))
     plane = plane.reshape(-1, TILE, width)
     left = lax.ppermute(plane, FLAT, shift(2, 1, 1))
     right = lax.ppermute(plane, FLAT, shift(2, 1, -1))
-    pool = tile_pool.reshape(RELS * POOL, TILE, TILE)
-    total, pool = run_stage(0, lists, pool, [plane, sibling(plane)])
+    total = run_stage(0, lists, pool, [plane, sibling(plane)])[0]
     left, right, total = lax.optimization_barrier((left, right, total))
     half = plane.shape[0] // 2
-    far = [
-        lax.ppermute(left[:half], FLAT, shift(2, 1, 1)),
-        lax.ppermute(right[half:], FLAT, shift(2, 1, -1)),
-    ]
+    first = lax.ppermute(left[:half], FLAT, shift(2, 1, 1))
+    second = lax.ppermute(right[half:], FLAT, shift(2, 1, -1))
     total = run_stage(1, lists, pool, [left, sibling(left), right, sibling(right)], total)[0]
-    *far, total = lax.optimization_barrier((*far, total))
-    beyond = [sibling(piece) for piece in far]
-    total = run_stage(2, lists, pool, far, total)[0]
-    kept, sent = run_stage(3, lists, pool, beyond, total, (here[:1] >> 1, now, selfterm))
+    first, total = lax.optimization_barrier((first, total))
+    other = sibling(first)
+    total = run_stage(2, lists, pool, [first], total)[0]
+    second, total = lax.optimization_barrier((second, total))
+    last = sibling(second)
+    total = run_stage(3, lists, pool, [other, second], total)[0]
+    kept, sent = run_stage(4, lists, pool, [last], total, (here[:1] >> 1, now, selfterm))
     got = lax.ppermute(sent, "chan", [(0, 1), (1, 0)])
     updated = jax.nn.relu(kept + got.astype(jnp.float32)).astype(jnp.bfloat16)
     return updated.reshape(1, 1, half_rows, width)

time: 67.5 us -> 66.5 us (0.985)
  starting transfers between devices: 22.8 us -> 21.6 us
  waiting for transfers between devices: 14.6 us -> 13.7 us
    ppermute x6, waiting for transfers between devices: 4.35 us -> 1.48 us  [ring(): lax.ppermute(rows, FLAT, shift(axis_first, axis_second, by))]
    ppermute x1, waiting for transfers between devices: 5.19 us -> 7.87 us  [shards(): left = lax.ppermute(plane, FLAT, shift(2, 1, 1))]
    ppermute x5, starting transfers between devices: 5.96 us -> 4.58 us  [sibling(): return lax.ppermute(rows, 'core', [(0, 1), (1, 0)])]
    ppermute x5, waiting for transfers between devices: 1.9 us -> 0.95 us  [sibling(): return lax.ppermute(rows, 'core', [(0, 1), (1, 0)])]
    ppermute x2, starting transfers between devices: 1.79 us -> 2.75 us  [the longest x1 1.54 us: shards(): second = lax.ppermute(right[half:], FLAT, shift(2, 1, -1))]
    ppermute x1, starting transfers between devices: 2.06 us -> 1.29 us  [shards(): got = lax.ppermute(sent, 'chan', [(0, 1), (1, 0)])]
    pallas_call x4 -> x5, Pallas kernels: 20.4 us -> 20.2 us  [run_stage(): pl.pallas_call(functools.partial(stage_kernel, st, len(bufs), first, last...]
  transfers between devices with their start and end apart: 16 -> 16, of which waited for: 7 -> 5; matrix products, arithmetic and copies ran while one was open for 4% -> 4% of each run, Pallas kernels for 29% -> 33%
where the time goes in v2:
time: 66.5 us; the launch traced here: 65.7 us
  Pallas kernels  23.9 us (36%)
  starting transfers between devices  21.6 us (32%)
  waiting for transfers between devices  13.7 us (21%)
  other arithmetic  3.1 us (5%)
  local copies, waits for them, and re-layouts  2.29 us (3%)
  matrix products  0.98 us (1%)
    pallas_call x5, Pallas kernels, run_stage(): pl.pallas_call(functools.partial(stage_kernel, st, len(bufs), first, last...  20.2 us
    ppermute x6, starting transfers between devices, ring(): lax.ppermute(rows, FLAT, shift(axis_first, axis_second, by))  10.3 us
    ppermute x1, waiting for transfers between devices, shards(): left = lax.ppermute(plane, FLAT, shift(2, 1, 1))  7.87 us
    ppermute x5, starting transfers between devices, sibling(): return lax.ppermute(rows, 'core', [(0, 1), (1, 0)])  4.58 us
    pallas_call x1, Pallas kernels, sort_slots(): pl.pallas_call(sort_kernel, out_shape=[jax.ShapeDtypeStruct((PAY_ROWS, TI...  3.65 us
    ppermute x1, waiting for transfers between devices, shards(): got = lax.ppermute(sent, 'chan', [(0, 1), (1, 0)])  3.41 us
    unnamed x4, local copies, waits for them, and re-layouts  2.19 us
    ppermute x1, starting transfers between devices, shards(): right = lax.ppermute(plane, FLAT, shift(2, 1, -1))  1.54 us
  transfers between devices with their start and end apart: 16, of which 5 were waited for; matrix products, arithmetic and copies ran while one was open for 4% of the time, Pallas kernels for 33%

profile of v2, /device:TPU:1, one launch (start us, length us, event | category | flops | bytes accessed | tf_op | source)
XLA Modules:
  0.0 65.7 jit_solution(940995438499364071)
XLA Ops:
  0.0 0.0 copy-start
  0.0 2.0 %collective-permute-start = (bf16[256,128]{1,0:T(8,128)(2,1)}, bf16[256,128]{1,0:T(8,128)(2,1)S(1)}, u32[]{:S(2)}, u32[]{:S(2)}) collective-permute-start(bf16[256,128]{1,0:T(8,128)(2,1)} %bitcast.39), channel_id=1, source_target_pairs={{0,2},{1,3},{4,6},{5,7},{8,10},{9,11},{12,14},{13,15},{16,18},{17,... | collective-permute-start | bytes 196616 | tf_op jit(solution)/shard_map/ppermute | solution.py:56
  2.0 1.3 %collective-permute-start.1 = (bf16[256,128]{1,0:T(8,128)(2,1)}, bf16[256,128]{1,0:T(8,128)(2,1)S(1)}, u32[]{:S(2)}, u32[]{:S(2)}) collective-permute-start(bf16[256,128]{1,0:T(8,128)(2,1)} %bitcast.40), channel_id=1, source_target_pairs={{0,66},{1,67},{4,70},{5,71},{8,74},{9,75},{12,78},{13,79},{16,82},... | collective-permute-start | bytes 196616 | tf_op jit(solution)/shard_map/ppermute | solution.py:56
  3.4 1.7 %collective-permute-start.2 = (bf16[256,128]{1,0:T(8,128)(2,1)}, bf16[256,128]{1,0:T(8,128)(2,1)S(1)}, u32[]{:S(2)}, u32[]{:S(2)}) collective-permute-start(bf16[256,128]{1,0:T(8,128)(2,1)} %bitcast.41), channel_id=1, source_target_pairs={{0,64},{1,65},{4,68},{5,69},{8,72},{9,73},{12,76},{13,77},{16,80},... | collective-permute-start | bytes 196616 | tf_op jit(solution)/shard_map/ppermute | solution.py:56
  5.0 0.7 %broadcast_shift-left_fusion = s32[4,1,64]{2,1,0:T(1,128)S(1)} fusion(s32[4,1,64]{2,1,0:T(1,128)} %param.14), kind=kLoop, calls=%fused_computation.11 | loop fusion | flops 256 | bytes 2048 | tf_op jit(solution)/shard_map/shift_left | solution.py:308
  5.7 1.0 %fusion.refs_7_ = f32[2,128,128]{2,1,0:T(8,128)S(1)} fusion(bf16[2,128,128]{2,1,0:T(8,128)(2,1)} %bitcast.42, bf16[128,128]{1,0:T(8,128)(2,1)} %param.10), kind=kOutput, calls=%fused_computation.3 | convolution fusion | flops 8388608 | bytes 229376 | tf_op jit(solution)/shard_map/dot_general | solution.py:305
  6.7 0.8 %fusion.2.packed_ref = s32[4,8,64]{2,1,0:T(8,128)S(1)} fusion(s32[4,1,64,8]{2,3,1,0:T(8,128)} %param.13, s32[4,1,64,8]{2,3,1,0:T(8,128)} %param.12, s32[4,1,64,8]{2,3,1,0:T(8,128)} %param.11, s32[4,64]{1,0:T(4,128)S(1)} %bitcast.44), kind=kLoop, calls=%fused_computation.6 | loop fusion | flops 10240 | bytes 33792 | tf_op jit(solution)/shard_map/or | solution.py:308
  7.5 0.0 copy-done
  7.5 0.0 collective-permute-done
  7.5 0.0 collective-permute-done.1
  7.5 0.7 %collective-permute-done.2 = bf16[256,128]{1,0:T(8,128)(2,1)S(1)} collective-permute-done((bf16[256,128]{1,0:T(8,128)(2,1)}, bf16[256,128]{1,0:T(8,128)(2,1)S(1)}, u32[]{:S(2)}, u32[]{:S(2)}) %collective-permute-start.2) | collective-permute-done | bytes 65568 | tf_op jit(solution)/shard_map/ppermute | solution.py:56
  8.2 0.9 %pad_maximum_fusion.1 = bf16[1024,128]{1,0:T(8,128)(2,1)S(1)} fusion(bf16[256,128]{1,0:T(8,128)(2,1)S(1)} %collective-permute-done.2, bf16[256,128]{1,0:T(8,128)(2,1)S(1)} %collective-permute-done.1, bf16[256,128]{1,0:T(8,128)(2,1)S(1)} %collective-permute-done, bf16[256,128]{1,0:T(8,128)(2,1)} %bitcast.43), kind=kLoop, calls=%fused_computation.1 | loop fusion | flops 1048576 | bytes 524288 | tf_op jit(solution)/shard_map/concatenate | solution.py:304
  9.1 1.8 %collective-permute-start.3 = (bf16[1024,128]{1,0:T(8,128)(2,1)S(1)}, bf16[1024,128]{1,0:T(8,128)(2,1)S(1)}, u32[]{:S(2)}, u32[]{:S(2)}) collective-permute-start(bf16[1024,128]{1,0:T(8,128)(2,1)S(1)} %pad_maximum_fusion.1), channel_id=1, source_target_pairs={{0,16},{1,5},{4,20},{5,9},{8,24},{9,13},{12,28},{13,1},{16,32},{17... | collective-permute-start | bytes 786440 | tf_op jit(solution)/shard_map/ppermute | solution.py:56
  10.9 2.2 %collective-permute-start.4 = (bf16[1024,128]{1,0:T(8,128)(2,1)S(1)}, bf16[1024,128]{1,0:T(8,128)(2,1)S(1)}, u32[]{:S(2)}, u32[]{:S(2)}) collective-permute-start(bf16[1024,128]{1,0:T(8,128)(2,1)S(1)} %pad_maximum_fusion.1), channel_id=1, source_target_pairs={{0,48},{1,13},{4,52},{5,1},{8,56},{9,5},{12,60},{13,9},{16,0},{17,... | collective-permute-start | bytes 786440 | tf_op jit(solution)/shard_map/ppermute | solution.py:56
  13.1 1.2 %collective-permute-start.5 = (bf16[1024,128]{1,0:T(8,128)(2,1)S(1)}, bf16[1024,128]{1,0:T(8,128)(2,1)S(1)}, u32[]{:S(2)}, u32[]{:S(2)}) collective-permute-start(bf16[1024,128]{1,0:T(8,128)(2,1)S(1)} %pad_maximum_fusion.1), channel_id=1, source_target_pairs={{0,32},{1,9},{4,36},{5,13},{8,40},{9,1},{12,44},{13,5},{16,48},{17... | collective-permute-start | bytes 786440 | tf_op jit(solution)/shard_map/ppermute | solution.py:56
  14.3 0.1 pad_add_fusion.here_ref
  14.4 0.0 copy-start.1
  14.4 2.2 %copy-done.1 = bf16[4,1,32,128,128]{4,3,2,1,0:T(8,128)(2,1)S(1)} copy-done((bf16[4,1,32,128,128]{4,3,2,1,0:T(8,128)(2,1)S(1)}, bf16[4,1,32,128,128]{4,3,2,1,0:T(8,128)(2,1)}, u32[]{:S(2)}) %copy-start.1) | copy-done | bytes 4194328
  16.6 3.6 %sort_slots.1 = (s32[24,128]{1,0:T(8,128)S(1)}, s32[8,128]{1,0:T(8,128)S(1)}, bf16[129,128,128]{2,1,0:T(8,128)(2,1)S(1)}) custom-call(s32[4]{0:T(128)S(1)} %pad_add_fusion.here_ref, s32[4,8,64]{2,1,0:T(8,128)S(1)} %fusion.2.packed_ref, bf16[128,128,128]{2,1,0:T(8,128)(2,1)S(1)} %bitcast.34), custom_call_target="tpu_custom_call" | custom-call | bytes 8388608 | tf_op jit(solution)/shard_map/sort_slots/pallas_call | solution.py:173
  20.3 0.0 collective-permute-done.3
  20.3 0.0 collective-permute-done.4
  20.3 0.8 %collective-permute-done.5 = bf16[1024,128]{1,0:T(8,128)(2,1)S(1)} collective-permute-done((bf16[1024,128]{1,0:T(8,128)(2,1)S(1)}, bf16[1024,128]{1,0:T(8,128)(2,1)S(1)}, u32[]{:S(2)}, u32[]{:S(2)}) %collective-permute-start.5) | collective-permute-done | bytes 262176 | tf_op jit(solution)/shard_map/ppermute | solution.py:56
  21.1 0.1 pad_maximum_fusion
  21.1 2.3 %collective-permute-start.8 = (bf16[32,128,128]{2,1,0:T(8,128)(2,1)S(1)}, bf16[32,128,128]{2,1,0:T(8,128)(2,1)S(1)}, u32[]{:S(2)}, u32[]{:S(2)}) collective-permute-start(bf16[32,128,128]{2,1,0:T(8,128)(2,1)S(1)} %bitcast.35), channel_id=1, source_target_pairs={{0,1},{1,0},{2,3},{3,2},{4,5},{5,4},{6,7},{7,6},{8,9},{9,8},{10,11... | collective-permute-start | bytes 3145736 | tf_op jit(solution)/shard_map/ppermute | solution.py:60
  23.4 1.1 %collective-permute-start.6 = (bf16[32,128,128]{2,1,0:T(8,128)(2,1)S(1)}, bf16[32,128,128]{2,1,0:T(8,128)(2,1)S(1)}, u32[]{:S(2)}, u32[]{:S(2)}) collective-permute-start(bf16[32,128,128]{2,1,0:T(8,128)(2,1)S(1)} %bitcast.36), channel_id=1, source_target_pairs={{0,4},{1,17},{4,8},{5,21},{8,12},{9,25},{12,0},{13,29},{16,20},{17... | collective-permute-start | bytes 3145736 | tf_op jit(solution)/shard_map/ppermute | solution.py:316
  24.6 1.5 %collective-permute-start.7 = (bf16[32,128,128]{2,1,0:T(8,128)(2,1)S(1)}, bf16[32,128,128]{2,1,0:T(8,128)(2,1)S(1)}, u32[]{:S(2)}, u32[]{:S(2)}) collective-permute-start(bf16[32,128,128]{2,1,0:T(8,128)(2,1)S(1)} %bitcast.37), channel_id=1, source_target_pairs={{0,12},{1,49},{4,0},{5,53},{8,4},{9,57},{12,8},{13,61},{16,28},{17... | collective-permute-start | bytes 3145736 | tf_op jit(solution)/shard_map/ppermute | solution.py:317
  26.1 0.0 collective-permute-done.8.refs_4_
  26.1 4.6 %stage0.1.refs_7_ = f32[16,128,128]{2,1,0:T(8,128)S(1)} custom-call(s32[24,128]{1,0:T(8,128)S(1)} %get-tuple-element.30.refs_0_, s32[8,128]{1,0:T(8,128)S(1)} %get-tuple-element.31.refs_1_, bf16[129,128,128]{2,1,0:T(8,128)(2,1)S(1)} %get-tuple-element.32.refs_2_.refs_3_, bf16[32,128,128]{2,1,0:T(8,128)(2,1)S(1)} %bitcast.38, ...), custom_call_target="tpu_custom_call" | custom-call | flops 4294967296 | bytes 8388608 | tf_op jit(solution)/shard_map/stage0/pallas_call | solution.py:280
  30.7 7.9 %collective-permute-done.6.refs_3_ = bf16[32,128,128]{2,1,0:T(8,128)(2,1)S(1)} collective-permute-done((bf16[32,128,128]{2,1,0:T(8,128)(2,1)S(1)}, bf16[32,128,128]{2,1,0:T(8,128)(2,1)S(1)}, u32[]{:S(2)}, u32[]{:S(2)}) %collective-permute-start.6) | collective-permute-done | bytes 1048608 | tf_op jit(solution)/shard_map/ppermute | solution.py:316
  38.6 0.0 collective-permute-done.7.refs_5_
  38.6 1.7 %collective-permute-start.11 = (bf16[32,128,128]{2,1,0:T(8,128)(2,1)S(1)}, bf16[32,128,128]{2,1,0:T(8,128)(2,1)S(1)}, u32[]{:S(2)}, u32[]{:S(2)}) collective-permute-start(bf16[32,128,128]{2,1,0:T(8,128)(2,1)S(1)} %collective-permute-done.6.refs_3_), channel_id=1, source_target_pairs={{0,1},{1,0},{2,3},{3,2},{4,5},{5,4},{6,7},{7,6},{8,9},{9,8},{10,11... | collective-permute-start | bytes 3145736 | tf_op jit(solution)/shard_map/ppermute | solution.py:60
  40.3 0.0 collective-permute-start.12
  40.4 1.2 %collective-permute-start.10 = (bf16[16,128,128]{2,1,0:T(8,128)(2,1)S(1)}, bf16[16,128,128]{2,1,0:T(8,128)(2,1)S(1)}, u32[]{:S(2)}, u32[]{:S(2)}) collective-permute-start(bf16[16,128,128]{2,1,0:T(8,128)(2,1)S(1)} %slice.7), channel_id=1, source_target_pairs={{0,4},{1,17},{4,8},{5,21},{8,12},{9,25},{12,0},{13,29},{16,20},{17... | collective-permute-start | bytes 1572872 | tf_op jit(solution)/shard_map/ppermute | solution.py:321
  41.7 1.5 %collective-permute-start.9 = (bf16[16,128,128]{2,1,0:T(8,128)(2,1)S(1)}, bf16[16,128,128]{2,1,0:T(8,128)(2,1)S(1)}, u32[]{:S(2)}, u32[]{:S(2)}) collective-permute-start(bf16[16,128,128]{2,1,0:T(8,128)(2,1)S(1)} %slice.6), channel_id=1, source_target_pairs={{0,12},{1,49},{4,0},{5,53},{8,4},{9,57},{12,8},{13,61},{16,28},{17... | collective-permute-start | bytes 1572872 | tf_op jit(solution)/shard_map/ppermute | solution.py:322
  43.2 0.0 collective-permute-done.11.refs_4_
  43.2 0.9 %collective-permute-done.12.refs_6_ = bf16[32,128,128]{2,1,0:T(8,128)(2,1)S(1)} collective-permute-done((bf16[32,128,128]{2,1,0:T(8,128)(2,1)S(1)}, bf16[32,128,128]{2,1,0:T(8,128)(2,1)S(1)}, u32[]{:S(2)}, u32[]{:S(2)}) %collective-permute-start.12) | collective-permute-done | bytes 1048608 | tf_op jit(solution)/shard_map/ppermute | solution.py:60
  44.1 7.5 %stage1.1.refs_4_ = f32[16,128,128]{2,1,0:T(8,128)S(1)} custom-call(s32[24,128]{1,0:T(8,128)S(1)} %get-tuple-element.30.refs_0_, s32[8,128]{1,0:T(8,128)S(1)} %get-tuple-element.31.refs_1_, bf16[129,128,128]{2,1,0:T(8,128)(2,1)S(1)} %get-tuple-element.32.refs_2_.refs_3_, ...), custom_call_target="tpu_custom_call", output_to_operand_aliasing={{}: (7, {})} | custom-call | flops 8589934592 | bytes 8388608 | tf_op jit(solution)/shard_map/stage1/pallas_call | solution.py:280
  51.7 0.0 collective-permute-done.10.refs_3_
  51.7 0.5 collective-permute-start.14
  52.1 2.5 %stage2.1.refs_5_ = f32[16,128,128]{2,1,0:T(8,128)S(1)} custom-call(s32[24,128]{1,0:T(8,128)S(1)} %get-tuple-element.30.refs_0_, s32[8,128]{1,0:T(8,128)S(1)} %get-tuple-element.31.refs_1_, bf16[129,128,128]{2,1,0:T(8,128)(2,1)S(1)} %get-tuple-element.32.refs_2_.refs_3_, ...), custom_call_target="tpu_custom_call", output_to_operand_aliasing={{}: (4, {})} | custom-call | flops 1073741824 | bytes 8388608 | tf_op jit(solution)/shard_map/stage2/pallas_call | solution.py:280
  54.7 0.0 collective-permute-done.9.refs_4_
  54.7 0.1 collective-permute-start.13
  54.8 0.0 collective-permute-done.14.refs_3_
  54.8 3.1 %stage3.1.refs_5_ = f32[16,128,128]{2,1,0:T(8,128)S(1)} custom-call(s32[24,128]{1,0:T(8,128)S(1)} %get-tuple-element.30.refs_0_, s32[8,128]{1,0:T(8,128)S(1)} %get-tuple-element.31.refs_1_, bf16[129,128,128]{2,1,0:T(8,128)(2,1)S(1)} %get-tuple-element.32.refs_2_.refs_3_, ...), custom_call_target="tpu_custom_call", output_to_operand_aliasing={{}: (5, {})} | custom-call | flops 2147483648 | bytes 8388608 | tf_op jit(solution)/shard_map/stage3/pallas_call | solution.py:280
  57.9 0.0 collective-permute-done.13.refs_4_
  57.9 2.5 %stage4.1 = (f32[2,128,128]{2,1,0:T(8,128)S(1)}, bf16[2,128,128]{2,1,0:T(8,128)(2,1)S(1)}) custom-call(s32[24,128]{1,0:T(8,128)S(1)} %get-tuple-element.30.refs_0_, s32[8,128]{1,0:T(8,128)S(1)} %get-tuple-element.31.refs_1_, s32[1]{0:T(128)S(6)} %shift_right_arithmetic.3.refs_2_, bf16[129,128,128]{2,1,0:T(8,128)(2,1)S(1)} %get-tuple-element.32.refs_2_.refs_3_, ...), custom_call_target="tpu_custom_call" | custom-call | flops 1073741824 | bytes 8388608 | tf_op jit(solution)/shard_map/stage4/pallas_call | solution.py:280
  60.4 1.3 %collective-permute-start.15 = (bf16[2,128,128]{2,1,0:T(8,128)(2,1)S(1)}, bf16[2,128,128]{2,1,0:T(8,128)(2,1)S(1)}, u32[]{:S(2)}, u32[]{:S(2)}) collective-permute-start(bf16[2,128,128]{2,1,0:T(8,128)(2,1)S(1)} %get-tuple-element.44), channel_id=1, source_target_pairs={{0,64},{64,0},{1,65},{65,1},{2,66},{66,2},{3,67},{67,3},{4,68},{68... | collective-permute-start | bytes 196616 | tf_op jit(solution)/shard_map/ppermute | solution.py:331
  61.7 3.4 %collective-permute-done.15 = bf16[2,128,128]{2,1,0:T(8,128)(2,1)S(1)} collective-permute-done((bf16[2,128,128]{2,1,0:T(8,128)(2,1)S(1)}, bf16[2,128,128]{2,1,0:T(8,128)(2,1)S(1)}, u32[]{:S(2)}, u32[]{:S(2)}) %collective-permute-start.15) | collective-permute-done | bytes 65568 | tf_op jit(solution)/shard_map/ppermute | solution.py:331
  65.1 0.6 maximum_convert_fusion
  (3 shorter events, 0.1 us)
Async XLA Ops:
  0.0 7.5 %copy-start = (bf16[8,128,128]{2,1,0:T(8,128)(2,1)S(1)}, bf16[8,128,128]{2,1,0:T(8,128)(2,1)}, u32[]{:S(2)}) copy-start(bf16[8,128,128]{2,1,0:T(8,128)(2,1)} %param.9) | copy-start | bytes 786436
  0.0 7.5 %collective-permute-start = (bf16[256,128]{1,0:T(8,128)(2,1)}, bf16[256,128]{1,0:T(8,128)(2,1)S(1)}, u32[]{:S(2)}, u32[]{:S(2)}) collective-permute-start(bf16[256,128]{1,0:T(8,128)(2,1)} %bitcast.39), channel_id=1, source_target_pairs={{0,2},{1,3},{4,6},{5,7},{8,10},{9,11},{12,14},{13,15},{16,18},{17,... | collective-permute-start | bytes 196616 | tf_op jit(solution)/shard_map/ppermute | solution.py:56
  2.0 5.5 %collective-permute-start.1 = (bf16[256,128]{1,0:T(8,128)(2,1)}, bf16[256,128]{1,0:T(8,128)(2,1)S(1)}, u32[]{:S(2)}, u32[]{:S(2)}) collective-permute-start(bf16[256,128]{1,0:T(8,128)(2,1)} %bitcast.40), channel_id=1, source_target_pairs={{0,66},{1,67},{4,70},{5,71},{8,74},{9,75},{12,78},{13,79},{16,82},... | collective-permute-start | bytes 196616 | tf_op jit(solution)/shard_map/ppermute | solution.py:56
  3.4 4.8 %collective-permute-start.2 = (bf16[256,128]{1,0:T(8,128)(2,1)}, bf16[256,128]{1,0:T(8,128)(2,1)S(1)}, u32[]{:S(2)}, u32[]{:S(2)}) collective-permute-start(bf16[256,128]{1,0:T(8,128)(2,1)} %bitcast.41), channel_id=1, source_target_pairs={{0,64},{1,65},{4,68},{5,69},{8,72},{9,73},{12,76},{13,77},{16,80},... | collective-permute-start | bytes 196616 | tf_op jit(solution)/shard_map/ppermute | solution.py:56
  9.1 11.2 %collective-permute-start.3 = (bf16[1024,128]{1,0:T(8,128)(2,1)S(1)}, bf16[1024,128]{1,0:T(8,128)(2,1)S(1)}, u32[]{:S(2)}, u32[]{:S(2)}) collective-permute-start(bf16[1024,128]{1,0:T(8,128)(2,1)S(1)} %pad_maximum_fusion.1), channel_id=1, source_target_pairs={{0,16},{1,5},{4,20},{5,9},{8,24},{9,13},{12,28},{13,1},{16,32},{17... | collective-permute-start | bytes 786440 | tf_op jit(solution)/shard_map/ppermute | solution.py:56
  10.9 9.4 %collective-permute-start.4 = (bf16[1024,128]{1,0:T(8,128)(2,1)S(1)}, bf16[1024,128]{1,0:T(8,128)(2,1)S(1)}, u32[]{:S(2)}, u32[]{:S(2)}) collective-permute-start(bf16[1024,128]{1,0:T(8,128)(2,1)S(1)} %pad_maximum_fusion.1), channel_id=1, source_target_pairs={{0,48},{1,13},{4,52},{5,1},{8,56},{9,5},{12,60},{13,9},{16,0},{17,... | collective-permute-start | bytes 786440 | tf_op jit(solution)/shard_map/ppermute | solution.py:56
  13.1 8.0 %collective-permute-start.5 = (bf16[1024,128]{1,0:T(8,128)(2,1)S(1)}, bf16[1024,128]{1,0:T(8,128)(2,1)S(1)}, u32[]{:S(2)}, u32[]{:S(2)}) collective-permute-start(bf16[1024,128]{1,0:T(8,128)(2,1)S(1)} %pad_maximum_fusion.1), channel_id=1, source_target_pairs={{0,32},{1,9},{4,36},{5,13},{8,40},{9,1},{12,44},{13,5},{16,48},{17... | collective-permute-start | bytes 786440 | tf_op jit(solution)/shard_map/ppermute | solution.py:56
  14.4 2.2 %copy-start.1 = (bf16[4,1,32,128,128]{4,3,2,1,0:T(8,128)(2,1)S(1)}, bf16[4,1,32,128,128]{4,3,2,1,0:T(8,128)(2,1)}, u32[]{:S(2)}) copy-start(bf16[4,1,32,128,128]{4,3,2,1,0:T(8,128)(2,1)} %param.15) | copy-start | bytes 12582916
  21.1 5.0 %collective-permute-start.8 = (bf16[32,128,128]{2,1,0:T(8,128)(2,1)S(1)}, bf16[32,128,128]{2,1,0:T(8,128)(2,1)S(1)}, u32[]{:S(2)}, u32[]{:S(2)}) collective-permute-start(bf16[32,128,128]{2,1,0:T(8,128)(2,1)S(1)} %bitcast.35), channel_id=1, source_target_pairs={{0,1},{1,0},{2,3},{3,2},{4,5},{5,4},{6,7},{7,6},{8,9},{9,8},{10,11... | collective-permute-start | bytes 3145736 | tf_op jit(solution)/shard_map/ppermute | solution.py:60
  23.4 15.2 %collective-permute-start.6 = (bf16[32,128,128]{2,1,0:T(8,128)(2,1)S(1)}, bf16[32,128,128]{2,1,0:T(8,128)(2,1)S(1)}, u32[]{:S(2)}, u32[]{:S(2)}) collective-permute-start(bf16[32,128,128]{2,1,0:T(8,128)(2,1)S(1)} %bitcast.36), channel_id=1, source_target_pairs={{0,4},{1,17},{4,8},{5,21},{8,12},{9,25},{12,0},{13,29},{16,20},{17... | collective-permute-start | bytes 3145736 | tf_op jit(solution)/shard_map/ppermute | solution.py:316
  24.6 14.0 %collective-permute-start.7 = (bf16[32,128,128]{2,1,0:T(8,128)(2,1)S(1)}, bf16[32,128,128]{2,1,0:T(8,128)(2,1)S(1)}, u32[]{:S(2)}, u32[]{:S(2)}) collective-permute-start(bf16[32,128,128]{2,1,0:T(8,128)(2,1)S(1)} %bitcast.37), channel_id=1, source_target_pairs={{0,12},{1,49},{4,0},{5,53},{8,4},{9,57},{12,8},{13,61},{16,28},{17... | collective-permute-start | bytes 3145736 | tf_op jit(solution)/shard_map/ppermute | solution.py:317
  38.6 4.6 %collective-permute-start.11 = (bf16[32,128,128]{2,1,0:T(8,128)(2,1)S(1)}, bf16[32,128,128]{2,1,0:T(8,128)(2,1)S(1)}, u32[]{:S(2)}, u32[]{:S(2)}) collective-permute-start(bf16[32,128,128]{2,1,0:T(8,128)(2,1)S(1)} %collective-permute-done.6.refs_3_), channel_id=1, source_target_pairs={{0,1},{1,0},{2,3},{3,2},{4,5},{5,4},{6,7},{7,6},{8,9},{9,8},{10,11... | collective-permute-start | bytes 3145736 | tf_op jit(solution)/shard_map/ppermute | solution.py:60
  40.3 3.8 %collective-permute-start.12 = (bf16[32,128,128]{2,1,0:T(8,128)(2,1)S(1)}, bf16[32,128,128]{2,1,0:T(8,128)(2,1)S(1)}, u32[]{:S(2)}, u32[]{:S(2)}) collective-permute-start(bf16[32,128,128]{2,1,0:T(8,128)(2,1)S(1)} %collective-permute-done.7.refs_5_), channel_id=1, source_target_pairs={{0,1},{1,0},{2,3},{3,2},{4,5},{5,4},{6,7},{7,6},{8,9},{9,8},{10,11... | collective-permute-start | bytes 3145736 | tf_op jit(solution)/shard_map/ppermute | solution.py:60
  40.4 11.2 %collective-permute-start.10 = (bf16[16,128,128]{2,1,0:T(8,128)(2,1)S(1)}, bf16[16,128,128]{2,1,0:T(8,128)(2,1)S(1)}, u32[]{:S(2)}, u32[]{:S(2)}) collective-permute-start(bf16[16,128,128]{2,1,0:T(8,128)(2,1)S(1)} %slice.7), channel_id=1, source_target_pairs={{0,4},{1,17},{4,8},{5,21},{8,12},{9,25},{12,0},{13,29},{16,20},{17... | collective-permute-start | bytes 1572872 | tf_op jit(solution)/shard_map/ppermute | solution.py:321
  41.7 13.0 %collective-permute-start.9 = (bf16[16,128,128]{2,1,0:T(8,128)(2,1)S(1)}, bf16[16,128,128]{2,1,0:T(8,128)(2,1)S(1)}, u32[]{:S(2)}, u32[]{:S(2)}) collective-permute-start(bf16[16,128,128]{2,1,0:T(8,128)(2,1)S(1)} %slice.6), channel_id=1, source_target_pairs={{0,12},{1,49},{4,0},{5,53},{8,4},{9,57},{12,8},{13,61},{16,28},{17... | collective-permute-start | bytes 1572872 | tf_op jit(solution)/shard_map/ppermute | solution.py:322
  51.7 3.1 %collective-permute-start.14 = (bf16[16,128,128]{2,1,0:T(8,128)(2,1)S(1)}, bf16[16,128,128]{2,1,0:T(8,128)(2,1)S(1)}, u32[]{:S(2)}, u32[]{:S(2)}) collective-permute-start(bf16[16,128,128]{2,1,0:T(8,128)(2,1)S(1)} %collective-permute-done.10.refs_3_), channel_id=1, source_target_pairs={{0,1},{1,0},{2,3},{3,2},{4,5},{5,4},{6,7},{7,6},{8,9},{9,8},{10,11... | collective-permute-start | bytes 1572872 | tf_op jit(solution)/shard_map/ppermute | solution.py:60
  54.7 3.2 %collective-permute-start.13 = (bf16[16,128,128]{2,1,0:T(8,128)(2,1)S(1)}, bf16[16,128,128]{2,1,0:T(8,128)(2,1)S(1)}, u32[]{:S(2)}, u32[]{:S(2)}) collective-permute-start(bf16[16,128,128]{2,1,0:T(8,128)(2,1)S(1)} %collective-permute-done.9.refs_4_), channel_id=1, source_target_pairs={{0,1},{1,0},{2,3},{3,2},{4,5},{5,4},{6,7},{7,6},{8,9},{9,8},{10,11... | collective-permute-start | bytes 1572872 | tf_op jit(solution)/shard_map/ppermute | solution.py:60
  60.4 4.7 %collective-permute-start.15 = (bf16[2,128,128]{2,1,0:T(8,128)(2,1)S(1)}, bf16[2,128,128]{2,1,0:T(8,128)(2,1)S(1)}, u32[]{:S(2)}, u32[]{:S(2)}) collective-permute-start(bf16[2,128,128]{2,1,0:T(8,128)(2,1)S(1)} %get-tuple-element.44), channel_id=1, source_target_pairs={{0,64},{64,0},{1,65},{65,1},{2,66},{66,2},{3,67},{67,3},{4,68},{68... | collective-permute-start | bytes 196616 | tf_op jit(solution)/shard_map/ppermute | solution.py:331

commit v3 on v2

--- a/solution.py
+++ b/solution.py
@@ -16,10 +16,10 @@
 BLOCKS = 64
 ZERO = RELS * POOL
 UNIT = 4
-WIDE = (16, 16, 8, 8, 8)
-SIZES = (64, 128, 16, 32, 16)
+WIDE = (16, 16, 8, 8, 8, 8)
+SIZES = (64, 128, 16, 32, 16, 64)
 STAGES = len(SIZES)
-FLOPS = (4 << 30, 8 << 30, 1 << 30, 2 << 30, 1 << 30)
+FLOPS = (4 << 30, 8 << 30, 1 << 30, 2 << 30, 1 << 30, 2 << 30)
 
 
 def most_chunks(st):
@@ -95,45 +95,42 @@
     lists, at, ids = [], [], []
     for r in range(RELS):
         packed = packed_ref[r]
-        cols = (packed >> 2) & 3
+        tile, cols = packed & 3, (packed >> 2) & 3
         ids.append((packed >> 4) & 31)
+        stays = (third == 3) & ((tile >> 1) == (my_x >> 1))
         dx = place((cols >> 1) * 2 + low - my_x)
-        at.append(buf + (second * 4 + dx) * 2 + (cols & 1))
+        at.append(jnp.where(stays, other * 32, buf) + (second * 4 + dx) * 2 + (cols & 1))
         live = slot < (packed >> 9)
-        lists.append(jnp.where(live, stage * TPB + (packed & 3), STAGES * TPB))
-    members = [
-        jnp.where(lists[r] == st * TPB + t, 1.0, 0.0)
-        for st in range(STAGES)
-        for r in range(RELS)
-        for t in range(TPB)
-    ]
-    member = jnp.concatenate(members, 0)
+        lists.append(jnp.where(live, jnp.where(stays, STAGES - 1, stage) * TPB + tile, STAGES * TPB))
+    square = (RELS * TPB * SLOTS, RELS * TPB * SLOTS)
+    row, col = iota(square, 0), iota(square, 1)
+    same = (row >> 3) == (col >> 3)
+    before = jnp.where(same & (col < row), 1.0, 0.0)
+    whole = jnp.where(same, 1.0, 0.0)
+    earlier = jnp.where(((col >> 3) < (row >> 3)) & ((col & 7) == 0), 1.0, 0.0)
     lanes = (BLOCKS, BLOCKS)
-    ahead = exact_dot(member, jnp.where(iota(lanes, 0) < iota(lanes, 1), 1.0, 0.0))
-    row_sum = exact_dot(member, jnp.ones((BLOCKS, TILE), jnp.float32))
-    wide = (GROUPS * SLOTS, GROUPS * SLOTS)
-    row, col = iota(wide, 0), iota(wide, 1)
-    same = (row >> 3) == (col >> 3)
-    above = exact_dot(jnp.where(same & (col < row), 1.0, 0.0), row_sum)
-    length = exact_dot(jnp.where(same, 1.0, 0.0), row_sum)
-    chunks = ((length.astype(jnp.int32) + (UNIT - 1)) >> 2).astype(jnp.float32)
-    earlier = ((row >> 7) == (col >> 7)) & ((col >> 3) < (row >> 3)) & ((col & 7) == 0)
-    begin = exact_dot(jnp.where(earlier, 1.0, 0.0), chunks)
-    step = iota(begin.shape, 0) >> 7
-    base = jnp.zeros_like(step)
-    for st in range(1, STAGES):
-        base = jnp.where(step == st, STARTS[st], base)
-    begin = begin + base.astype(jnp.float32)
-    end = (begin + chunks).astype(jnp.int32)
-    pos = member * ((begin * UNIT + above)[:, :BLOCKS] + ahead)
+    upper = jnp.where(iota(lanes, 0) < iota(lanes, 1), 1.0, 0.0)
+    ones = jnp.ones((BLOCKS, TILE), jnp.float32)
+    pos, end = [], []
+    for st in range(STAGES):
+        member = jnp.concatenate(
+            [jnp.where(lists[r] == st * TPB + t, 1.0, 0.0) for r in range(RELS) for t in range(TPB)], 0
+        )
+        row_sum = exact_dot(member, ones)
+        above = exact_dot(before, row_sum)
+        length = exact_dot(whole, row_sum)
+        chunks = ((length.astype(jnp.int32) + (UNIT - 1)) >> 2).astype(jnp.float32)
+        begin = exact_dot(earlier, chunks) + STARTS[st]
+        end.append((begin + chunks).astype(jnp.int32))
+        pos.append(member * ((begin * UNIT + above)[:, :BLOCKS] + exact_dot(member, upper)))
 
     out = jnp.zeros((PAY_ROWS, 2 * TILE), jnp.float32)
     for r in range(RELS):
         where = jnp.zeros(shape, jnp.float32)
         for st in range(STAGES):
             for t in range(TPB):
-                first = ((st * RELS + r) * TPB + t) * SLOTS
-                where = where + pos[first : first + SLOTS]
+                first = (r * TPB + t) * SLOTS
+                where = where + pos[st][first : first + SLOTS]
         where = jnp.where(lists[r] == STAGES * TPB, -1, where.astype(jnp.int32))
         high, low_part = where >> 7, where & 127
         weight = (ids[r] + (r * POOL - ZERO)).astype(jnp.float32)
@@ -158,12 +155,10 @@
     for st in range(STAGES):
         tile = jnp.zeros((TAB_ROWS, TILE), jnp.int32)
         for g in range(RELS * TPB):
-            first = (st * RELS * TPB + g) * SLOTS
-            tile = tile + jnp.where(index >= end[first : first + SLOTS], 1, 0)
+            tile = tile + jnp.where(index >= end[st][g * SLOTS : (g + 1) * SLOTS], 1, 0)
         inside = (index >= STARTS[st]) & (index < STARTS[st + 1])
         table = jnp.where(inside, jnp.minimum(tile, RELS * TPB - 1), table)
-        last = (st * RELS * TPB + RELS * TPB - 1) * SLOTS
-        total = end[last : last + SLOTS] - STARTS[st]
+        total = end[st][-SLOTS:] - STARTS[st]
         table = jnp.where(index == (TAB_ROWS - 1) * TILE + st, total, table)
     tab_ref[...] = table
     fetch.wait()
@@ -186,26 +181,22 @@
     )(here, packed, pool)
 
 
-def stage_kernel(st, count, first, last, *refs):
+def stage_kernel(st, count, *refs):
     refs = list(refs)
-    pay, tab = refs[:2]
-    del refs[:2]
-    if last:
-        chan = refs.pop(0)
-    pool = refs.pop(0)
-    bufs = refs[:count]
-    del refs[:count]
+    pay, tab, pool = refs[:3]
+    bufs = refs[3 : 3 + count]
+    del refs[: 3 + count]
     copies = []
-    if first:
+    if st == 0:
         total = refs.pop(0)
         total[...] = jnp.zeros_like(total)
+    elif st < STAGES - 2:
+        _, total, *refs = refs
+    elif st == STAGES - 2:
+        _, chan, transforms, total, theirs, *refs = refs
     else:
-        before = refs.pop(0)
-        if last:
-            transforms, selfterm, mine, theirs, total, agg, *refs = refs
-            total[...] = before[...]
-        else:
-            total = refs.pop(0)
+        before, chan, transforms, selfterm, mine, total, *refs = refs
+        total[...] = before[...]
     if count > 1:
         rows, sems = refs
         at = 0
@@ -235,50 +226,42 @@
 
     turns = (tab[TAB_ROWS - 1, st] + (WIDE[st] - 1)) >> (WIDE[st].bit_length() - 1)
     lax.fori_loop(0, turns, turn, 0)
-    if last:
-        for t in range(TPB):
-            acc = None
-            for r in range(RELS):
-                part = jnp.dot(
-                    total[r * TPB + t].astype(jnp.bfloat16), transforms[r], preferred_element_type=jnp.float32
-                )
-                acc = part if acc is None else acc + part
-            agg[t] = acc
-        half = TPB // 2
-        for u in range(half):
-            mine[u] = agg[chan[0] * half + u] + selfterm[u]
-            theirs[u] = agg[(1 - chan[0]) * half + u].astype(jnp.bfloat16)
-
-
-def run_stage(st, lists, pool, bufs, before=None, tail=None):
-    first, last = before is None, tail is not None
-    args, specs = list(lists), [SMEM] * 2
-    if last:
-        args.append(tail[0])
-        specs.append(SMEM)
-    args += [pool, *bufs]
-    specs += [VMEM] + [ANY if len(bufs) > 1 else VMEM] * len(bufs)
+
+    def final(tile):
+        parts = [
+            jnp.dot(total[r * TPB + tile].astype(jnp.bfloat16), transforms[r], preferred_element_type=jnp.float32)
+            for r in range(RELS)
+        ]
+        return (parts[0] + parts[1]) + (parts[2] + parts[3])
+
+    half = TPB // 2
+    for u in range(half):
+        if st == STAGES - 2:
+            theirs[u] = final((1 - chan[0]) * half + u).astype(jnp.bfloat16)
+        if st == STAGES - 1:
+            mine[u] = final(chan[0] * half + u) + selfterm[u]
+
+
+def run_stage(st, lists, pool, bufs, *more):
+    args = [*lists, pool, *bufs, *more]
+    specs = [SMEM] * 2 + [VMEM] + [ANY if len(bufs) > 1 else VMEM] * len(bufs)
+    specs += [VMEM, SMEM, VMEM, VMEM][: len(more)]
     wide = (RELS * TPB, TILE, TILE)
+    half = (TPB // 2, TILE, TILE)
+    out = [jax.ShapeDtypeStruct(wide, jnp.float32)]
     scratch, aliases = [], {}
-    if first:
-        out = [jax.ShapeDtypeStruct(wide, jnp.float32)]
-    else:
-        args.append(before)
-        specs.append(VMEM)
-        if last:
-            args += tail[1:]
-            specs += [VMEM] * 2
-            half = (TPB // 2, TILE, TILE)
-            out = [jax.ShapeDtypeStruct(half, jnp.float32), jax.ShapeDtypeStruct(half, jnp.bfloat16)]
-            scratch = [pltpu.VMEM(wide, jnp.float32), pltpu.VMEM((TPB, TILE, TILE), jnp.float32)]
-        else:
-            out = [jax.ShapeDtypeStruct(wide, jnp.float32)]
-            aliases = {len(args) - 1: 0}
+    if st == STAGES - 1:
+        out = [jax.ShapeDtypeStruct(half, jnp.float32)]
+        scratch = [pltpu.VMEM(wide, jnp.float32)]
+    elif st > 0:
+        aliases = {3 + len(bufs): 0}
+    if st == STAGES - 2:
+        out.append(jax.ShapeDtypeStruct(half, jnp.bfloat16))
     if len(bufs) > 1:
         scratch.append(pltpu.VMEM((SIZES[st], TILE, TILE), jnp.bfloat16))
         scratch.append(pltpu.SemaphoreType.DMA((len(bufs),)))
     return pl.pallas_call(
-        functools.partial(stage_kernel, st, len(bufs), first, last),
+        functools.partial(stage_kernel, st, len(bufs)),
         out_shape=out,
         in_specs=specs,
         out_specs=[VMEM] * len(out),
@@ -327,8 +310,9 @@
     second, total = lax.optimization_barrier((second, total))
     last = sibling(second)
     total = run_stage(3, lists, pool, [other, second], total)[0]
-    kept, sent = run_stage(4, lists, pool, [last], total, (here[:1] >> 1, now, selfterm))
+    total, sent = run_stage(4, lists, pool, [last], total, here[:1] >> 1, now)
     got = lax.ppermute(sent, "chan", [(0, 1), (1, 0)])
+    kept = run_stage(5, lists, pool, [first, second, other, last], total, here[:1] >> 1, now, selfterm)[0]
     updated = jax.nn.relu(kept + got.astype(jnp.float32)).astype(jnp.bfloat16)
     return updated.reshape(1, 1, half_rows, width)
 

time: 66.5 us -> 64.3 us (0.967)
  waiting for transfers between devices: 13.7 us -> 11 us
  starting transfers between devices: 21.6 us -> 22.3 us
    ppermute x1, waiting for transfers between devices: 3.41 us -> 0.01 us  [shards(): got = lax.ppermute(sent, 'chan', [(0, 1), (1, 0)])]
    pallas_call x5 -> x6, Pallas kernels: 20.2 us -> 20.9 us  [run_stage(): pl.pallas_call(functools.partial(stage_kernel, st, len(bufs)), out_shape=...]
  transfers between devices with their start and end apart: 16 -> 16, of which waited for: 5 -> 4; matrix products, arithmetic and copies ran while one was open for 4% -> 4% of each run, Pallas kernels for 33% -> 35%
where the time goes in v3:
time: 64.3 us; the launch traced here: 63.7 us
  Pallas kernels  23.9 us (37%)
  starting transfers between devices  22.3 us (35%)
  waiting for transfers between devices  11 us (17%)
  other arithmetic  3.1 us (5%)
  local copies, waits for them, and re-layouts  2.29 us (4%)
  matrix products  0.98 us (2%)
    pallas_call x6, Pallas kernels, run_stage(): pl.pallas_call(functools.partial(stage_kernel, st, len(bufs)), out_shape=...  20.9 us
    ppermute x6, starting transfers between devices, ring(): lax.ppermute(rows, FLAT, shift(axis_first, axis_second, by))  10.3 us
    ppermute x1, waiting for transfers between devices, shards(): left = lax.ppermute(plane, FLAT, shift(2, 1, 1))  7.87 us
    ppermute x5, starting transfers between devices, sibling(): return lax.ppermute(rows, 'core', [(0, 1), (1, 0)])  4.71 us
    pallas_call x1, Pallas kernels, sort_slots(): pl.pallas_call(sort_kernel, out_shape=[jax.ShapeDtypeStruct((PAY_ROWS, TI...  2.99 us
    unnamed x4, local copies, waits for them, and re-layouts  2.19 us
    ppermute x6, waiting for transfers between devices, ring(): lax.ppermute(rows, FLAT, shift(axis_first, axis_second, by))  2.14 us
    ppermute x1, starting transfers between devices, shards(): got = lax.ppermute(sent, 'chan', [(0, 1), (1, 0)])  1.89 us
  transfers between devices with their start and end apart: 16, of which 4 were waited for; matrix products, arithmetic and copies ran while one was open for 4% of the time, Pallas kernels for 35%

profile of v3, /device:TPU:1, one launch (start us, length us, event | category | flops | bytes accessed | tf_op | source)
XLA Modules:
  0.0 63.7 jit_solution(2555748422536911617)
XLA Ops:
  0.0 0.0 copy-start
  0.0 2.0 %collective-permute-start = (bf16[256,128]{1,0:T(8,128)(2,1)}, bf16[256,128]{1,0:T(8,128)(2,1)S(1)}, u32[]{:S(2)}, u32[]{:S(2)}) collective-permute-start(bf16[256,128]{1,0:T(8,128)(2,1)} %bitcast.39), channel_id=1, source_target_pairs={{0,2},{1,3},{4,6},{5,7},{8,10},{9,11},{12,14},{13,15},{16,18},{17,... | collective-permute-start | bytes 196616 | tf_op jit(solution)/shard_map/ppermute | solution.py:56
  2.0 1.3 %collective-permute-start.1 = (bf16[256,128]{1,0:T(8,128)(2,1)}, bf16[256,128]{1,0:T(8,128)(2,1)S(1)}, u32[]{:S(2)}, u32[]{:S(2)}) collective-permute-start(bf16[256,128]{1,0:T(8,128)(2,1)} %bitcast.40), channel_id=1, source_target_pairs={{0,66},{1,67},{4,70},{5,71},{8,74},{9,75},{12,78},{13,79},{16,82},... | collective-permute-start | bytes 196616 | tf_op jit(solution)/shard_map/ppermute | solution.py:56
  3.4 1.7 %collective-permute-start.2 = (bf16[256,128]{1,0:T(8,128)(2,1)}, bf16[256,128]{1,0:T(8,128)(2,1)S(1)}, u32[]{:S(2)}, u32[]{:S(2)}) collective-permute-start(bf16[256,128]{1,0:T(8,128)(2,1)} %bitcast.41), channel_id=1, source_target_pairs={{0,64},{1,65},{4,68},{5,69},{8,72},{9,73},{12,76},{13,77},{16,80},... | collective-permute-start | bytes 196616 | tf_op jit(solution)/shard_map/ppermute | solution.py:56
  5.0 0.7 %broadcast_shift-left_fusion = s32[4,1,64]{2,1,0:T(1,128)S(1)} fusion(s32[4,1,64]{2,1,0:T(1,128)} %param.14), kind=kLoop, calls=%fused_computation.11 | loop fusion | flops 256 | bytes 2048 | tf_op jit(solution)/shard_map/shift_left | solution.py:291
  5.7 1.0 %fusion.refs_10_ = f32[2,128,128]{2,1,0:T(8,128)S(1)} fusion(bf16[2,128,128]{2,1,0:T(8,128)(2,1)} %bitcast.42, bf16[128,128]{1,0:T(8,128)(2,1)} %param.10), kind=kOutput, calls=%fused_computation.3 | convolution fusion | flops 8388608 | bytes 229376 | tf_op jit(solution)/shard_map/dot_general | solution.py:288
  6.7 0.8 %fusion.2.packed_ref = s32[4,8,64]{2,1,0:T(8,128)S(1)} fusion(s32[4,1,64,8]{2,3,1,0:T(8,128)} %param.13, s32[4,1,64,8]{2,3,1,0:T(8,128)} %param.12, s32[4,1,64,8]{2,3,1,0:T(8,128)} %param.11, s32[4,64]{1,0:T(4,128)S(1)} %bitcast.44), kind=kLoop, calls=%fused_computation.6 | loop fusion | flops 10240 | bytes 33792 | tf_op jit(solution)/shard_map/or | solution.py:291
  7.5 0.0 copy-done
  7.5 0.0 collective-permute-done
  7.5 0.0 collective-permute-done.1
  7.5 0.7 %collective-permute-done.2 = bf16[256,128]{1,0:T(8,128)(2,1)S(1)} collective-permute-done((bf16[256,128]{1,0:T(8,128)(2,1)}, bf16[256,128]{1,0:T(8,128)(2,1)S(1)}, u32[]{:S(2)}, u32[]{:S(2)}) %collective-permute-start.2) | collective-permute-done | bytes 65568 | tf_op jit(solution)/shard_map/ppermute | solution.py:56
  8.2 0.9 %pad_maximum_fusion.1 = bf16[1024,128]{1,0:T(8,128)(2,1)S(1)} fusion(bf16[256,128]{1,0:T(8,128)(2,1)S(1)} %collective-permute-done.2, bf16[256,128]{1,0:T(8,128)(2,1)S(1)} %collective-permute-done.1, bf16[256,128]{1,0:T(8,128)(2,1)S(1)} %collective-permute-done, bf16[256,128]{1,0:T(8,128)(2,1)} %bitcast.43), kind=kLoop, calls=%fused_computation.1 | loop fusion | flops 1048576 | bytes 524288 | tf_op jit(solution)/shard_map/concatenate | solution.py:287
  9.1 1.8 %collective-permute-start.3 = (bf16[1024,128]{1,0:T(8,128)(2,1)S(1)}, bf16[1024,128]{1,0:T(8,128)(2,1)S(1)}, u32[]{:S(2)}, u32[]{:S(2)}) collective-permute-start(bf16[1024,128]{1,0:T(8,128)(2,1)S(1)} %pad_maximum_fusion.1), channel_id=1, source_target_pairs={{0,16},{1,5},{4,20},{5,9},{8,24},{9,13},{12,28},{13,1},{16,32},{17... | collective-permute-start | bytes 786440 | tf_op jit(solution)/shard_map/ppermute | solution.py:56
  10.9 2.2 %collective-permute-start.4 = (bf16[1024,128]{1,0:T(8,128)(2,1)S(1)}, bf16[1024,128]{1,0:T(8,128)(2,1)S(1)}, u32[]{:S(2)}, u32[]{:S(2)}) collective-permute-start(bf16[1024,128]{1,0:T(8,128)(2,1)S(1)} %pad_maximum_fusion.1), channel_id=1, source_target_pairs={{0,48},{1,13},{4,52},{5,1},{8,56},{9,5},{12,60},{13,9},{16,0},{17,... | collective-permute-start | bytes 786440 | tf_op jit(solution)/shard_map/ppermute | solution.py:56
  13.1 1.2 %collective-permute-start.5 = (bf16[1024,128]{1,0:T(8,128)(2,1)S(1)}, bf16[1024,128]{1,0:T(8,128)(2,1)S(1)}, u32[]{:S(2)}, u32[]{:S(2)}) collective-permute-start(bf16[1024,128]{1,0:T(8,128)(2,1)S(1)} %pad_maximum_fusion.1), channel_id=1, source_target_pairs={{0,32},{1,9},{4,36},{5,13},{8,40},{9,1},{12,44},{13,5},{16,48},{17... | collective-permute-start | bytes 786440 | tf_op jit(solution)/shard_map/ppermute | solution.py:56
  14.3 0.1 pad_add_fusion.here_ref
  14.4 0.0 copy-start.1
  14.4 2.2 %copy-done.1 = bf16[4,1,32,128,128]{4,3,2,1,0:T(8,128)(2,1)S(1)} copy-done((bf16[4,1,32,128,128]{4,3,2,1,0:T(8,128)(2,1)S(1)}, bf16[4,1,32,128,128]{4,3,2,1,0:T(8,128)(2,1)}, u32[]{:S(2)}) %copy-start.1) | copy-done | bytes 4194328
  16.6 3.0 %sort_slots.1 = (s32[24,128]{1,0:T(8,128)S(1)}, s32[8,128]{1,0:T(8,128)S(1)}, bf16[129,128,128]{2,1,0:T(8,128)(2,1)S(1)}) custom-call(s32[4]{0:T(128)S(1)} %pad_add_fusion.here_ref, s32[4,8,64]{2,1,0:T(8,128)S(1)} %fusion.2.packed_ref, bf16[128,128,128]{2,1,0:T(8,128)(2,1)S(1)} %bitcast.34), custom_call_target="tpu_custom_call" | custom-call | bytes 8388608 | tf_op jit(solution)/shard_map/sort_slots/pallas_call | solution.py:168
  19.6 0.0 collective-permute-done.3
  19.6 0.0 collective-permute-done.4
  19.6 1.4 %collective-permute-done.5 = bf16[1024,128]{1,0:T(8,128)(2,1)S(1)} collective-permute-done((bf16[1024,128]{1,0:T(8,128)(2,1)S(1)}, bf16[1024,128]{1,0:T(8,128)(2,1)S(1)}, u32[]{:S(2)}, u32[]{:S(2)}) %collective-permute-start.5) | collective-permute-done | bytes 262176 | tf_op jit(solution)/shard_map/ppermute | solution.py:56
  21.1 0.1 pad_maximum_fusion
  21.1 2.3 %collective-permute-start.8 = (bf16[32,128,128]{2,1,0:T(8,128)(2,1)S(1)}, bf16[32,128,128]{2,1,0:T(8,128)(2,1)S(1)}, u32[]{:S(2)}, u32[]{:S(2)}) collective-permute-start(bf16[32,128,128]{2,1,0:T(8,128)(2,1)S(1)} %bitcast.35), channel_id=1, source_target_pairs={{0,1},{1,0},{2,3},{3,2},{4,5},{5,4},{6,7},{7,6},{8,9},{9,8},{10,11... | collective-permute-start | bytes 3145736 | tf_op jit(solution)/shard_map/ppermute | solution.py:60
  23.4 1.1 %collective-permute-start.6 = (bf16[32,128,128]{2,1,0:T(8,128)(2,1)S(1)}, bf16[32,128,128]{2,1,0:T(8,128)(2,1)S(1)}, u32[]{:S(2)}, u32[]{:S(2)}) collective-permute-start(bf16[32,128,128]{2,1,0:T(8,128)(2,1)S(1)} %bitcast.36), channel_id=1, source_target_pairs={{0,4},{1,17},{4,8},{5,21},{8,12},{9,25},{12,0},{13,29},{16,20},{17... | collective-permute-start | bytes 3145736 | tf_op jit(solution)/shard_map/ppermute | solution.py:299
  24.6 1.5 %collective-permute-start.7 = (bf16[32,128,128]{2,1,0:T(8,128)(2,1)S(1)}, bf16[32,128,128]{2,1,0:T(8,128)(2,1)S(1)}, u32[]{:S(2)}, u32[]{:S(2)}) collective-permute-start(bf16[32,128,128]{2,1,0:T(8,128)(2,1)S(1)} %bitcast.37), channel_id=1, source_target_pairs={{0,12},{1,49},{4,0},{5,53},{8,4},{9,57},{12,8},{13,61},{16,28},{17... | collective-permute-start | bytes 3145736 | tf_op jit(solution)/shard_map/ppermute | solution.py:300
  26.1 0.0 collective-permute-done.8.refs_4_
  26.1 4.6 %stage0.1.refs_7_ = f32[16,128,128]{2,1,0:T(8,128)S(1)} custom-call(s32[24,128]{1,0:T(8,128)S(1)} %get-tuple-element.30.refs_0_, s32[8,128]{1,0:T(8,128)S(1)} %get-tuple-element.31.refs_1_, bf16[129,128,128]{2,1,0:T(8,128)(2,1)S(1)} %get-tuple-element.32.refs_2_, bf16[32,128,128]{2,1,0:T(8,128)(2,1)S(1)} %bitcast.38, ...), custom_call_target="tpu_custom_call" | custom-call | flops 4294967296 | bytes 8388608 | tf_op jit(solution)/shard_map/stage0/pallas_call | solution.py:263
  30.7 7.9 %collective-permute-done.6.refs_3_ = bf16[32,128,128]{2,1,0:T(8,128)(2,1)S(1)} collective-permute-done((bf16[32,128,128]{2,1,0:T(8,128)(2,1)S(1)}, bf16[32,128,128]{2,1,0:T(8,128)(2,1)S(1)}, u32[]{:S(2)}, u32[]{:S(2)}) %collective-permute-start.6) | collective-permute-done | bytes 1048608 | tf_op jit(solution)/shard_map/ppermute | solution.py:299
  38.6 0.0 collective-permute-done.7.refs_5_
  38.6 1.7 %collective-permute-start.10 = (bf16[32,128,128]{2,1,0:T(8,128)(2,1)S(1)}, bf16[32,128,128]{2,1,0:T(8,128)(2,1)S(1)}, u32[]{:S(2)}, u32[]{:S(2)}) collective-permute-start(bf16[32,128,128]{2,1,0:T(8,128)(2,1)S(1)} %collective-permute-done.6.refs_3_), channel_id=1, source_target_pairs={{0,1},{1,0},{2,3},{3,2},{4,5},{5,4},{6,7},{7,6},{8,9},{9,8},{10,11... | collective-permute-start | bytes 3145736 | tf_op jit(solution)/shard_map/ppermute | solution.py:60
  40.3 0.0 collective-permute-start.11
  40.4 1.2 %collective-permute-start.9 = (bf16[16,128,128]{2,1,0:T(8,128)(2,1)S(1)}, bf16[16,128,128]{2,1,0:T(8,128)(2,1)S(1)}, u32[]{:S(2)}, u32[]{:S(2)}) collective-permute-start(bf16[16,128,128]{2,1,0:T(8,128)(2,1)S(1)} %slice.6), channel_id=1, source_target_pairs={{0,4},{1,17},{4,8},{5,21},{8,12},{9,25},{12,0},{13,29},{16,20},{17... | collective-permute-start | bytes 1572872 | tf_op jit(solution)/shard_map/ppermute | solution.py:304
  41.7 1.5 %collective-permute-start.12 = (bf16[16,128,128]{2,1,0:T(8,128)(2,1)S(1)}, bf16[16,128,128]{2,1,0:T(8,128)(2,1)S(1)}, u32[]{:S(2)}, u32[]{:S(2)}) collective-permute-start(bf16[16,128,128]{2,1,0:T(8,128)(2,1)S(1)} %slice.7), channel_id=1, source_target_pairs={{0,12},{1,49},{4,0},{5,53},{8,4},{9,57},{12,8},{13,61},{16,28},{17... | collective-permute-start | bytes 1572872 | tf_op jit(solution)/shard_map/ppermute | solution.py:305
  43.2 0.0 collective-permute-done.10.refs_4_
  43.2 0.9 %collective-permute-done.11.refs_6_ = bf16[32,128,128]{2,1,0:T(8,128)(2,1)S(1)} collective-permute-done((bf16[32,128,128]{2,1,0:T(8,128)(2,1)S(1)}, bf16[32,128,128]{2,1,0:T(8,128)(2,1)S(1)}, u32[]{:S(2)}, u32[]{:S(2)}) %collective-permute-start.11) | collective-permute-done | bytes 1048608 | tf_op jit(solution)/shard_map/ppermute | solution.py:60
  44.1 7.5 %stage1.1.refs_4_ = f32[16,128,128]{2,1,0:T(8,128)S(1)} custom-call(s32[24,128]{1,0:T(8,128)S(1)} %get-tuple-element.30.refs_0_, s32[8,128]{1,0:T(8,128)S(1)} %get-tuple-element.31.refs_1_, bf16[129,128,128]{2,1,0:T(8,128)(2,1)S(1)} %get-tuple-element.32.refs_2_, ...), custom_call_target="tpu_custom_call", output_to_operand_aliasing={{}: (7, {})} | custom-call | flops 8589934592 | bytes 8388608 | tf_op jit(solution)/shard_map/stage1/pallas_call | solution.py:263
  51.7 0.0 collective-permute-done.9.refs_3_
  51.7 0.5 collective-permute-start.13
  52.1 1.7 %stage2.1.refs_5_ = f32[16,128,128]{2,1,0:T(8,128)S(1)} custom-call(s32[24,128]{1,0:T(8,128)S(1)} %get-tuple-element.30.refs_0_, s32[8,128]{1,0:T(8,128)S(1)} %get-tuple-element.31.refs_1_, bf16[129,128,128]{2,1,0:T(8,128)(2,1)S(1)} %get-tuple-element.32.refs_2_, ...), custom_call_target="tpu_custom_call", output_to_operand_aliasing={{}: (4, {})} | custom-call | flops 1073741824 | bytes 8388608 | tf_op jit(solution)/shard_map/stage2/pallas_call | solution.py:263
  53.8 0.0 collective-permute-done.12.refs_4_
  53.8 0.2 collective-permute-start.14
  54.0 0.0 collective-permute-done.13.refs_3_.refs_5_
  54.0 2.2 %stage3.1.refs_4_ = f32[16,128,128]{2,1,0:T(8,128)S(1)} custom-call(s32[24,128]{1,0:T(8,128)S(1)} %get-tuple-element.30.refs_0_, s32[8,128]{1,0:T(8,128)S(1)} %get-tuple-element.31.refs_1_, bf16[129,128,128]{2,1,0:T(8,128)(2,1)S(1)} %get-tuple-element.32.refs_2_, ...), custom_call_target="tpu_custom_call", output_to_operand_aliasing={{}: (5, {})} | custom-call | flops 2147483648 | bytes 8388608 | tf_op jit(solution)/shard_map/stage3/pallas_call | solution.py:263
  56.2 0.0 collective-permute-done.14.refs_3_.refs_6_
  56.3 1.9 %stage4.1 = (f32[16,128,128]{2,1,0:T(8,128)S(1)}, bf16[2,128,128]{2,1,0:T(8,128)(2,1)S(1)}) custom-call(s32[24,128]{1,0:T(8,128)S(1)} %get-tuple-element.30.refs_0_, s32[8,128]{1,0:T(8,128)S(1)} %get-tuple-element.31.refs_1_, bf16[129,128,128]{2,1,0:T(8,128)(2,1)S(1)} %get-tuple-element.32.refs_2_, ...), custom_call_target="tpu_custom_call", output_to_operand_aliasing={{0}: (4, {})} | custom-call | flops 1073741824 | bytes 8388608 | tf_op jit(solution)/shard_map/stage4/pallas_call | solution.py:263
  58.2 1.9 %collective-permute-start.15 = (bf16[2,128,128]{2,1,0:T(8,128)(2,1)S(1)}, bf16[2,128,128]{2,1,0:T(8,128)(2,1)S(1)}, u32[]{:S(2)}, u32[]{:S(2)}) collective-permute-start(bf16[2,128,128]{2,1,0:T(8,128)(2,1)S(1)} %get-tuple-element.44), channel_id=1, source_target_pairs={{0,64},{64,0},{1,65},{65,1},{2,66},{66,2},{3,67},{67,3},{4,68},{68... | collective-permute-start | bytes 196616 | tf_op jit(solution)/shard_map/ppermute | solution.py:314
  60.1 3.0 %stage5.1 = f32[2,128,128]{2,1,0:T(8,128)S(1)} custom-call(s32[24,128]{1,0:T(8,128)S(1)} %get-tuple-element.30.refs_0_, s32[8,128]{1,0:T(8,128)S(1)} %get-tuple-element.31.refs_1_, bf16[129,128,128]{2,1,0:T(8,128)(2,1)S(1)} %get-tuple-element.32.refs_2_, bf16[16,128,128]{2,1,0:T(8,128)(2,1)S(1)} %collective-permute-done.9.refs_3_, ...), custom_call_target="tpu_custom_call" | custom-call | flops 2147483648 | bytes 8388608 | tf_op jit(solution)/shard_map/stage5/pallas_call | solution.py:263
  63.1 0.0 collective-permute-done.15
  63.1 0.7 %maximum_convert_fusion = bf16[2,128,128]{2,1,0:T(8,128)(2,1)} fusion(f32[2,128,128]{2,1,0:T(8,128)S(1)} %stage5.1, bf16[2,128,128]{2,1,0:T(8,128)(2,1)S(1)} %collective-permute-done.15), kind=kLoop, calls=%fused_computation.2 | loop fusion | flops 131072 | bytes 262144 | tf_op jit(solution)/shard_map/convert_element_type | solution.py:316
  (3 shorter events, 0.1 us)
Async XLA Ops:
  0.0 7.5 %copy-start = (bf16[8,128,128]{2,1,0:T(8,128)(2,1)S(1)}, bf16[8,128,128]{2,1,0:T(8,128)(2,1)}, u32[]{:S(2)}) copy-start(bf16[8,128,128]{2,1,0:T(8,128)(2,1)} %param.9) | copy-start | bytes 786436
  0.0 7.5 %collective-permute-start = (bf16[256,128]{1,0:T(8,128)(2,1)}, bf16[256,128]{1,0:T(8,128)(2,1)S(1)}, u32[]{:S(2)}, u32[]{:S(2)}) collective-permute-start(bf16[256,128]{1,0:T(8,128)(2,1)} %bitcast.39), channel_id=1, source_target_pairs={{0,2},{1,3},{4,6},{5,7},{8,10},{9,11},{12,14},{13,15},{16,18},{17,... | collective-permute-start | bytes 196616 | tf_op jit(solution)/shard_map/ppermute | solution.py:56
  2.0 5.5 %collective-permute-start.1 = (bf16[256,128]{1,0:T(8,128)(2,1)}, bf16[256,128]{1,0:T(8,128)(2,1)S(1)}, u32[]{:S(2)}, u32[]{:S(2)}) collective-permute-start(bf16[256,128]{1,0:T(8,128)(2,1)} %bitcast.40), channel_id=1, source_target_pairs={{0,66},{1,67},{4,70},{5,71},{8,74},{9,75},{12,78},{13,79},{16,82},... | collective-permute-start | bytes 196616 | tf_op jit(solution)/shard_map/ppermute | solution.py:56
  3.4 4.8 %collective-permute-start.2 = (bf16[256,128]{1,0:T(8,128)(2,1)}, bf16[256,128]{1,0:T(8,128)(2,1)S(1)}, u32[]{:S(2)}, u32[]{:S(2)}) collective-permute-start(bf16[256,128]{1,0:T(8,128)(2,1)} %bitcast.41), channel_id=1, source_target_pairs={{0,64},{1,65},{4,68},{5,69},{8,72},{9,73},{12,76},{13,77},{16,80},... | collective-permute-start | bytes 196616 | tf_op jit(solution)/shard_map/ppermute | solution.py:56
  9.1 10.5 %collective-permute-start.3 = (bf16[1024,128]{1,0:T(8,128)(2,1)S(1)}, bf16[1024,128]{1,0:T(8,128)(2,1)S(1)}, u32[]{:S(2)}, u32[]{:S(2)}) collective-permute-start(bf16[1024,128]{1,0:T(8,128)(2,1)S(1)} %pad_maximum_fusion.1), channel_id=1, source_target_pairs={{0,16},{1,5},{4,20},{5,9},{8,24},{9,13},{12,28},{13,1},{16,32},{17... | collective-permute-start | bytes 786440 | tf_op jit(solution)/shard_map/ppermute | solution.py:56
  10.9 8.7 %collective-permute-start.4 = (bf16[1024,128]{1,0:T(8,128)(2,1)S(1)}, bf16[1024,128]{1,0:T(8,128)(2,1)S(1)}, u32[]{:S(2)}, u32[]{:S(2)}) collective-permute-start(bf16[1024,128]{1,0:T(8,128)(2,1)S(1)} %pad_maximum_fusion.1), channel_id=1, source_target_pairs={{0,48},{1,13},{4,52},{5,1},{8,56},{9,5},{12,60},{13,9},{16,0},{17,... | collective-permute-start | bytes 786440 | tf_op jit(solution)/shard_map/ppermute | solution.py:56
  13.1 8.0 %collective-permute-start.5 = (bf16[1024,128]{1,0:T(8,128)(2,1)S(1)}, bf16[1024,128]{1,0:T(8,128)(2,1)S(1)}, u32[]{:S(2)}, u32[]{:S(2)}) collective-permute-start(bf16[1024,128]{1,0:T(8,128)(2,1)S(1)} %pad_maximum_fusion.1), channel_id=1, source_target_pairs={{0,32},{1,9},{4,36},{5,13},{8,40},{9,1},{12,44},{13,5},{16,48},{17... | collective-permute-start | bytes 786440 | tf_op jit(solution)/shard_map/ppermute | solution.py:56
  14.4 2.2 %copy-start.1 = (bf16[4,1,32,128,128]{4,3,2,1,0:T(8,128)(2,1)S(1)}, bf16[4,1,32,128,128]{4,3,2,1,0:T(8,128)(2,1)}, u32[]{:S(2)}) copy-start(bf16[4,1,32,128,128]{4,3,2,1,0:T(8,128)(2,1)} %param.15) | copy-start | bytes 12582916
  21.1 5.0 %collective-permute-start.8 = (bf16[32,128,128]{2,1,0:T(8,128)(2,1)S(1)}, bf16[32,128,128]{2,1,0:T(8,128)(2,1)S(1)}, u32[]{:S(2)}, u32[]{:S(2)}) collective-permute-start(bf16[32,128,128]{2,1,0:T(8,128)(2,1)S(1)} %bitcast.35), channel_id=1, source_target_pairs={{0,1},{1,0},{2,3},{3,2},{4,5},{5,4},{6,7},{7,6},{8,9},{9,8},{10,11... | collective-permute-start | bytes 3145736 | tf_op jit(solution)/shard_map/ppermute | solution.py:60
  23.4 15.2 %collective-permute-start.6 = (bf16[32,128,128]{2,1,0:T(8,128)(2,1)S(1)}, bf16[32,128,128]{2,1,0:T(8,128)(2,1)S(1)}, u32[]{:S(2)}, u32[]{:S(2)}) collective-permute-start(bf16[32,128,128]{2,1,0:T(8,128)(2,1)S(1)} %bitcast.36), channel_id=1, source_target_pairs={{0,4},{1,17},{4,8},{5,21},{8,12},{9,25},{12,0},{13,29},{16,20},{17... | collective-permute-start | bytes 3145736 | tf_op jit(solution)/shard_map/ppermute | solution.py:299
  24.6 14.0 %collective-permute-start.7 = (bf16[32,128,128]{2,1,0:T(8,128)(2,1)S(1)}, bf16[32,128,128]{2,1,0:T(8,128)(2,1)S(1)}, u32[]{:S(2)}, u32[]{:S(2)}) collective-permute-start(bf16[32,128,128]{2,1,0:T(8,128)(2,1)S(1)} %bitcast.37), channel_id=1, source_target_pairs={{0,12},{1,49},{4,0},{5,53},{8,4},{9,57},{12,8},{13,61},{16,28},{17... | collective-permute-start | bytes 3145736 | tf_op jit(solution)/shard_map/ppermute | solution.py:300
  38.6 4.6 %collective-permute-start.10 = (bf16[32,128,128]{2,1,0:T(8,128)(2,1)S(1)}, bf16[32,128,128]{2,1,0:T(8,128)(2,1)S(1)}, u32[]{:S(2)}, u32[]{:S(2)}) collective-permute-start(bf16[32,128,128]{2,1,0:T(8,128)(2,1)S(1)} %collective-permute-done.6.refs_3_), channel_id=1, source_target_pairs={{0,1},{1,0},{2,3},{3,2},{4,5},{5,4},{6,7},{7,6},{8,9},{9,8},{10,11... | collective-permute-start | bytes 3145736 | tf_op jit(solution)/shard_map/ppermute | solution.py:60
  40.3 3.8 %collective-permute-start.11 = (bf16[32,128,128]{2,1,0:T(8,128)(2,1)S(1)}, bf16[32,128,128]{2,1,0:T(8,128)(2,1)S(1)}, u32[]{:S(2)}, u32[]{:S(2)}) collective-permute-start(bf16[32,128,128]{2,1,0:T(8,128)(2,1)S(1)} %collective-permute-done.7.refs_5_), channel_id=1, source_target_pairs={{0,1},{1,0},{2,3},{3,2},{4,5},{5,4},{6,7},{7,6},{8,9},{9,8},{10,11... | collective-permute-start | bytes 3145736 | tf_op jit(solution)/shard_map/ppermute | solution.py:60
  40.4 11.2 %collective-permute-start.9 = (bf16[16,128,128]{2,1,0:T(8,128)(2,1)S(1)}, bf16[16,128,128]{2,1,0:T(8,128)(2,1)S(1)}, u32[]{:S(2)}, u32[]{:S(2)}) collective-permute-start(bf16[16,128,128]{2,1,0:T(8,128)(2,1)S(1)} %slice.6), channel_id=1, source_target_pairs={{0,4},{1,17},{4,8},{5,21},{8,12},{9,25},{12,0},{13,29},{16,20},{17... | collective-permute-start | bytes 1572872 | tf_op jit(solution)/shard_map/ppermute | solution.py:304
  41.7 12.2 %collective-permute-start.12 = (bf16[16,128,128]{2,1,0:T(8,128)(2,1)S(1)}, bf16[16,128,128]{2,1,0:T(8,128)(2,1)S(1)}, u32[]{:S(2)}, u32[]{:S(2)}) collective-permute-start(bf16[16,128,128]{2,1,0:T(8,128)(2,1)S(1)} %slice.7), channel_id=1, source_target_pairs={{0,12},{1,49},{4,0},{5,53},{8,4},{9,57},{12,8},{13,61},{16,28},{17... | collective-permute-start | bytes 1572872 | tf_op jit(solution)/shard_map/ppermute | solution.py:305
  51.7 2.4 %collective-permute-start.13 = (bf16[16,128,128]{2,1,0:T(8,128)(2,1)S(1)}, bf16[16,128,128]{2,1,0:T(8,128)(2,1)S(1)}, u32[]{:S(2)}, u32[]{:S(2)}) collective-permute-start(bf16[16,128,128]{2,1,0:T(8,128)(2,1)S(1)} %collective-permute-done.9.refs_3_), channel_id=1, source_target_pairs={{0,1},{1,0},{2,3},{3,2},{4,5},{5,4},{6,7},{7,6},{8,9},{9,8},{10,11... | collective-permute-start | bytes 1572872 | tf_op jit(solution)/shard_map/ppermute | solution.py:60
  53.8 2.4 %collective-permute-start.14 = (bf16[16,128,128]{2,1,0:T(8,128)(2,1)S(1)}, bf16[16,128,128]{2,1,0:T(8,128)(2,1)S(1)}, u32[]{:S(2)}, u32[]{:S(2)}) collective-permute-start(bf16[16,128,128]{2,1,0:T(8,128)(2,1)S(1)} %collective-permute-done.12.refs_4_), channel_id=1, source_target_pairs={{0,1},{1,0},{2,3},{3,2},{4,5},{5,4},{6,7},{7,6},{8,9},{9,8},{10,11... | collective-permute-start | bytes 1572872 | tf_op jit(solution)/shard_map/ppermute | solution.py:60
  58.2 4.9 %collective-permute-start.15 = (bf16[2,128,128]{2,1,0:T(8,128)(2,1)S(1)}, bf16[2,128,128]{2,1,0:T(8,128)(2,1)S(1)}, u32[]{:S(2)}, u32[]{:S(2)}) collective-permute-start(bf16[2,128,128]{2,1,0:T(8,128)(2,1)S(1)} %get-tuple-element.44), channel_id=1, source_target_pairs={{0,64},{64,0},{1,65},{65,1},{2,66},{66,2},{3,67},{67,3},{4,68},{68... | collective-permute-start | bytes 196616 | tf_op jit(solution)/shard_map/ppermute | solution.py:314

commit v4 on v3

--- a/solution.py
+++ b/solution.py
@@ -29,6 +29,7 @@
 
 STARTS = tuple(sum(most_chunks(i) for i in range(st)) for st in range(STAGES + 1))
 PAY_ROWS = -(-STARTS[-1] * UNIT // (8 * TILE)) * 8
+PAY_SPANS = tuple((STARTS[st] * UNIT // TILE, -(-STARTS[st + 1] * UNIT // TILE)) for st in range(STAGES))
 TAB_ROWS = 8
 GROUPS = STAGES * RELS * TPB
 
@@ -53,7 +54,11 @@
 
 
 def ring(rows, axis_first, axis_second):
-    return [rows] + [lax.ppermute(rows, FLAT, shift(axis_first, axis_second, by)) for by in (1, -1, 2)]
+    pieces = [rows] + [lax.ppermute(rows, FLAT, shift(axis_first, axis_second, by)) for by in (1, -1, 2)]
+    joined = jnp.zeros((len(pieces) * rows.shape[0], rows.shape[1]), rows.dtype)
+    for i, piece in enumerate(pieces):
+        joined = lax.dynamic_update_slice(joined, piece, (i * rows.shape[0], 0))
+    return joined
 
 
 def sibling(rows):
@@ -73,7 +78,8 @@
     return jnp.dot(left.astype(jnp.bfloat16), right.astype(jnp.bfloat16), preferred_element_type=jnp.float32)
 
 
-def sort_kernel(here_ref, packed_ref, pool_hbm, pay_ref, tab_ref, pool_ref, sem):
+def sort_kernel(here_ref, packed_ref, pool_hbm, *refs):
+    *pay_refs, tab_ref, pool_ref, sem = refs
     fetch = pltpu.make_async_copy(pool_hbm, pool_ref.at[pl.ds(0, ZERO)], sem)
     fetch.start()
     pool_ref[ZERO] = jnp.zeros((TILE, TILE), pool_ref.dtype)
@@ -148,7 +154,9 @@
                 preferred_element_type=jnp.float32,
             )
     out = out.astype(jnp.int32)
-    pay_ref[...] = ((out[:, :TILE] + ZERO) << 7) | out[:, TILE:]
+    pay = ((out[:, :TILE] + ZERO) << 7) | out[:, TILE:]
+    for ref, (first, last) in zip(pay_refs, PAY_SPANS, strict=True):
+        ref[...] = pay[first:last]
 
     index = iota((TAB_ROWS, TILE), 0) * TILE + iota((TAB_ROWS, TILE), 1)
     table = jnp.zeros((TAB_ROWS, TILE), jnp.int32)
@@ -168,12 +176,12 @@
     return pl.pallas_call(
         sort_kernel,
         out_shape=[
-            jax.ShapeDtypeStruct((PAY_ROWS, TILE), jnp.int32),
+            *(jax.ShapeDtypeStruct((last - first, TILE), jnp.int32) for first, last in PAY_SPANS),
             jax.ShapeDtypeStruct((TAB_ROWS, TILE), jnp.int32),
             jax.ShapeDtypeStruct((ZERO + 1, TILE, TILE), pool.dtype),
         ],
         in_specs=[SMEM, VMEM, ANY],
-        out_specs=[VMEM] * 3,
+        out_specs=[VMEM] * (STAGES + 2),
         scratch_shapes=[pltpu.SemaphoreType.DMA],
         compiler_params=pltpu.CompilerParams(vmem_limit_bytes=24 << 20),
         cost_estimate=pl.CostEstimate(flops=0, bytes_accessed=8 << 20, transcendentals=0),
@@ -216,7 +224,7 @@
             chunk = STARTS[st] + i * WIDE[st] + c
             left, right = [], []
             for u in range(UNIT):
-                value = pay[chunk >> 5, (chunk & 31) * UNIT + u]
+                value = pay[(chunk >> 5) - PAY_SPANS[st][0], (chunk & 31) * UNIT + u]
                 left.append(pool[value >> 7])
                 right.append(rows[value & 127])
             total[tab[chunk >> 7, chunk & 127]] += jnp.dot(
@@ -243,7 +251,7 @@
 
 
 def run_stage(st, lists, pool, bufs, *more):
-    args = [*lists, pool, *bufs, *more]
+    args = [lists[st], lists[-1], pool, *bufs, *more]
     specs = [SMEM] * 2 + [VMEM] + [ANY if len(bufs) > 1 else VMEM] * len(bufs)
     specs += [VMEM, SMEM, VMEM, VMEM][: len(more)]
     wide = (RELS * TPB, TILE, TILE)
@@ -284,16 +292,15 @@
     def by_slot(table):
         return table[:, 0].transpose(0, 2, 1)
 
-    line = jnp.concatenate(ring(own, 0, 0), 0)
+    line = ring(own, 0, 0)
     selfterm = jnp.dot(own, self_weight, preferred_element_type=jnp.float32).reshape(-1, TILE, width)
     now = lax.dynamic_slice_in_dim(transforms, chan * RELS, RELS, 0)
     packed = by_slot(tile_rows) | (by_slot(tile_cols) << 2) | (by_slot(tile_ids) << 4)
     packed = packed | (tile_count[:, 0][:, None, :] << 9)
     line, packed, selfterm, now = lax.optimization_barrier((line, packed, selfterm, now))
-    plane = jnp.concatenate(ring(line, 1, 2), 0)
+    plane = ring(line, 1, 2)
     pool = tile_pool.reshape(RELS * POOL, TILE, TILE)
-    pay, tab, pool = sort_slots(here, packed, pool)
-    lists = (pay, tab)
+    *lists, pool = sort_slots(here, packed, pool)
     plane, lists, pool = lax.optimization_barrier((plane, lists, pool))
     plane = plane.reshape(-1, TILE, width)
     left = lax.ppermute(plane, FLAT, shift(2, 1, 1))

time: 64.3 us -> 63.7 us (level)
  local copies, waits for them, and re-layouts: 2.29 us -> 3.46 us
  waiting for transfers between devices: 11 us -> 10 us
  other arithmetic: 3.1 us -> 2.18 us
    dynamic_update_slice x0 -> x8, local copies, waits for them, and re-layouts: none -> 1.17 us  [ring(): joined = lax.dynamic_update_slice(joined, piece, (i * rows.shape[0], 0))]
    concatenate x2 -> x0, other arithmetic: 0.93 us -> none  [the longest x1 0.86 us: shards(): line = jnp.concatenate(ring(own, 0, 0), 0)]
    ppermute x6, waiting for transfers between devices: 2.14 us -> 1.25 us  [ring(): lax.ppermute(rows, FLAT, shift(axis_first, axis_second, by))]
  transfers between devices with their start and end apart: 16 -> 16, of which waited for: 4 -> 3; matrix products, arithmetic and copies ran while one was open for 4% -> 6% of each run, Pallas kernels for 35% -> 35%
where the time goes in v4:
time: 63.7 us; the launch traced here: 63.6 us
  Pallas kernels  24.2 us (38%)
  starting transfers between devices  22.5 us (35%)
  waiting for transfers between devices  10 us (16%)
  local copies, waits for them, and re-layouts  3.46 us (5%)
  other arithmetic  2.18 us (3%)
  matrix products  0.98 us (2%)
    pallas_call x6, Pallas kernels, run_stage(): pl.pallas_call(functools.partial(stage_kernel, st, len(bufs)), out_shape=...  21.2 us
    ppermute x6, starting transfers between devices, ring(): lax.ppermute(rows, FLAT, shift(axis_first, axis_second, by))  10.2 us
    ppermute x1, waiting for transfers between devices, shards(): left = lax.ppermute(plane, FLAT, shift(2, 1, 1))  7.84 us
    ppermute x5, starting transfers between devices, sibling(): return lax.ppermute(rows, 'core', [(0, 1), (1, 0)])  4.56 us
    pallas_call x1, Pallas kernels, sort_slots(): pl.pallas_call(sort_kernel, out_shape=[*(jax.ShapeDtypeStruct((last - fir...  2.99 us
    ppermute x1, starting transfers between devices, shards(): got = lax.ppermute(sent, 'chan', [(0, 1), (1, 0)])  2.36 us
    unnamed x4, local copies, waits for them, and re-layouts  2.19 us
    ppermute x1, starting transfers between devices, shards(): right = lax.ppermute(plane, FLAT, shift(2, 1, -1))  1.54 us
  transfers between devices with their start and end apart: 16, of which 3 were waited for; matrix products, arithmetic and copies ran while one was open for 6% of the time, Pallas kernels for 35%

profile of v4, /device:TPU:1, one launch (start us, length us, event | category | flops | bytes accessed | tf_op | source)
XLA Modules:
  0.0 63.6 jit_solution(6767828656842769386)
XLA Ops:
  0.0 0.0 copy-start
  0.0 2.0 %collective-permute-start = (bf16[256,128]{1,0:T(8,128)(2,1)}, bf16[256,128]{1,0:T(8,128)(2,1)S(1)}, u32[]{:S(2)}, u32[]{:S(2)}) collective-permute-start(bf16[256,128]{1,0:T(8,128)(2,1)} %bitcast.39), channel_id=1, source_target_pairs={{0,2},{1,3},{4,6},{5,7},{8,10},{9,11},{12,14},{13,15},{16,18},{17,... | collective-permute-start | bytes 196616 | tf_op jit(solution)/shard_map/ppermute | solution.py:57
  2.0 1.3 %collective-permute-start.1 = (bf16[256,128]{1,0:T(8,128)(2,1)}, bf16[256,128]{1,0:T(8,128)(2,1)S(1)}, u32[]{:S(2)}, u32[]{:S(2)}) collective-permute-start(bf16[256,128]{1,0:T(8,128)(2,1)} %bitcast.40), channel_id=1, source_target_pairs={{0,66},{1,67},{4,70},{5,71},{8,74},{9,75},{12,78},{13,79},{16,82},... | collective-permute-start | bytes 196616 | tf_op jit(solution)/shard_map/ppermute | solution.py:57
  3.4 1.7 %collective-permute-start.2 = (bf16[256,128]{1,0:T(8,128)(2,1)}, bf16[256,128]{1,0:T(8,128)(2,1)S(1)}, u32[]{:S(2)}, u32[]{:S(2)}) collective-permute-start(bf16[256,128]{1,0:T(8,128)(2,1)} %bitcast.41), channel_id=1, source_target_pairs={{0,64},{1,65},{4,68},{5,69},{8,72},{9,73},{12,76},{13,77},{16,80},... | collective-permute-start | bytes 196616 | tf_op jit(solution)/shard_map/ppermute | solution.py:57
  5.0 0.9 %dynamic_update_slice.24 = bf16[1024,128]{1,0:T(8,128)(2,1)S(1)} pad(bf16[256,128]{1,0:T(8,128)(2,1)} %bitcast.42, bf16[]{:T(256)} %constant.19.clone.1), padding=0_768x0_0 | pad | bytes 327682 | tf_op jit(solution)/shard_map/dynamic_update_slice | solution.py:60
  5.9 0.7 %broadcast_shift-left_fusion = s32[4,1,64]{2,1,0:T(1,128)S(1)} fusion(s32[4,1,64]{2,1,0:T(1,128)} %param.14), kind=kLoop, calls=%fused_computation.16 | loop fusion | flops 256 | bytes 2048 | tf_op jit(solution)/shard_map/shift_left | solution.py:299
  6.6 1.0 %fusion.refs_10_ = f32[2,128,128]{2,1,0:T(8,128)S(1)} fusion(bf16[2,128,128]{2,1,0:T(8,128)(2,1)} %bitcast.43, bf16[128,128]{1,0:T(8,128)(2,1)} %param.10), kind=kOutput, calls=%fused_computation.1 | convolution fusion | flops 8388608 | bytes 229376 | tf_op jit(solution)/shard_map/dot_general | solution.py:296
  7.6 0.8 %fusion.2.packed_ref = s32[4,8,64]{2,1,0:T(8,128)S(1)} fusion(s32[4,1,64,8]{2,3,1,0:T(8,128)} %param.13, s32[4,1,64,8]{2,3,1,0:T(8,128)} %param.12, s32[4,1,64,8]{2,3,1,0:T(8,128)} %param.11, s32[4,64]{1,0:T(4,128)S(1)} %bitcast.44), kind=kLoop, calls=%fused_computation.4 | loop fusion | flops 10240 | bytes 33792 | tf_op jit(solution)/shard_map/or | solution.py:299
  8.4 0.0 copy-done
  8.4 0.0 collective-permute-done
  8.5 0.0 collective-permute-done.1
  8.5 0.0 collective-permute-done.2
  8.5 1.7 %collective-permute-start.3 = (bf16[1024,128]{1,0:T(8,128)(2,1)S(1)}, bf16[1024,128]{1,0:T(8,128)(2,1)S(1)}, u32[]{:S(2)}, u32[]{:S(2)}) collective-permute-start(bf16[1024,128]{1,0:T(8,128)(2,1)S(1)} %constant_dynamic-update-slice_fusion.3), channel_id=1, source_target_pairs={{0,16},{1,5},{4,20},{5,9},{8,24},{9,13},{12,28},{13,1},{16,32},{17... | collective-permute-start | bytes 786440 | tf_op jit(solution)/shard_map/ppermute | solution.py:57
  10.2 2.2 %collective-permute-start.4 = (bf16[1024,128]{1,0:T(8,128)(2,1)S(1)}, bf16[1024,128]{1,0:T(8,128)(2,1)S(1)}, u32[]{:S(2)}, u32[]{:S(2)}) collective-permute-start(bf16[1024,128]{1,0:T(8,128)(2,1)S(1)} %constant_dynamic-update-slice_fusion.3), channel_id=1, source_target_pairs={{0,48},{1,13},{4,52},{5,1},{8,56},{9,5},{12,60},{13,9},{16,0},{17,... | collective-permute-start | bytes 786440 | tf_op jit(solution)/shard_map/ppermute | solution.py:57
  12.4 1.2 %collective-permute-start.5 = (bf16[1024,128]{1,0:T(8,128)(2,1)S(1)}, bf16[1024,128]{1,0:T(8,128)(2,1)S(1)}, u32[]{:S(2)}, u32[]{:S(2)}) collective-permute-start(bf16[1024,128]{1,0:T(8,128)(2,1)S(1)} %constant_dynamic-update-slice_fusion.3), channel_id=1, source_target_pairs={{0,32},{1,9},{4,36},{5,13},{8,40},{9,1},{12,44},{13,5},{16,48},{17... | collective-permute-start | bytes 786440 | tf_op jit(solution)/shard_map/ppermute | solution.py:57
  13.6 0.1 pad_add_fusion.here_ref
  13.7 0.1 dynamic_update_slice.28
  13.8 0.0 copy-start.1
  13.9 2.2 %copy-done.1 = bf16[4,1,32,128,128]{4,3,2,1,0:T(8,128)(2,1)S(1)} copy-done((bf16[4,1,32,128,128]{4,3,2,1,0:T(8,128)(2,1)S(1)}, bf16[4,1,32,128,128]{4,3,2,1,0:T(8,128)(2,1)}, u32[]{:S(2)}) %copy-start.1) | copy-done | bytes 4194328
  16.0 3.0 %sort_slots.1 = (s32[5,128]{1,0:T(8,128)S(1)}, s32[9,128]{1,0:T(8,128)S(1)}, s32[2,128]{1,0:T(2,128)S(1)}, s32[3,128]{1,0:T(4,128)S(1)}, s32[2,128]{1,0:T(2,128)...) custom-call(s32[4]{0:T(128)S(1)} %pad_add_fusion.here_ref, ...), custom_call_target="tpu_custom_call" | custom-call | bytes 8388608 | tf_op jit(solution)/shard_map/sort_slots/pallas_call | solution.py:176
  19.0 0.0 collective-permute-done.3
  19.1 0.0 collective-permute-done.4
  19.1 1.2 %collective-permute-done.5 = bf16[1024,128]{1,0:T(8,128)(2,1)S(1)} collective-permute-done((bf16[1024,128]{1,0:T(8,128)(2,1)S(1)}, bf16[1024,128]{1,0:T(8,128)(2,1)S(1)}, u32[]{:S(2)}, u32[]{:S(2)}) %collective-permute-start.5) | collective-permute-done | bytes 262176 | tf_op jit(solution)/shard_map/ppermute | solution.py:57
  20.4 2.1 %collective-permute-start.8 = (bf16[32,128,128]{2,1,0:T(8,128)(2,1)S(1)}, bf16[32,128,128]{2,1,0:T(8,128)(2,1)S(1)}, u32[]{:S(2)}, u32[]{:S(2)}) collective-permute-start(bf16[32,128,128]{2,1,0:T(8,128)(2,1)S(1)} %bitcast.35), channel_id=1, source_target_pairs={{0,1},{1,0},{2,3},{3,2},{4,5},{5,4},{6,7},{7,6},{8,9},{9,8},{10,11... | collective-permute-start | bytes 3145736 | tf_op jit(solution)/shard_map/ppermute | solution.py:65
  22.6 1.1 %collective-permute-start.6 = (bf16[32,128,128]{2,1,0:T(8,128)(2,1)S(1)}, bf16[32,128,128]{2,1,0:T(8,128)(2,1)S(1)}, u32[]{:S(2)}, u32[]{:S(2)}) collective-permute-start(bf16[32,128,128]{2,1,0:T(8,128)(2,1)S(1)} %bitcast.36), channel_id=1, source_target_pairs={{0,4},{1,17},{4,8},{5,21},{8,12},{9,25},{12,0},{13,29},{16,20},{17... | collective-permute-start | bytes 3145736 | tf_op jit(solution)/shard_map/ppermute | solution.py:306
  23.7 1.5 %collective-permute-start.7 = (bf16[32,128,128]{2,1,0:T(8,128)(2,1)S(1)}, bf16[32,128,128]{2,1,0:T(8,128)(2,1)S(1)}, u32[]{:S(2)}, u32[]{:S(2)}) collective-permute-start(bf16[32,128,128]{2,1,0:T(8,128)(2,1)S(1)} %bitcast.37), channel_id=1, source_target_pairs={{0,12},{1,49},{4,0},{5,53},{8,4},{9,57},{12,8},{13,61},{16,28},{17... | collective-permute-start | bytes 3145736 | tf_op jit(solution)/shard_map/ppermute | solution.py:307
  25.2 0.0 collective-permute-done.8.refs_4_
  25.2 4.6 %stage0.1.refs_7_ = f32[16,128,128]{2,1,0:T(8,128)S(1)} custom-call(s32[5,128]{1,0:T(8,128)S(1)} %get-tuple-element.49.refs_0_, s32[8,128]{1,0:T(8,128)S(1)} %get-tuple-element.46.refs_1_, bf16[129,128,128]{2,1,0:T(8,128)(2,1)S(1)} %get-tuple-element.47.refs_2_, bf16[32,128,128]{2,1,0:T(8,128)(2,1)S(1)} %bitcast.38, ...), custom_call_target="tpu_custom_call" | custom-call | flops 4294967296 | bytes 8388608 | tf_op jit(solution)/shard_map/stage0/pallas_call | solution.py:271
  29.9 7.8 %collective-permute-done.6.refs_3_ = bf16[32,128,128]{2,1,0:T(8,128)(2,1)S(1)} collective-permute-done((bf16[32,128,128]{2,1,0:T(8,128)(2,1)S(1)}, bf16[32,128,128]{2,1,0:T(8,128)(2,1)S(1)}, u32[]{:S(2)}, u32[]{:S(2)}) %collective-permute-start.6) | collective-permute-done | bytes 1048608 | tf_op jit(solution)/shard_map/ppermute | solution.py:306
  37.7 0.0 collective-permute-done.7.refs_5_
  37.7 1.7 %collective-permute-start.10 = (bf16[32,128,128]{2,1,0:T(8,128)(2,1)S(1)}, bf16[32,128,128]{2,1,0:T(8,128)(2,1)S(1)}, u32[]{:S(2)}, u32[]{:S(2)}) collective-permute-start(bf16[32,128,128]{2,1,0:T(8,128)(2,1)S(1)} %collective-permute-done.6.refs_3_), channel_id=1, source_target_pairs={{0,1},{1,0},{2,3},{3,2},{4,5},{5,4},{6,7},{7,6},{8,9},{9,8},{10,11... | collective-permute-start | bytes 3145736 | tf_op jit(solution)/shard_map/ppermute | solution.py:65
  39.5 0.0 collective-permute-start.11
  39.6 1.2 %collective-permute-start.9 = (bf16[16,128,128]{2,1,0:T(8,128)(2,1)S(1)}, bf16[16,128,128]{2,1,0:T(8,128)(2,1)S(1)}, u32[]{:S(2)}, u32[]{:S(2)}) collective-permute-start(bf16[16,128,128]{2,1,0:T(8,128)(2,1)S(1)} %slice.6), channel_id=1, source_target_pairs={{0,4},{1,17},{4,8},{5,21},{8,12},{9,25},{12,0},{13,29},{16,20},{17... | collective-permute-start | bytes 1572872 | tf_op jit(solution)/shard_map/ppermute | solution.py:311
  40.8 1.5 %collective-permute-start.12 = (bf16[16,128,128]{2,1,0:T(8,128)(2,1)S(1)}, bf16[16,128,128]{2,1,0:T(8,128)(2,1)S(1)}, u32[]{:S(2)}, u32[]{:S(2)}) collective-permute-start(bf16[16,128,128]{2,1,0:T(8,128)(2,1)S(1)} %slice.7), channel_id=1, source_target_pairs={{0,12},{1,49},{4,0},{5,53},{8,4},{9,57},{12,8},{13,61},{16,28},{17... | collective-permute-start | bytes 1572872 | tf_op jit(solution)/shard_map/ppermute | solution.py:312
  42.3 0.0 collective-permute-done.10.refs_4_
  42.3 0.9 %collective-permute-done.11.refs_6_ = bf16[32,128,128]{2,1,0:T(8,128)(2,1)S(1)} collective-permute-done((bf16[32,128,128]{2,1,0:T(8,128)(2,1)S(1)}, bf16[32,128,128]{2,1,0:T(8,128)(2,1)S(1)}, u32[]{:S(2)}, u32[]{:S(2)}) %collective-permute-start.11) | collective-permute-done | bytes 1048608 | tf_op jit(solution)/shard_map/ppermute | solution.py:65
  43.2 7.9 %stage1.1.refs_4_ = f32[16,128,128]{2,1,0:T(8,128)S(1)} custom-call(s32[9,128]{1,0:T(8,128)S(1)} %get-tuple-element.51.refs_0_, s32[8,128]{1,0:T(8,128)S(1)} %get-tuple-element.46.refs_1_, bf16[129,128,128]{2,1,0:T(8,128)(2,1)S(1)} %get-tuple-element.47.refs_2_, ...), custom_call_target="tpu_custom_call", output_to_operand_aliasing={{}: (7, {})} | custom-call | flops 8589934592 | bytes 8388608 | tf_op jit(solution)/shard_map/stage1/pallas_call | solution.py:271
  51.1 0.0 collective-permute-done.9.refs_3_
  51.1 0.5 collective-permute-start.13
  51.6 1.5 %stage2.1.refs_5_ = f32[16,128,128]{2,1,0:T(8,128)S(1)} custom-call(s32[2,128]{1,0:T(2,128)S(1)} %get-tuple-element.55.refs_0_, s32[8,128]{1,0:T(8,128)S(1)} %get-tuple-element.46.refs_1_, bf16[129,128,128]{2,1,0:T(8,128)(2,1)S(1)} %get-tuple-element.47.refs_2_, ...), custom_call_target="tpu_custom_call", output_to_operand_aliasing={{}: (4, {})} | custom-call | flops 1073741824 | bytes 8388608 | tf_op jit(solution)/shard_map/stage2/pallas_call | solution.py:271
  53.1 0.0 collective-permute-done.12.refs_4_
  53.1 0.2 collective-permute-start.14
  53.3 0.0 collective-permute-done.13.refs_3_.refs_5_
  53.3 2.1 %stage3.1.refs_4_ = f32[16,128,128]{2,1,0:T(8,128)S(1)} custom-call(s32[3,128]{1,0:T(4,128)S(1)} %get-tuple-element.59.refs_0_, s32[8,128]{1,0:T(8,128)S(1)} %get-tuple-element.46.refs_1_, bf16[129,128,128]{2,1,0:T(8,128)(2,1)S(1)} %get-tuple-element.47.refs_2_, ...), custom_call_target="tpu_custom_call", output_to_operand_aliasing={{}: (5, {})} | custom-call | flops 2147483648 | bytes 8388608 | tf_op jit(solution)/shard_map/stage3/pallas_call | solution.py:271
  55.4 0.0 collective-permute-done.14.refs_3_.refs_6_
  55.4 1.7 %stage4.1 = (f32[16,128,128]{2,1,0:T(8,128)S(1)}, bf16[2,128,128]{2,1,0:T(8,128)(2,1)S(1)}) custom-call(s32[2,128]{1,0:T(2,128)S(1)} %get-tuple-element.58.refs_0_, s32[8,128]{1,0:T(8,128)S(1)} %get-tuple-element.46.refs_1_, bf16[129,128,128]{2,1,0:T(8,128)(2,1)S(1)} %get-tuple-element.47.refs_2_, ...), custom_call_target="tpu_custom_call", output_to_operand_aliasing={{0}: (4, {})} | custom-call | flops 1073741824 | bytes 8388608 | tf_op jit(solution)/shard_map/stage4/pallas_call | solution.py:271
  57.2 2.4 %collective-permute-start.15 = (bf16[2,128,128]{2,1,0:T(8,128)(2,1)S(1)}, bf16[2,128,128]{2,1,0:T(8,128)(2,1)S(1)}, u32[]{:S(2)}, u32[]{:S(2)}) collective-permute-start(bf16[2,128,128]{2,1,0:T(8,128)(2,1)S(1)} %get-tuple-element.64), channel_id=1, source_target_pairs={{0,64},{64,0},{1,65},{65,1},{2,66},{66,2},{3,67},{67,3},{4,68},{68... | collective-permute-start | bytes 196616 | tf_op jit(solution)/shard_map/ppermute | solution.py:321
  59.5 3.4 %stage5.1 = f32[2,128,128]{2,1,0:T(8,128)S(1)} custom-call(s32[5,128]{1,0:T(8,128)S(1)} %get-tuple-element.45.refs_0_, s32[8,128]{1,0:T(8,128)S(1)} %get-tuple-element.46.refs_1_, bf16[129,128,128]{2,1,0:T(8,128)(2,1)S(1)} %get-tuple-element.47.refs_2_, bf16[16,128,128]{2,1,0:T(8,128)(2,1)S(1)} %collective-permute-done.9.refs_3_, ...), custom_call_target="tpu_custom_call" | custom-call | flops 2147483648 | bytes 8388608 | tf_op jit(solution)/shard_map/stage5/pallas_call | solution.py:271
  63.0 0.0 collective-permute-done.15
  63.0 0.7 %maximum_convert_fusion = bf16[2,128,128]{2,1,0:T(8,128)(2,1)} fusion(f32[2,128,128]{2,1,0:T(8,128)S(1)} %stage5.1, bf16[2,128,128]{2,1,0:T(8,128)(2,1)S(1)} %collective-permute-done.15), kind=kLoop, calls=%fused_computation | loop fusion | flops 131072 | bytes 262144 | tf_op jit(solution)/shard_map/convert_element_type | solution.py:323
  (9 shorter events, 0.2 us)
Async XLA Ops:
  0.0 8.4 %copy-start = (bf16[8,128,128]{2,1,0:T(8,128)(2,1)S(1)}, bf16[8,128,128]{2,1,0:T(8,128)(2,1)}, u32[]{:S(2)}) copy-start(bf16[8,128,128]{2,1,0:T(8,128)(2,1)} %param.9) | copy-start | bytes 786436
  0.0 8.4 %collective-permute-start = (bf16[256,128]{1,0:T(8,128)(2,1)}, bf16[256,128]{1,0:T(8,128)(2,1)S(1)}, u32[]{:S(2)}, u32[]{:S(2)}) collective-permute-start(bf16[256,128]{1,0:T(8,128)(2,1)} %bitcast.39), channel_id=1, source_target_pairs={{0,2},{1,3},{4,6},{5,7},{8,10},{9,11},{12,14},{13,15},{16,18},{17,... | collective-permute-start | bytes 196616 | tf_op jit(solution)/shard_map/ppermute | solution.py:57
  2.0 6.4 %collective-permute-start.1 = (bf16[256,128]{1,0:T(8,128)(2,1)}, bf16[256,128]{1,0:T(8,128)(2,1)S(1)}, u32[]{:S(2)}, u32[]{:S(2)}) collective-permute-start(bf16[256,128]{1,0:T(8,128)(2,1)} %bitcast.40), channel_id=1, source_target_pairs={{0,66},{1,67},{4,70},{5,71},{8,74},{9,75},{12,78},{13,79},{16,82},... | collective-permute-start | bytes 196616 | tf_op jit(solution)/shard_map/ppermute | solution.py:57
  3.4 5.1 %collective-permute-start.2 = (bf16[256,128]{1,0:T(8,128)(2,1)}, bf16[256,128]{1,0:T(8,128)(2,1)S(1)}, u32[]{:S(2)}, u32[]{:S(2)}) collective-permute-start(bf16[256,128]{1,0:T(8,128)(2,1)} %bitcast.41), channel_id=1, source_target_pairs={{0,64},{1,65},{4,68},{5,69},{8,72},{9,73},{12,76},{13,77},{16,80},... | collective-permute-start | bytes 196616 | tf_op jit(solution)/shard_map/ppermute | solution.py:57
  8.5 10.5 %collective-permute-start.3 = (bf16[1024,128]{1,0:T(8,128)(2,1)S(1)}, bf16[1024,128]{1,0:T(8,128)(2,1)S(1)}, u32[]{:S(2)}, u32[]{:S(2)}) collective-permute-start(bf16[1024,128]{1,0:T(8,128)(2,1)S(1)} %constant_dynamic-update-slice_fusion.3), channel_id=1, source_target_pairs={{0,16},{1,5},{4,20},{5,9},{8,24},{9,13},{12,28},{13,1},{16,32},{17... | collective-permute-start | bytes 786440 | tf_op jit(solution)/shard_map/ppermute | solution.py:57
  10.2 8.9 %collective-permute-start.4 = (bf16[1024,128]{1,0:T(8,128)(2,1)S(1)}, bf16[1024,128]{1,0:T(8,128)(2,1)S(1)}, u32[]{:S(2)}, u32[]{:S(2)}) collective-permute-start(bf16[1024,128]{1,0:T(8,128)(2,1)S(1)} %constant_dynamic-update-slice_fusion.3), channel_id=1, source_target_pairs={{0,48},{1,13},{4,52},{5,1},{8,56},{9,5},{12,60},{13,9},{16,0},{17,... | collective-permute-start | bytes 786440 | tf_op jit(solution)/shard_map/ppermute | solution.py:57
  12.4 8.0 %collective-permute-start.5 = (bf16[1024,128]{1,0:T(8,128)(2,1)S(1)}, bf16[1024,128]{1,0:T(8,128)(2,1)S(1)}, u32[]{:S(2)}, u32[]{:S(2)}) collective-permute-start(bf16[1024,128]{1,0:T(8,128)(2,1)S(1)} %constant_dynamic-update-slice_fusion.3), channel_id=1, source_target_pairs={{0,32},{1,9},{4,36},{5,13},{8,40},{9,1},{12,44},{13,5},{16,48},{17... | collective-permute-start | bytes 786440 | tf_op jit(solution)/shard_map/ppermute | solution.py:57
  13.8 2.2 %copy-start.1 = (bf16[4,1,32,128,128]{4,3,2,1,0:T(8,128)(2,1)S(1)}, bf16[4,1,32,128,128]{4,3,2,1,0:T(8,128)(2,1)}, u32[]{:S(2)}) copy-start(bf16[4,1,32,128,128]{4,3,2,1,0:T(8,128)(2,1)} %param.15) | copy-start | bytes 12582916
  20.4 4.8 %collective-permute-start.8 = (bf16[32,128,128]{2,1,0:T(8,128)(2,1)S(1)}, bf16[32,128,128]{2,1,0:T(8,128)(2,1)S(1)}, u32[]{:S(2)}, u32[]{:S(2)}) collective-permute-start(bf16[32,128,128]{2,1,0:T(8,128)(2,1)S(1)} %bitcast.35), channel_id=1, source_target_pairs={{0,1},{1,0},{2,3},{3,2},{4,5},{5,4},{6,7},{7,6},{8,9},{9,8},{10,11... | collective-permute-start | bytes 3145736 | tf_op jit(solution)/shard_map/ppermute | solution.py:65
  22.6 15.2 %collective-permute-start.6 = (bf16[32,128,128]{2,1,0:T(8,128)(2,1)S(1)}, bf16[32,128,128]{2,1,0:T(8,128)(2,1)S(1)}, u32[]{:S(2)}, u32[]{:S(2)}) collective-permute-start(bf16[32,128,128]{2,1,0:T(8,128)(2,1)S(1)} %bitcast.36), channel_id=1, source_target_pairs={{0,4},{1,17},{4,8},{5,21},{8,12},{9,25},{12,0},{13,29},{16,20},{17... | collective-permute-start | bytes 3145736 | tf_op jit(solution)/shard_map/ppermute | solution.py:306
  23.7 14.0 %collective-permute-start.7 = (bf16[32,128,128]{2,1,0:T(8,128)(2,1)S(1)}, bf16[32,128,128]{2,1,0:T(8,128)(2,1)S(1)}, u32[]{:S(2)}, u32[]{:S(2)}) collective-permute-start(bf16[32,128,128]{2,1,0:T(8,128)(2,1)S(1)} %bitcast.37), channel_id=1, source_target_pairs={{0,12},{1,49},{4,0},{5,53},{8,4},{9,57},{12,8},{13,61},{16,28},{17... | collective-permute-start | bytes 3145736 | tf_op jit(solution)/shard_map/ppermute | solution.py:307
  37.7 4.6 %collective-permute-start.10 = (bf16[32,128,128]{2,1,0:T(8,128)(2,1)S(1)}, bf16[32,128,128]{2,1,0:T(8,128)(2,1)S(1)}, u32[]{:S(2)}, u32[]{:S(2)}) collective-permute-start(bf16[32,128,128]{2,1,0:T(8,128)(2,1)S(1)} %collective-permute-done.6.refs_3_), channel_id=1, source_target_pairs={{0,1},{1,0},{2,3},{3,2},{4,5},{5,4},{6,7},{7,6},{8,9},{9,8},{10,11... | collective-permute-start | bytes 3145736 | tf_op jit(solution)/shard_map/ppermute | solution.py:65
  39.5 3.8 %collective-permute-start.11 = (bf16[32,128,128]{2,1,0:T(8,128)(2,1)S(1)}, bf16[32,128,128]{2,1,0:T(8,128)(2,1)S(1)}, u32[]{:S(2)}, u32[]{:S(2)}) collective-permute-start(bf16[32,128,128]{2,1,0:T(8,128)(2,1)S(1)} %collective-permute-done.7.refs_5_), channel_id=1, source_target_pairs={{0,1},{1,0},{2,3},{3,2},{4,5},{5,4},{6,7},{7,6},{8,9},{9,8},{10,11... | collective-permute-start | bytes 3145736 | tf_op jit(solution)/shard_map/ppermute | solution.py:65
  39.6 11.6 %collective-permute-start.9 = (bf16[16,128,128]{2,1,0:T(8,128)(2,1)S(1)}, bf16[16,128,128]{2,1,0:T(8,128)(2,1)S(1)}, u32[]{:S(2)}, u32[]{:S(2)}) collective-permute-start(bf16[16,128,128]{2,1,0:T(8,128)(2,1)S(1)} %slice.6), channel_id=1, source_target_pairs={{0,4},{1,17},{4,8},{5,21},{8,12},{9,25},{12,0},{13,29},{16,20},{17... | collective-permute-start | bytes 1572872 | tf_op jit(solution)/shard_map/ppermute | solution.py:311
  40.8 12.3 %collective-permute-start.12 = (bf16[16,128,128]{2,1,0:T(8,128)(2,1)S(1)}, bf16[16,128,128]{2,1,0:T(8,128)(2,1)S(1)}, u32[]{:S(2)}, u32[]{:S(2)}) collective-permute-start(bf16[16,128,128]{2,1,0:T(8,128)(2,1)S(1)} %slice.7), channel_id=1, source_target_pairs={{0,12},{1,49},{4,0},{5,53},{8,4},{9,57},{12,8},{13,61},{16,28},{17... | collective-permute-start | bytes 1572872 | tf_op jit(solution)/shard_map/ppermute | solution.py:312
  51.1 2.2 %collective-permute-start.13 = (bf16[16,128,128]{2,1,0:T(8,128)(2,1)S(1)}, bf16[16,128,128]{2,1,0:T(8,128)(2,1)S(1)}, u32[]{:S(2)}, u32[]{:S(2)}) collective-permute-start(bf16[16,128,128]{2,1,0:T(8,128)(2,1)S(1)} %collective-permute-done.9.refs_3_), channel_id=1, source_target_pairs={{0,1},{1,0},{2,3},{3,2},{4,5},{5,4},{6,7},{7,6},{8,9},{9,8},{10,11... | collective-permute-start | bytes 1572872 | tf_op jit(solution)/shard_map/ppermute | solution.py:65
  53.1 2.3 %collective-permute-start.14 = (bf16[16,128,128]{2,1,0:T(8,128)(2,1)S(1)}, bf16[16,128,128]{2,1,0:T(8,128)(2,1)S(1)}, u32[]{:S(2)}, u32[]{:S(2)}) collective-permute-start(bf16[16,128,128]{2,1,0:T(8,128)(2,1)S(1)} %collective-permute-done.12.refs_4_), channel_id=1, source_target_pairs={{0,1},{1,0},{2,3},{3,2},{4,5},{5,4},{6,7},{7,6},{8,9},{9,8},{10,11... | collective-permute-start | bytes 1572872 | tf_op jit(solution)/shard_map/ppermute | solution.py:65
  57.2 5.8 %collective-permute-start.15 = (bf16[2,128,128]{2,1,0:T(8,128)(2,1)S(1)}, bf16[2,128,128]{2,1,0:T(8,128)(2,1)S(1)}, u32[]{:S(2)}, u32[]{:S(2)}) collective-permute-start(bf16[2,128,128]{2,1,0:T(8,128)(2,1)S(1)} %get-tuple-element.64), channel_id=1, source_target_pairs={{0,64},{64,0},{1,65},{65,1},{2,66},{66,2},{3,67},{67,3},{4,68},{68... | collective-permute-start | bytes 196616 | tf_op jit(solution)/shard_map/ppermute | solution.py:321

commit v5 on v4

--- a/solution.py
+++ b/solution.py
@@ -16,7 +16,7 @@
 BLOCKS = 64
 ZERO = RELS * POOL
 UNIT = 4
-WIDE = (16, 16, 8, 8, 8, 8)
+WIDE = (16, 16, 16, 8, 16, 8)
 SIZES = (64, 128, 16, 32, 16, 64)
 STAGES = len(SIZES)
 FLOPS = (4 << 30, 8 << 30, 1 << 30, 2 << 30, 1 << 30, 2 << 30)

time: 63.7 us -> 63.4 us (level)
  no operation moved by 1% of the time
where the time goes in v5:
time: 63.4 us; the launch traced here: 63.3 us
  Pallas kernels  23.9 us (38%)
  starting transfers between devices  22.5 us (35%)
  waiting for transfers between devices  10 us (16%)
  local copies, waits for them, and re-layouts  3.46 us (5%)
  other arithmetic  2.18 us (3%)
  matrix products  0.98 us (2%)
    pallas_call x6, Pallas kernels, run_stage(): pl.pallas_call(functools.partial(stage_kernel, st, len(bufs)), out_shape=...  20.9 us
    ppermute x6, starting transfers between devices, ring(): lax.ppermute(rows, FLAT, shift(axis_first, axis_second, by))  10.2 us
    ppermute x1, waiting for transfers between devices, shards(): left = lax.ppermute(plane, FLAT, shift(2, 1, 1))  7.84 us
    ppermute x5, starting transfers between devices, sibling(): return lax.ppermute(rows, 'core', [(0, 1), (1, 0)])  4.55 us
    pallas_call x1, Pallas kernels, sort_slots(): pl.pallas_call(sort_kernel, out_shape=[*(jax.ShapeDtypeStruct((last - fir...  2.99 us
    ppermute x1, starting transfers between devices, shards(): got = lax.ppermute(sent, 'chan', [(0, 1), (1, 0)])  2.34 us
    unnamed x4, local copies, waits for them, and re-layouts  2.19 us
    ppermute x1, starting transfers between devices, shards(): right = lax.ppermute(plane, FLAT, shift(2, 1, -1))  1.54 us
  transfers between devices with their start and end apart: 16, of which 3 were waited for; matrix products, arithmetic and copies ran while one was open for 6% of the time, Pallas kernels for 35%

profile of v5, /device:TPU:1, one launch (start us, length us, event | category | flops | bytes accessed | tf_op | source)
XLA Modules:
  0.0 63.3 jit_solution(6207719346191760995)
XLA Ops:
  0.0 0.0 copy-start
  0.0 2.0 %collective-permute-start = (bf16[256,128]{1,0:T(8,128)(2,1)}, bf16[256,128]{1,0:T(8,128)(2,1)S(1)}, u32[]{:S(2)}, u32[]{:S(2)}) collective-permute-start(bf16[256,128]{1,0:T(8,128)(2,1)} %bitcast.39), channel_id=1, source_target_pairs={{0,2},{1,3},{4,6},{5,7},{8,10},{9,11},{12,14},{13,15},{16,18},{17,... | collective-permute-start | bytes 196616 | tf_op jit(solution)/shard_map/ppermute | solution.py:57
  2.0 1.3 %collective-permute-start.1 = (bf16[256,128]{1,0:T(8,128)(2,1)}, bf16[256,128]{1,0:T(8,128)(2,1)S(1)}, u32[]{:S(2)}, u32[]{:S(2)}) collective-permute-start(bf16[256,128]{1,0:T(8,128)(2,1)} %bitcast.40), channel_id=1, source_target_pairs={{0,66},{1,67},{4,70},{5,71},{8,74},{9,75},{12,78},{13,79},{16,82},... | collective-permute-start | bytes 196616 | tf_op jit(solution)/shard_map/ppermute | solution.py:57
  3.4 1.7 %collective-permute-start.2 = (bf16[256,128]{1,0:T(8,128)(2,1)}, bf16[256,128]{1,0:T(8,128)(2,1)S(1)}, u32[]{:S(2)}, u32[]{:S(2)}) collective-permute-start(bf16[256,128]{1,0:T(8,128)(2,1)} %bitcast.41), channel_id=1, source_target_pairs={{0,64},{1,65},{4,68},{5,69},{8,72},{9,73},{12,76},{13,77},{16,80},... | collective-permute-start | bytes 196616 | tf_op jit(solution)/shard_map/ppermute | solution.py:57
  5.0 0.9 %dynamic_update_slice.24 = bf16[1024,128]{1,0:T(8,128)(2,1)S(1)} pad(bf16[256,128]{1,0:T(8,128)(2,1)} %bitcast.42, bf16[]{:T(256)} %constant.19.clone.1), padding=0_768x0_0 | pad | bytes 327682 | tf_op jit(solution)/shard_map/dynamic_update_slice | solution.py:60
  5.9 0.7 %broadcast_shift-left_fusion = s32[4,1,64]{2,1,0:T(1,128)S(1)} fusion(s32[4,1,64]{2,1,0:T(1,128)} %param.14), kind=kLoop, calls=%fused_computation.16 | loop fusion | flops 256 | bytes 2048 | tf_op jit(solution)/shard_map/shift_left | solution.py:299
  6.6 1.0 %fusion.refs_10_ = f32[2,128,128]{2,1,0:T(8,128)S(1)} fusion(bf16[2,128,128]{2,1,0:T(8,128)(2,1)} %bitcast.43, bf16[128,128]{1,0:T(8,128)(2,1)} %param.10), kind=kOutput, calls=%fused_computation.1 | convolution fusion | flops 8388608 | bytes 229376 | tf_op jit(solution)/shard_map/dot_general | solution.py:296
  7.6 0.8 %fusion.2.packed_ref = s32[4,8,64]{2,1,0:T(8,128)S(1)} fusion(s32[4,1,64,8]{2,3,1,0:T(8,128)} %param.13, s32[4,1,64,8]{2,3,1,0:T(8,128)} %param.12, s32[4,1,64,8]{2,3,1,0:T(8,128)} %param.11, s32[4,64]{1,0:T(4,128)S(1)} %bitcast.44), kind=kLoop, calls=%fused_computation.4 | loop fusion | flops 10240 | bytes 33792 | tf_op jit(solution)/shard_map/or | solution.py:299
  8.4 0.0 copy-done
  8.4 0.0 collective-permute-done
  8.5 0.0 collective-permute-done.1
  8.5 0.0 collective-permute-done.2
  8.5 1.7 %collective-permute-start.3 = (bf16[1024,128]{1,0:T(8,128)(2,1)S(1)}, bf16[1024,128]{1,0:T(8,128)(2,1)S(1)}, u32[]{:S(2)}, u32[]{:S(2)}) collective-permute-start(bf16[1024,128]{1,0:T(8,128)(2,1)S(1)} %constant_dynamic-update-slice_fusion.3), channel_id=1, source_target_pairs={{0,16},{1,5},{4,20},{5,9},{8,24},{9,13},{12,28},{13,1},{16,32},{17... | collective-permute-start | bytes 786440 | tf_op jit(solution)/shard_map/ppermute | solution.py:57
  10.2 2.2 %collective-permute-start.4 = (bf16[1024,128]{1,0:T(8,128)(2,1)S(1)}, bf16[1024,128]{1,0:T(8,128)(2,1)S(1)}, u32[]{:S(2)}, u32[]{:S(2)}) collective-permute-start(bf16[1024,128]{1,0:T(8,128)(2,1)S(1)} %constant_dynamic-update-slice_fusion.3), channel_id=1, source_target_pairs={{0,48},{1,13},{4,52},{5,1},{8,56},{9,5},{12,60},{13,9},{16,0},{17,... | collective-permute-start | bytes 786440 | tf_op jit(solution)/shard_map/ppermute | solution.py:57
  12.4 1.2 %collective-permute-start.5 = (bf16[1024,128]{1,0:T(8,128)(2,1)S(1)}, bf16[1024,128]{1,0:T(8,128)(2,1)S(1)}, u32[]{:S(2)}, u32[]{:S(2)}) collective-permute-start(bf16[1024,128]{1,0:T(8,128)(2,1)S(1)} %constant_dynamic-update-slice_fusion.3), channel_id=1, source_target_pairs={{0,32},{1,9},{4,36},{5,13},{8,40},{9,1},{12,44},{13,5},{16,48},{17... | collective-permute-start | bytes 786440 | tf_op jit(solution)/shard_map/ppermute | solution.py:57
  13.6 0.1 pad_add_fusion.here_ref
  13.7 0.1 dynamic_update_slice.28
  13.8 0.0 copy-start.1
  13.9 2.2 %copy-done.1 = bf16[4,1,32,128,128]{4,3,2,1,0:T(8,128)(2,1)S(1)} copy-done((bf16[4,1,32,128,128]{4,3,2,1,0:T(8,128)(2,1)S(1)}, bf16[4,1,32,128,128]{4,3,2,1,0:T(8,128)(2,1)}, u32[]{:S(2)}) %copy-start.1) | copy-done | bytes 4194328
  16.0 3.0 %sort_slots.1 = (s32[5,128]{1,0:T(8,128)S(1)}, s32[9,128]{1,0:T(8,128)S(1)}, s32[2,128]{1,0:T(2,128)S(1)}, s32[3,128]{1,0:T(4,128)S(1)}, s32[2,128]{1,0:T(2,128)...) custom-call(s32[4]{0:T(128)S(1)} %pad_add_fusion.here_ref, ...), custom_call_target="tpu_custom_call" | custom-call | bytes 8388608 | tf_op jit(solution)/shard_map/sort_slots/pallas_call | solution.py:176
  19.0 0.0 collective-permute-done.3
  19.1 0.0 collective-permute-done.4
  19.1 1.2 %collective-permute-done.5 = bf16[1024,128]{1,0:T(8,128)(2,1)S(1)} collective-permute-done((bf16[1024,128]{1,0:T(8,128)(2,1)S(1)}, bf16[1024,128]{1,0:T(8,128)(2,1)S(1)}, u32[]{:S(2)}, u32[]{:S(2)}) %collective-permute-start.5) | collective-permute-done | bytes 262176 | tf_op jit(solution)/shard_map/ppermute | solution.py:57
  20.4 2.1 %collective-permute-start.8 = (bf16[32,128,128]{2,1,0:T(8,128)(2,1)S(1)}, bf16[32,128,128]{2,1,0:T(8,128)(2,1)S(1)}, u32[]{:S(2)}, u32[]{:S(2)}) collective-permute-start(bf16[32,128,128]{2,1,0:T(8,128)(2,1)S(1)} %bitcast.35), channel_id=1, source_target_pairs={{0,1},{1,0},{2,3},{3,2},{4,5},{5,4},{6,7},{7,6},{8,9},{9,8},{10,11... | collective-permute-start | bytes 3145736 | tf_op jit(solution)/shard_map/ppermute | solution.py:65
  22.6 1.1 %collective-permute-start.6 = (bf16[32,128,128]{2,1,0:T(8,128)(2,1)S(1)}, bf16[32,128,128]{2,1,0:T(8,128)(2,1)S(1)}, u32[]{:S(2)}, u32[]{:S(2)}) collective-permute-start(bf16[32,128,128]{2,1,0:T(8,128)(2,1)S(1)} %bitcast.36), channel_id=1, source_target_pairs={{0,4},{1,17},{4,8},{5,21},{8,12},{9,25},{12,0},{13,29},{16,20},{17... | collective-permute-start | bytes 3145736 | tf_op jit(solution)/shard_map/ppermute | solution.py:306
  23.7 1.5 %collective-permute-start.7 = (bf16[32,128,128]{2,1,0:T(8,128)(2,1)S(1)}, bf16[32,128,128]{2,1,0:T(8,128)(2,1)S(1)}, u32[]{:S(2)}, u32[]{:S(2)}) collective-permute-start(bf16[32,128,128]{2,1,0:T(8,128)(2,1)S(1)} %bitcast.37), channel_id=1, source_target_pairs={{0,12},{1,49},{4,0},{5,53},{8,4},{9,57},{12,8},{13,61},{16,28},{17... | collective-permute-start | bytes 3145736 | tf_op jit(solution)/shard_map/ppermute | solution.py:307
  25.2 0.0 collective-permute-done.8.refs_4_
  25.2 4.6 %stage0.1.refs_7_ = f32[16,128,128]{2,1,0:T(8,128)S(1)} custom-call(s32[5,128]{1,0:T(8,128)S(1)} %get-tuple-element.49.refs_0_, s32[8,128]{1,0:T(8,128)S(1)} %get-tuple-element.46.refs_1_, bf16[129,128,128]{2,1,0:T(8,128)(2,1)S(1)} %get-tuple-element.47.refs_2_, bf16[32,128,128]{2,1,0:T(8,128)(2,1)S(1)} %bitcast.38, ...), custom_call_target="tpu_custom_call" | custom-call | flops 4294967296 | bytes 8388608 | tf_op jit(solution)/shard_map/stage0/pallas_call | solution.py:271
  29.9 7.8 %collective-permute-done.6.refs_3_ = bf16[32,128,128]{2,1,0:T(8,128)(2,1)S(1)} collective-permute-done((bf16[32,128,128]{2,1,0:T(8,128)(2,1)S(1)}, bf16[32,128,128]{2,1,0:T(8,128)(2,1)S(1)}, u32[]{:S(2)}, u32[]{:S(2)}) %collective-permute-start.6) | collective-permute-done | bytes 1048608 | tf_op jit(solution)/shard_map/ppermute | solution.py:306
  37.7 0.0 collective-permute-done.7.refs_5_
  37.7 1.7 %collective-permute-start.10 = (bf16[32,128,128]{2,1,0:T(8,128)(2,1)S(1)}, bf16[32,128,128]{2,1,0:T(8,128)(2,1)S(1)}, u32[]{:S(2)}, u32[]{:S(2)}) collective-permute-start(bf16[32,128,128]{2,1,0:T(8,128)(2,1)S(1)} %collective-permute-done.6.refs_3_), channel_id=1, source_target_pairs={{0,1},{1,0},{2,3},{3,2},{4,5},{5,4},{6,7},{7,6},{8,9},{9,8},{10,11... | collective-permute-start | bytes 3145736 | tf_op jit(solution)/shard_map/ppermute | solution.py:65
  39.5 0.0 collective-permute-start.11
  39.6 1.2 %collective-permute-start.9 = (bf16[16,128,128]{2,1,0:T(8,128)(2,1)S(1)}, bf16[16,128,128]{2,1,0:T(8,128)(2,1)S(1)}, u32[]{:S(2)}, u32[]{:S(2)}) collective-permute-start(bf16[16,128,128]{2,1,0:T(8,128)(2,1)S(1)} %slice.6), channel_id=1, source_target_pairs={{0,4},{1,17},{4,8},{5,21},{8,12},{9,25},{12,0},{13,29},{16,20},{17... | collective-permute-start | bytes 1572872 | tf_op jit(solution)/shard_map/ppermute | solution.py:311
  40.8 1.5 %collective-permute-start.12 = (bf16[16,128,128]{2,1,0:T(8,128)(2,1)S(1)}, bf16[16,128,128]{2,1,0:T(8,128)(2,1)S(1)}, u32[]{:S(2)}, u32[]{:S(2)}) collective-permute-start(bf16[16,128,128]{2,1,0:T(8,128)(2,1)S(1)} %slice.7), channel_id=1, source_target_pairs={{0,12},{1,49},{4,0},{5,53},{8,4},{9,57},{12,8},{13,61},{16,28},{17... | collective-permute-start | bytes 1572872 | tf_op jit(solution)/shard_map/ppermute | solution.py:312
  42.3 0.0 collective-permute-done.10.refs_4_
  42.3 0.9 %collective-permute-done.11.refs_6_ = bf16[32,128,128]{2,1,0:T(8,128)(2,1)S(1)} collective-permute-done((bf16[32,128,128]{2,1,0:T(8,128)(2,1)S(1)}, bf16[32,128,128]{2,1,0:T(8,128)(2,1)S(1)}, u32[]{:S(2)}, u32[]{:S(2)}) %collective-permute-start.11) | collective-permute-done | bytes 1048608 | tf_op jit(solution)/shard_map/ppermute | solution.py:65
  43.2 7.9 %stage1.1.refs_4_ = f32[16,128,128]{2,1,0:T(8,128)S(1)} custom-call(s32[9,128]{1,0:T(8,128)S(1)} %get-tuple-element.51.refs_0_, s32[8,128]{1,0:T(8,128)S(1)} %get-tuple-element.46.refs_1_, bf16[129,128,128]{2,1,0:T(8,128)(2,1)S(1)} %get-tuple-element.47.refs_2_, ...), custom_call_target="tpu_custom_call", output_to_operand_aliasing={{}: (7, {})} | custom-call | flops 8589934592 | bytes 8388608 | tf_op jit(solution)/shard_map/stage1/pallas_call | solution.py:271
  51.1 0.0 collective-permute-done.9.refs_3_
  51.1 0.1 collective-permute-start.13
  51.2 1.3 %stage2.1.refs_5_ = f32[16,128,128]{2,1,0:T(8,128)S(1)} custom-call(s32[2,128]{1,0:T(2,128)S(1)} %get-tuple-element.55.refs_0_, s32[8,128]{1,0:T(8,128)S(1)} %get-tuple-element.46.refs_1_, bf16[129,128,128]{2,1,0:T(8,128)(2,1)S(1)} %get-tuple-element.47.refs_2_, ...), custom_call_target="tpu_custom_call", output_to_operand_aliasing={{}: (4, {})} | custom-call | flops 1073741824 | bytes 8388608 | tf_op jit(solution)/shard_map/stage2/pallas_call | solution.py:271
  52.6 0.0 collective-permute-done.12.refs_4_
  52.6 0.6 collective-permute-start.14
  53.1 0.0 collective-permute-done.13.refs_3_.refs_5_
  53.1 2.1 %stage3.1.refs_4_ = f32[16,128,128]{2,1,0:T(8,128)S(1)} custom-call(s32[3,128]{1,0:T(4,128)S(1)} %get-tuple-element.59.refs_0_, s32[8,128]{1,0:T(8,128)S(1)} %get-tuple-element.46.refs_1_, bf16[129,128,128]{2,1,0:T(8,128)(2,1)S(1)} %get-tuple-element.47.refs_2_, ...), custom_call_target="tpu_custom_call", output_to_operand_aliasing={{}: (5, {})} | custom-call | flops 2147483648 | bytes 8388608 | tf_op jit(solution)/shard_map/stage3/pallas_call | solution.py:271
  55.2 0.0 collective-permute-done.14.refs_3_.refs_6_
  55.3 1.6 %stage4.1 = (f32[16,128,128]{2,1,0:T(8,128)S(1)}, bf16[2,128,128]{2,1,0:T(8,128)(2,1)S(1)}) custom-call(s32[2,128]{1,0:T(2,128)S(1)} %get-tuple-element.58.refs_0_, s32[8,128]{1,0:T(8,128)S(1)} %get-tuple-element.46.refs_1_, bf16[129,128,128]{2,1,0:T(8,128)(2,1)S(1)} %get-tuple-element.47.refs_2_, ...), custom_call_target="tpu_custom_call", output_to_operand_aliasing={{0}: (4, {})} | custom-call | flops 1073741824 | bytes 8388608 | tf_op jit(solution)/shard_map/stage4/pallas_call | solution.py:271
  56.8 2.3 %collective-permute-start.15 = (bf16[2,128,128]{2,1,0:T(8,128)(2,1)S(1)}, bf16[2,128,128]{2,1,0:T(8,128)(2,1)S(1)}, u32[]{:S(2)}, u32[]{:S(2)}) collective-permute-start(bf16[2,128,128]{2,1,0:T(8,128)(2,1)S(1)} %get-tuple-element.64), channel_id=1, source_target_pairs={{0,64},{64,0},{1,65},{65,1},{2,66},{66,2},{3,67},{67,3},{4,68},{68... | collective-permute-start | bytes 196616 | tf_op jit(solution)/shard_map/ppermute | solution.py:321
  59.2 3.4 %stage5.1 = f32[2,128,128]{2,1,0:T(8,128)S(1)} custom-call(s32[5,128]{1,0:T(8,128)S(1)} %get-tuple-element.45.refs_0_, s32[8,128]{1,0:T(8,128)S(1)} %get-tuple-element.46.refs_1_, bf16[129,128,128]{2,1,0:T(8,128)(2,1)S(1)} %get-tuple-element.47.refs_2_, bf16[16,128,128]{2,1,0:T(8,128)(2,1)S(1)} %collective-permute-done.9.refs_3_, ...), custom_call_target="tpu_custom_call" | custom-call | flops 2147483648 | bytes 8388608 | tf_op jit(solution)/shard_map/stage5/pallas_call | solution.py:271
  62.6 0.0 collective-permute-done.15
  62.6 0.7 %maximum_convert_fusion = bf16[2,128,128]{2,1,0:T(8,128)(2,1)} fusion(f32[2,128,128]{2,1,0:T(8,128)S(1)} %stage5.1, bf16[2,128,128]{2,1,0:T(8,128)(2,1)S(1)} %collective-permute-done.15), kind=kLoop, calls=%fused_computation | loop fusion | flops 131072 | bytes 262144 | tf_op jit(solution)/shard_map/convert_element_type | solution.py:323
  (9 shorter events, 0.2 us)
Async XLA Ops:
  0.0 8.4 %copy-start = (bf16[8,128,128]{2,1,0:T(8,128)(2,1)S(1)}, bf16[8,128,128]{2,1,0:T(8,128)(2,1)}, u32[]{:S(2)}) copy-start(bf16[8,128,128]{2,1,0:T(8,128)(2,1)} %param.9) | copy-start | bytes 786436
  0.0 8.4 %collective-permute-start = (bf16[256,128]{1,0:T(8,128)(2,1)}, bf16[256,128]{1,0:T(8,128)(2,1)S(1)}, u32[]{:S(2)}, u32[]{:S(2)}) collective-permute-start(bf16[256,128]{1,0:T(8,128)(2,1)} %bitcast.39), channel_id=1, source_target_pairs={{0,2},{1,3},{4,6},{5,7},{8,10},{9,11},{12,14},{13,15},{16,18},{17,... | collective-permute-start | bytes 196616 | tf_op jit(solution)/shard_map/ppermute | solution.py:57
  2.0 6.4 %collective-permute-start.1 = (bf16[256,128]{1,0:T(8,128)(2,1)}, bf16[256,128]{1,0:T(8,128)(2,1)S(1)}, u32[]{:S(2)}, u32[]{:S(2)}) collective-permute-start(bf16[256,128]{1,0:T(8,128)(2,1)} %bitcast.40), channel_id=1, source_target_pairs={{0,66},{1,67},{4,70},{5,71},{8,74},{9,75},{12,78},{13,79},{16,82},... | collective-permute-start | bytes 196616 | tf_op jit(solution)/shard_map/ppermute | solution.py:57
  3.4 5.1 %collective-permute-start.2 = (bf16[256,128]{1,0:T(8,128)(2,1)}, bf16[256,128]{1,0:T(8,128)(2,1)S(1)}, u32[]{:S(2)}, u32[]{:S(2)}) collective-permute-start(bf16[256,128]{1,0:T(8,128)(2,1)} %bitcast.41), channel_id=1, source_target_pairs={{0,64},{1,65},{4,68},{5,69},{8,72},{9,73},{12,76},{13,77},{16,80},... | collective-permute-start | bytes 196616 | tf_op jit(solution)/shard_map/ppermute | solution.py:57
  8.5 10.5 %collective-permute-start.3 = (bf16[1024,128]{1,0:T(8,128)(2,1)S(1)}, bf16[1024,128]{1,0:T(8,128)(2,1)S(1)}, u32[]{:S(2)}, u32[]{:S(2)}) collective-permute-start(bf16[1024,128]{1,0:T(8,128)(2,1)S(1)} %constant_dynamic-update-slice_fusion.3), channel_id=1, source_target_pairs={{0,16},{1,5},{4,20},{5,9},{8,24},{9,13},{12,28},{13,1},{16,32},{17... | collective-permute-start | bytes 786440 | tf_op jit(solution)/shard_map/ppermute | solution.py:57
  10.2 8.9 %collective-permute-start.4 = (bf16[1024,128]{1,0:T(8,128)(2,1)S(1)}, bf16[1024,128]{1,0:T(8,128)(2,1)S(1)}, u32[]{:S(2)}, u32[]{:S(2)}) collective-permute-start(bf16[1024,128]{1,0:T(8,128)(2,1)S(1)} %constant_dynamic-update-slice_fusion.3), channel_id=1, source_target_pairs={{0,48},{1,13},{4,52},{5,1},{8,56},{9,5},{12,60},{13,9},{16,0},{17,... | collective-permute-start | bytes 786440 | tf_op jit(solution)/shard_map/ppermute | solution.py:57
  12.4 8.0 %collective-permute-start.5 = (bf16[1024,128]{1,0:T(8,128)(2,1)S(1)}, bf16[1024,128]{1,0:T(8,128)(2,1)S(1)}, u32[]{:S(2)}, u32[]{:S(2)}) collective-permute-start(bf16[1024,128]{1,0:T(8,128)(2,1)S(1)} %constant_dynamic-update-slice_fusion.3), channel_id=1, source_target_pairs={{0,32},{1,9},{4,36},{5,13},{8,40},{9,1},{12,44},{13,5},{16,48},{17... | collective-permute-start | bytes 786440 | tf_op jit(solution)/shard_map/ppermute | solution.py:57
  13.8 2.2 %copy-start.1 = (bf16[4,1,32,128,128]{4,3,2,1,0:T(8,128)(2,1)S(1)}, bf16[4,1,32,128,128]{4,3,2,1,0:T(8,128)(2,1)}, u32[]{:S(2)}) copy-start(bf16[4,1,32,128,128]{4,3,2,1,0:T(8,128)(2,1)} %param.15) | copy-start | bytes 12582916
  20.4 4.8 %collective-permute-start.8 = (bf16[32,128,128]{2,1,0:T(8,128)(2,1)S(1)}, bf16[32,128,128]{2,1,0:T(8,128)(2,1)S(1)}, u32[]{:S(2)}, u32[]{:S(2)}) collective-permute-start(bf16[32,128,128]{2,1,0:T(8,128)(2,1)S(1)} %bitcast.35), channel_id=1, source_target_pairs={{0,1},{1,0},{2,3},{3,2},{4,5},{5,4},{6,7},{7,6},{8,9},{9,8},{10,11... | collective-permute-start | bytes 3145736 | tf_op jit(solution)/shard_map/ppermute | solution.py:65
  22.6 15.2 %collective-permute-start.6 = (bf16[32,128,128]{2,1,0:T(8,128)(2,1)S(1)}, bf16[32,128,128]{2,1,0:T(8,128)(2,1)S(1)}, u32[]{:S(2)}, u32[]{:S(2)}) collective-permute-start(bf16[32,128,128]{2,1,0:T(8,128)(2,1)S(1)} %bitcast.36), channel_id=1, source_target_pairs={{0,4},{1,17},{4,8},{5,21},{8,12},{9,25},{12,0},{13,29},{16,20},{17... | collective-permute-start | bytes 3145736 | tf_op jit(solution)/shard_map/ppermute | solution.py:306
  23.7 14.0 %collective-permute-start.7 = (bf16[32,128,128]{2,1,0:T(8,128)(2,1)S(1)}, bf16[32,128,128]{2,1,0:T(8,128)(2,1)S(1)}, u32[]{:S(2)}, u32[]{:S(2)}) collective-permute-start(bf16[32,128,128]{2,1,0:T(8,128)(2,1)S(1)} %bitcast.37), channel_id=1, source_target_pairs={{0,12},{1,49},{4,0},{5,53},{8,4},{9,57},{12,8},{13,61},{16,28},{17... | collective-permute-start | bytes 3145736 | tf_op jit(solution)/shard_map/ppermute | solution.py:307
  37.7 4.6 %collective-permute-start.10 = (bf16[32,128,128]{2,1,0:T(8,128)(2,1)S(1)}, bf16[32,128,128]{2,1,0:T(8,128)(2,1)S(1)}, u32[]{:S(2)}, u32[]{:S(2)}) collective-permute-start(bf16[32,128,128]{2,1,0:T(8,128)(2,1)S(1)} %collective-permute-done.6.refs_3_), channel_id=1, source_target_pairs={{0,1},{1,0},{2,3},{3,2},{4,5},{5,4},{6,7},{7,6},{8,9},{9,8},{10,11... | collective-permute-start | bytes 3145736 | tf_op jit(solution)/shard_map/ppermute | solution.py:65
  39.5 3.8 %collective-permute-start.11 = (bf16[32,128,128]{2,1,0:T(8,128)(2,1)S(1)}, bf16[32,128,128]{2,1,0:T(8,128)(2,1)S(1)}, u32[]{:S(2)}, u32[]{:S(2)}) collective-permute-start(bf16[32,128,128]{2,1,0:T(8,128)(2,1)S(1)} %collective-permute-done.7.refs_5_), channel_id=1, source_target_pairs={{0,1},{1,0},{2,3},{3,2},{4,5},{5,4},{6,7},{7,6},{8,9},{9,8},{10,11... | collective-permute-start | bytes 3145736 | tf_op jit(solution)/shard_map/ppermute | solution.py:65
  39.6 11.6 %collective-permute-start.9 = (bf16[16,128,128]{2,1,0:T(8,128)(2,1)S(1)}, bf16[16,128,128]{2,1,0:T(8,128)(2,1)S(1)}, u32[]{:S(2)}, u32[]{:S(2)}) collective-permute-start(bf16[16,128,128]{2,1,0:T(8,128)(2,1)S(1)} %slice.6), channel_id=1, source_target_pairs={{0,4},{1,17},{4,8},{5,21},{8,12},{9,25},{12,0},{13,29},{16,20},{17... | collective-permute-start | bytes 1572872 | tf_op jit(solution)/shard_map/ppermute | solution.py:311
  40.8 11.8 %collective-permute-start.12 = (bf16[16,128,128]{2,1,0:T(8,128)(2,1)S(1)}, bf16[16,128,128]{2,1,0:T(8,128)(2,1)S(1)}, u32[]{:S(2)}, u32[]{:S(2)}) collective-permute-start(bf16[16,128,128]{2,1,0:T(8,128)(2,1)S(1)} %slice.7), channel_id=1, source_target_pairs={{0,12},{1,49},{4,0},{5,53},{8,4},{9,57},{12,8},{13,61},{16,28},{17... | collective-permute-start | bytes 1572872 | tf_op jit(solution)/shard_map/ppermute | solution.py:312
  51.1 2.0 %collective-permute-start.13 = (bf16[16,128,128]{2,1,0:T(8,128)(2,1)S(1)}, bf16[16,128,128]{2,1,0:T(8,128)(2,1)S(1)}, u32[]{:S(2)}, u32[]{:S(2)}) collective-permute-start(bf16[16,128,128]{2,1,0:T(8,128)(2,1)S(1)} %collective-permute-done.9.refs_3_), channel_id=1, source_target_pairs={{0,1},{1,0},{2,3},{3,2},{4,5},{5,4},{6,7},{7,6},{8,9},{9,8},{10,11... | collective-permute-start | bytes 1572872 | tf_op jit(solution)/shard_map/ppermute | solution.py:65
  52.6 2.7 %collective-permute-start.14 = (bf16[16,128,128]{2,1,0:T(8,128)(2,1)S(1)}, bf16[16,128,128]{2,1,0:T(8,128)(2,1)S(1)}, u32[]{:S(2)}, u32[]{:S(2)}) collective-permute-start(bf16[16,128,128]{2,1,0:T(8,128)(2,1)S(1)} %collective-permute-done.12.refs_4_), channel_id=1, source_target_pairs={{0,1},{1,0},{2,3},{3,2},{4,5},{5,4},{6,7},{7,6},{8,9},{9,8},{10,11... | collective-permute-start | bytes 1572872 | tf_op jit(solution)/shard_map/ppermute | solution.py:65
  56.8 5.8 %collective-permute-start.15 = (bf16[2,128,128]{2,1,0:T(8,128)(2,1)S(1)}, bf16[2,128,128]{2,1,0:T(8,128)(2,1)S(1)}, u32[]{:S(2)}, u32[]{:S(2)}) collective-permute-start(bf16[2,128,128]{2,1,0:T(8,128)(2,1)S(1)} %get-tuple-element.64), channel_id=1, source_target_pairs={{0,64},{64,0},{1,65},{65,1},{2,66},{66,2},{3,67},{67,3},{4,68},{68... | collective-permute-start | bytes 196616 | tf_op jit(solution)/shard_map/ppermute | solution.py:321
